TPU v7x, 256 devices: a whole 4x4x8 slice. The times are simulated.
256 devices in a mesh: tm: 8 (over y_hi, x), dp: 32 (over z, y_lo, core).
Axes of the slice: x: 4, y: 4 (y_hi: 2, y_lo: 2; y = y_hi * 2 + y_lo), z: 8, core: 2. Of those that a mesh axis runs over, the one named last changes fastest.
Arguments:
- features: bfloat16 [32, 3072, 1024], P('dp', 'tm'), may hold values from -6 to 6
- cotangent: bfloat16 [32, 3072, 1024], P('dp', 'tm'), may hold values from -6 to 6
- lengths: int32 [32], P('dp'), may hold values from 768 to 3072, as said below
- norm_gain: float32 [1024], replicated, may hold values from 0.5 to 1.5
- lift_weight: bfloat16 [1024, 2048], replicated, may hold values from -0.1875 to 0.1875
- conv_kernel: float32 [9, 1024], replicated, may hold values from -2 to 2
- proj_weight: bfloat16 [1024, 1024], replicated, may hold values from -0.1875 to 0.1875
Outputs:
- output: bfloat16 [32, 3072, 1024], P('dp', 'tm')
- grad_features: bfloat16 [32, 3072, 1024], P('dp', 'tm')
- grads: float32 [3155968], P(('tm', 'dp'))
Inputs may be any that keep to these rules, and one draw needn't show every extreme that they name: `lengths`: one recording has exactly 3072 valid frames and another exactly 768.
All inputs are finite; a program needn't handle non-finite values.
Results may differ from a plain program's by a relative error of at most 0.015.
Values may be sent and summed in bfloat16 or wider, within the bound.
No kernel may reach another device: no remote copies, remote signals or barrier semaphores. Data moves between devices by JAX's collectives and lax.ppermute only.
A program may use at most 128 MiB of HBM per device.

v0:
```python
import functools

import jax
import jax.numpy as jnp
from jax import lax
from jax.experimental import pallas as pl
from jax.experimental.pallas import tpu as pltpu
from jax.sharding import Mesh, PartitionSpec as P


eps_norm = 1e-05
BF = jnp.bfloat16
F32 = jnp.float32
WIN = 12


def any_spec():
    return pl.BlockSpec(memory_space=pl.ANY)


def hbm_spec():
    return pl.BlockSpec(memory_space=pltpu.HBM)


def vmem_spec():
    return pl.BlockSpec(memory_space=pltpu.VMEM)


def smem_spec():
    return pl.BlockSpec(memory_space=pltpu.SMEM)


def place(part_a, part_b, wide, begin, count):
    at = 0
    while at < count:
        window, inside = divmod(begin + at, 96)
        low = inside % 48
        step = min(48 - low, count - at)
        rows = wide[at : at + step, :].astype(BF)
        yh, rest = divmod(window, 64)
        if inside < 48:
            part_a[yh, rest, low : low + step, :] = rows
        else:
            part_b[yh * 2 + rest % 2, rest // 2, low : low + step, :] = rows
        at += step


def weight_kernel(gain_ref, n0h, n1h, k0h, k1h, a0h, a1h, g0h, g1h, wh, *rest):
    outs, rest = rest[:8], rest[8:]
    n0, n1, k0, k1, a0, a1, g0, g1, w, part_a, part_b, wide, extra, sem, sem_in = rest
    core = lax.axis_index("c")
    loads = [
        pltpu.make_async_copy(src, dst, sem_in.at[i])
        for i, (src, dst) in enumerate(
            zip(
                (a0h, g0h, a1h, g1h, n0h, k0h, n1h, k1h, wh.at[:, pl.ds(core * 1024, 1024)]),
                (a0, g0, a1, g1, n0, k0, n1, k1, w),
            )
        )
    ]
    for load in loads:
        load.start()
    contract = (((0,), (0,)), ((), ()))
    for load in loads[:4]:
        load.wait()
    for m in range(4):
        cols = slice(256 * m, 256 * m + 256)
        done = lax.dot_general(a0[:, cols], g0[...], contract, preferred_element_type=F32)
        done = done + lax.dot_general(a1[:, cols], g1[...], contract, preferred_element_type=F32)
        for v in range(4):
            wide[pl.ds(v, 256, stride=4), :] = done[:, 128 * v : 128 * v + 128]
        place(part_a, part_b, wide, 8192 + 1024 * m, 1024)
    for load in loads[4:]:
        load.wait()
    gains = []
    for m in range(4):
        cols = slice(256 * m, 256 * m + 256)
        done = lax.dot_general(n0[:, cols], k0[0:ROWS, :], contract, preferred_element_type=F32)
        done = done + lax.dot_general(n1[:, cols], k1[0:ROWS, :], contract, preferred_element_type=F32)
        folded = jnp.zeros((256, 128), F32)
        for v in range(8):
            piece = done[:, 128 * v : 128 * v + 128]
            wide[pl.ds(v, 256, stride=8), :] = piece
            folded = folded + piece * w[cols, 128 * v : 128 * v + 128].astype(F32)
        gains.append(jnp.sum(folded.T, axis=0, keepdims=True))
        place(part_a, part_b, wide, 2048 * m, 2048)
    for m in range(4):
        for j in range(2):
            at = 256 * m + 128 * j
            extra[40 + 2 * m + j : 41 + 2 * m + j, :] = gains[m][:, 128 * j : 128 * j + 128] / gain_ref[:, at : at + 128]
    taps = k0[ROWS:, :].astype(F32) + k1[ROWS:, :].astype(F32)
    for p in range(5):
        for v in range(8):
            extra[8 * p + v : 8 * p + v + 1, :] = taps[p : p + 1, 128 * v : 128 * v + 128]
    small = part_b.at[4, 0]
    small[...] = extra[...].astype(BF)
    copies = []
    for s in range(4):
        x = (lax.axis_index("x") + s) % 4
        y = (lax.axis_index(("yh", "yl")) + s) % 4
        for yh in range(2):
            copies.append((part_a.at[yh, pl.ds(x * 16, 16)], outs[s].at[pl.ds(yh * 16, 16)]))
        copies.append((small, outs[s].at[32]))
        copies.append((part_b.at[y], outs[4 + s]))
    copies = [pltpu.make_async_copy(src, dst, sem.at[i]) for i, (src, dst) in enumerate(copies)]
    for copy in copies:
        copy.start()
    for copy in copies:
        copy.wait()


def weight_blocks(gain, operands):
    blocks = [jax.ShapeDtypeStruct((33, 48, 128), BF)] * 4 + [jax.ShapeDtypeStruct((32, 48, 128), BF)] * 4
    return pl.pallas_call(
        weight_kernel,
        out_shape=blocks,
        in_specs=[vmem_spec()] + [hbm_spec(), any_spec()] * 4 + [hbm_spec()],
        out_specs=[hbm_spec()] * 8,
        scratch_shapes=[pltpu.VMEM(o.shape, BF) for o in operands[:8]]
        + [
            pltpu.VMEM((1024, 1024), BF),
            pltpu.VMEM((2, 64, 48, 128), BF),
            pltpu.VMEM((5, 32, 48, 128), BF),
            pltpu.VMEM((2048, 128), F32),
            pltpu.VMEM((48, 128), F32),
            pltpu.SemaphoreType.DMA((16,)),
            pltpu.SemaphoreType.DMA((9,)),
        ],
        compiler_params=pltpu.CompilerParams(vmem_limit_bytes=57 << 20),
        name="weight_grads",
    )(gain, *operands)


def sum_of(refs, index):
    total = refs[0][index].astype(F32)
    for ref in refs[1:]:
        total = total + ref[index].astype(F32)
    return total.astype(BF)


def first_x_kernel(i0, i1, i2, i3, mark, *outs):
    for s in range(4):
        y = (lax.axis_index(("yh", "yl")) + s) % 4
        base = (y // 2) * 16 + y % 2
        for z in range(8):
            outs[s][z] = sum_of((i0, i1, i2, i3), base + 2 * z)
        outs[s][8] = sum_of((i0, i1, i2, i3), 32)


def first_y_kernel(i0, i1, i2, i3, *outs):
    for s in range(4):
        x = (lax.axis_index("x") + s) % 4
        for z in range(8):
            outs[s][z] = sum_of((i0, i1, i2, i3), x * 8 + z)


def second_kernel(a0, a1, a2, a3, b0, b1, b2, b3, out):
    small = sum_of((a0, a1, a2, a3), 8)
    for z in range(8):
        out[z, 0:48, :] = sum_of((a0, a1, a2, a3), z)
        out[z, 48:96, :] = sum_of((b0, b1, b2, b3), z)
        out[z, 96:144, :] = small


def send(blocks, axes):
    n = 4
    got = [blocks[0]]
    for step in (2, 1, 3):
        got.append(lax.ppermute(blocks[step], axes, [(i, (i + step) % n) for i in range(n)]))
    return got


def reduce_terms(blocks, mark):
    got_x = send(blocks[:4], "x")
    got_y = send(blocks[4:], ("yh", "yl"))
    block9 = jax.ShapeDtypeStruct((9, 48, 128), BF)
    block8 = jax.ShapeDtypeStruct((8, 48, 128), BF)
    after_x = pl.pallas_call(
        first_x_kernel,
        out_shape=[block9] * 4,
        in_specs=[vmem_spec()] * 5,
        out_specs=[vmem_spec()] * 4,
        compiler_params=pltpu.CompilerParams(vmem_limit_bytes=8 << 20),
        name="sum_after_x",
    )(*got_x, mark)
    after_y = pl.pallas_call(
        first_y_kernel,
        out_shape=[block8] * 4,
        in_specs=[vmem_spec()] * 4,
        out_specs=[vmem_spec()] * 4,
        compiler_params=pltpu.CompilerParams(vmem_limit_bytes=8 << 20),
        name="sum_after_y",
    )(*got_y)
    got_a = send(after_x, ("yh", "yl"))
    got_b = send(after_y, "x")
    ready = pl.pallas_call(
        second_kernel,
        out_shape=jax.ShapeDtypeStruct((8, 144, 128), BF),
        in_specs=[vmem_spec()] * 8,
        out_specs=vmem_spec(),
        compiler_params=pltpu.CompilerParams(vmem_limit_bytes=6 << 20),
        name="sum_before_z",
    )(*got_a, *got_b)
    return lax.all_to_all(ready, "z", split_axis=0, concat_axis=0, tiled=True)


ALL = ("yh", "x", "z", "yl", "c")


def total_kernel(parts, total, head):
    done = parts[0].astype(F32)
    for z in range(1, 8):
        done = done + parts[z].astype(F32)
    total[...] = done
    head[...] = done[0:48, :]


def chunk_kernel(own, other, next0, next1, out, half0, half1, flat, *, chunk, scale):
    core = lax.axis_index("c")
    chip = lax.axis_index(("yh", "x", "z", "yl"))
    first = core == 0
    mine, others = own[...], other[...]
    half0[0:96, :] = jnp.where(first, mine[0:96], others[0:96])
    half1[0:96, :] = jnp.where(first, others[0:96], mine[0:96])
    small0 = jnp.where(first, mine[96:144], others[96:144])
    small1 = jnp.where(first, others[96:144], mine[96:144])
    both = small0[40:48] + small1[40:48]
    last = chip == 127
    half0[96:144, :] = jnp.where(last, small0, next0[...])
    half1[96:144, :] = jnp.where(last, small1, next1[...])

    @pl.when(last)
    def _():
        half1[128:136, :] = both

    for p in range(18):
        pair = chip * WIN + p
        proj = (pair >= 1024) & (pair < 1536)
        for h, half in ((0, half0), (1, half1)):
            tile = half[8 * p : 8 * p + 8, :] * scale

            @pl.when(proj)
            def _(p=p, h=h, tile=tile):
                flat[16 * p + 4 * h : 16 * p + 4 * h + 4, :] = tile[0:4]
                flat[16 * p + 8 + 4 * h : 16 * p + 12 + 4 * h, :] = tile[4:8]

            @pl.when(jnp.logical_not(proj))
            def _(p=p, h=h, tile=tile):
                flat[16 * p + 8 * h : 16 * p + 8 * h + 8, :] = tile

    begin = (2 * chip + core) * chunk - chip * (WIN * 2048)
    row, lane = begin // 128, begin % 128
    low = pltpu.roll(flat[pl.ds(row, 104), :], (128 - lane) % 128, axis=1)
    high = pltpu.roll(flat[pl.ds(row + 1, 104), :], (128 - lane) % 128, axis=1)
    at = lax.broadcasted_iota(jnp.int32, (104, 128), 1)
    out[...] = jnp.where(at < 128 - lane, low, high)


def own_chunk(swapped, chunk, grad_scale):
    total, head = pl.pallas_call(
        total_kernel,
        out_shape=[jax.ShapeDtypeStruct((144, 128), F32), jax.ShapeDtypeStruct((48, 128), F32)],
        in_specs=[vmem_spec()],
        out_specs=[vmem_spec()] * 2,
        compiler_params=pltpu.CompilerParams(vmem_limit_bytes=4 << 20),
        name="sum_after_z",
    )(swapped)
    next0 = lax.ppermute(head, ALL, [(2 * j, 2 * j - 1) for j in range(1, 128)])
    next1 = lax.ppermute(head, ALL, [(2 * j + 1, 2 * j - 1) for j in range(1, 128)])
    other = lax.ppermute(total, "c", [(0, 1), (1, 0)])
    out = pl.pallas_call(
        functools.partial(chunk_kernel, chunk=chunk, scale=grad_scale),
        out_shape=jax.ShapeDtypeStruct((104, 128), F32),
        in_specs=[vmem_spec()] * 4,
        out_specs=vmem_spec(),
        scratch_shapes=[pltpu.VMEM((144, 128), F32), pltpu.VMEM((144, 128), F32), pltpu.VMEM((312, 128), F32)],
        compiler_params=pltpu.CompilerParams(vmem_limit_bytes=4 << 20),
        name="own_chunk",
    )(total, other, next0, next1)
    return out.reshape(-1)[:chunk]


def pair_swap(array):
    return lax.ppermute(array, "c", [(0, 1), (1, 0)])


ROWS = 384
EDGE = 16
LONG = ROWS + 2 * EDGE


def inside(length_ref, first, shape):
    at = lax.axis_index(("yh", "x")) * ROWS + first + lax.broadcasted_iota(jnp.int32, shape, 0)
    return (at >= 0) & (at < length_ref[0])


def normed_rows(rows, gain):
    values = rows.astype(F32)
    center = values - jnp.mean(values, axis=-1, keepdims=True)
    scale = lax.rsqrt(jnp.mean(center * center, axis=-1, keepdims=True) + eps_norm)
    return (center * scale * gain).astype(BF)


def early_kernel(length_ref, gain_ref, xh, gh, normed_o, keep_o, give_o, x, g, sem, sem_out):
    core = lax.axis_index("c")
    loads = [pltpu.make_async_copy(xh, x, sem.at[0]), pltpu.make_async_copy(gh, g, sem.at[1])]
    for load in loads:
        load.start()
    for load in loads:
        load.wait()
    gain = gain_ref[...]

    def step(i, _):
        for j in range(2):
            r = pl.multiple_of(i * 64 + 32 * j, 32)
            rows = pl.ds(r, 32)
            x[rows, :] = normed_rows(x[rows, :], gain)
            g[rows, :] = jnp.where(inside(length_ref, r, (32, 1024)), g[rows, :].astype(F32), 0.0).astype(BF)
        return 0

    lax.fori_loop(0, ROWS // 64, step, 0)
    sends = [
        pltpu.make_async_copy(x, normed_o, sem_out.at[0]),
        pltpu.make_async_copy(g.at[:, pl.ds(core * 512, 512)], keep_o, sem_out.at[1]),
        pltpu.make_async_copy(g.at[:, pl.ds(512 - core * 512, 512)], give_o, sem_out.at[2]),
    ]
    for copy in sends:
        copy.start()
    for copy in sends:
        copy.wait()


def early(lengths, gain, x, g):
    wide = jax.ShapeDtypeStruct((ROWS, 1024), BF)
    half = jax.ShapeDtypeStruct((ROWS, 512), BF)
    return pl.pallas_call(
        early_kernel,
        out_shape=[wide, half, half],
        in_specs=[smem_spec(), vmem_spec()] + [hbm_spec()] * 2,
        out_specs=[hbm_spec()] * 3,
        scratch_shapes=[
            pltpu.VMEM((ROWS, 1024), BF),
            pltpu.VMEM((ROWS, 1024), BF),
            pltpu.SemaphoreType.DMA((2,)),
            pltpu.SemaphoreType.DMA((3,)),
        ],
        name="early",
    )(lengths, gain, x, g)


def main_kernel(info_ref, gain_ref, taps_ref, nh, gkh, ggh, beforeh, afterh, wh, pwh, *rest):
    act_o, both_o, keep_o, give_o = rest[:4]
    gs, w, pw, nm, act, both, lifts0, lifts1, gat, gcon, acf, mask, krows, sem, sem_out = rest[4:]
    core = lax.axis_index("c")
    pairs = [
        (beforeh.at[0], nm.at[pl.ds(0, EDGE)]),
        (afterh.at[0], nm.at[pl.ds(EDGE + ROWS, EDGE)]),
        (beforeh.at[1], gs.at[pl.ds(0, EDGE)]),
        (afterh.at[1], gs.at[pl.ds(EDGE + ROWS, EDGE)]),
        (nh, nm.at[pl.ds(EDGE, ROWS)]),
        (gkh, gs.at[pl.ds(EDGE, ROWS), pl.ds(core * 512, 512)]),
        (ggh, gs.at[pl.ds(EDGE, ROWS), pl.ds(512 - core * 512, 512)]),
    ]
    for n in range(4):
        pairs.append((wh.at[:, pl.ds(256 * n, 256)], w.at[:, pl.ds(256 * n, 256)]))
        pairs.append((wh.at[:, pl.ds(1024 + 256 * n, 256)], w.at[:, pl.ds(1024 + 256 * n, 256)]))
        pairs.append((pwh.at[pl.ds(256 * n, 256)], pw.at[pl.ds(256 * n, 256)]))
    loads = [pltpu.make_async_copy(src, dst, sem.at[i]) for i, (src, dst) in enumerate(pairs)]
    for load in loads:
        load.start()
    mask[...] = inside(info_ref, -EDGE, (LONG, 128)).astype(F32)
    krows[...] = jnp.zeros((2, 16, 1024), F32)
    for load in loads[:4]:
        load.wait()
    for first in (0, EDGE + ROWS):
        rows = pl.ds(first, EDGE)
        nm[rows, :] = normed_rows(nm[rows, :], gain_ref[...])
        gs[rows, :] = jnp.where(inside(info_ref, first - EDGE, (EDGE, 1024)), gs[rows, :].astype(F32), 0.0).astype(BF)
    for load in loads[4:7]:
        load.wait()

    def multiply(n, lifts):
        for load in loads[7 + 3 * n : 10 + 3 * n]:
            load.wait()
        lanes = slice(256 * n, 256 * n + 256)
        lift_value = jnp.dot(nm[...], w[:, lanes], preferred_element_type=F32)
        lift_gate = jnp.dot(nm[...], w[:, 1024 + 256 * n : 1280 + 256 * n], preferred_element_type=F32)
        back = lax.dot_general(gs[...], pw[lanes, :], (((1,), (1,)), ((), ())), preferred_element_type=F32)
        for h in range(2):
            lifts[h] = lift_value[:, 128 * h : 128 * h + 128]
            lifts[2 + h] = lift_gate[:, 128 * h : 128 * h + 128]
            lifts[4 + h] = back[:, 128 * h : 128 * h + 128]

    def channels(n, h, lifts):
        at = 256 * n + 128 * h
        taps = [taps_ref[k : k + 1, at : at + 128] for k in range(9)]
        for i in range(10):
            rows = pl.ds(8 + 40 * i, 40)
            s = jax.nn.sigmoid(lifts[2 + h, rows, :])
            lifts[2 + h, rows, :] = s
            gat[h, rows, :] = (lifts[h, rows, :] * s * mask[rows, :]).astype(BF).astype(F32)
        for i in range(7):
            r = 12 + 56 * i
            rows = pl.ds(r, 56)
            conv = taps[0] * gat[h, pl.ds(r - 4, 56), :]
            for k in range(1, 9):
                conv = conv + taps[k] * gat[h, pl.ds(r + k - 4, 56), :]
            s = jax.nn.sigmoid(conv)
            acf[h, rows, :] = conv * s
            grad = lifts[4 + h, rows, :] * s * (1.0 + conv * (1.0 - s))
            gcon[h, rows, :] = grad.astype(BF).astype(F32)
        sums = [jnp.zeros((8, 128), F32) for _ in range(9)]
        for i in range(8):
            r = EDGE + 48 * i
            rows = pl.ds(r, 48)
            own = pl.ds(r - EDGE, 48)
            grad = taps[0] * gcon[h, pl.ds(r + 4, 48), :]
            for k in range(1, 9):
                grad = grad + taps[k] * gcon[h, pl.ds(r + 4 - k, 48), :]
            s = lifts[2 + h, rows, :]
            first = grad * mask[rows, :] * s
            both[0, own, at : at + 128] = first.astype(BF)
            both[1, own, at : at + 128] = (first * lifts[h, rows, :] * (1.0 - s)).astype(BF)
            act[own, at : at + 128] = acf[h, rows, :].astype(BF)
            here = gcon[h, rows, :]
            for k in range(9):
                product = here * gat[h, pl.ds(r + k - 4, 48), :]
                sums[k] = sums[k] + jnp.sum(product.reshape(6, 8, 128), axis=0)
        for k in range(9):
            krows[k % 2, k // 2 : k // 2 + 1, at : at + 128] = jnp.sum(sums[k], axis=0, keepdims=True)

    lifts = (lifts0, lifts1)
    multiply(0, lifts0)
    for n in range(4):
        if n < 3:
            multiply(n + 1, lifts[(n + 1) % 2])
        for h in range(2):
            channels(n, h, lifts[n % 2])
    for c in range(2):
        both[c, ROWS:, :] = krows[c].astype(BF)
    sends = [
        (both.at[1 - core], give_o),
        (act, act_o),
        (both.at[core], keep_o),
        (both, both_o),
    ]
    sends = [pltpu.make_async_copy(src, dst, sem_out.at[i]) for i, (src, dst) in enumerate(sends)]
    for copy in sends:
        copy.start()
    for copy in sends:
        copy.wait()


def forward_backward(lengths, gain, taps, normed, gb_keep, gb_give, before, after, w, pw):
    wide = jax.ShapeDtypeStruct((ROWS, 1024), BF)
    tall = jax.ShapeDtypeStruct((ROWS + 16, 1024), BF)
    return pl.pallas_call(
        main_kernel,
        out_shape=[wide, jax.ShapeDtypeStruct((2, ROWS + 16, 1024), BF), tall, tall],
        in_specs=[smem_spec(), vmem_spec(), vmem_spec()] + [hbm_spec()] * 7,
        out_specs=[hbm_spec()] * 4,
        scratch_shapes=[
            pltpu.VMEM((LONG, 1024), BF),
            pltpu.VMEM((1024, 2048), BF),
            pltpu.VMEM((1024, 1024), BF),
            pltpu.VMEM((LONG, 1024), BF),
            pltpu.VMEM((ROWS, 1024), BF),
            pltpu.VMEM((2, ROWS + 16, 1024), BF),
            pltpu.VMEM((6, LONG, 128), F32),
            pltpu.VMEM((6, LONG, 128), F32),
            pltpu.VMEM((2, LONG, 128), F32),
            pltpu.VMEM((2, LONG, 128), F32),
            pltpu.VMEM((2, LONG, 128), F32),
            pltpu.VMEM((LONG, 128), F32),
            pltpu.VMEM((2, 16, 1024), F32),
            pltpu.SemaphoreType.DMA((19,)),
            pltpu.SemaphoreType.DMA((4,)),
        ],
        name="forward_backward",
    )(lengths, gain, taps, normed, gb_keep, gb_give, before, after, w, pw)


def outputs_kernel(info_ref, gain_ref, xh, gh, acth, bothh, wh, pwh, after_this, out_o, grad_o, mark_o, *rest):
    mark_o[...] = jnp.zeros((8, 128), F32)
    x, g, act, both, w, pw, sem, sem_out = rest
    pairs = [(acth, act), (pwh, pw), (xh, x), (bothh, both), (wh, w), (gh, g)]
    loads = [pltpu.make_async_copy(src, dst, sem.at[i]) for i, (src, dst) in enumerate(pairs)]
    for load in loads:
        load.start()
    for load in loads[:3]:
        load.wait()
    contract = (((1,), (1,)), ((), ()))
    for i in range(3):
        rows = slice(128 * i, 128 * i + 128)
        branch = jnp.dot(act[rows, :], pw[...], preferred_element_type=F32)
        branch = jnp.where(inside(info_ref, 128 * i, (128, 1024)), branch, 0.0)
        act[rows, :] = (x[rows, :].astype(F32) + branch).astype(BF)
    first = pltpu.make_async_copy(act, out_o, sem_out.at[0])
    first.start()
    for load in loads[3:]:
        load.wait()
    for i in range(3):
        rows = slice(128 * i, 128 * i + 128)
        grad = lax.dot_general(both[0, rows, :], w[:, :1024], contract, preferred_element_type=F32)
        grad = grad + lax.dot_general(both[1, rows, :], w[:, 1024:], contract, preferred_element_type=F32)
        u = grad * gain_ref[...]
        values = x[rows, :].astype(F32)
        center = values - jnp.mean(values, axis=-1, keepdims=True)
        scale = lax.rsqrt(jnp.mean(center * center, axis=-1, keepdims=True) + eps_norm)
        xhat = center * scale
        u = scale * (u - jnp.mean(u, axis=-1, keepdims=True) - xhat * jnp.mean(u * xhat, axis=-1, keepdims=True))
        g[rows, :] = (g[rows, :].astype(F32) + u).astype(BF)
    second = pltpu.make_async_copy(g, grad_o, sem_out.at[1])
    second.start()
    first.wait()
    second.wait()


def outputs(info, gain, x, g, act, both, w, pw, after_this):
    wide = jax.ShapeDtypeStruct((ROWS, 1024), BF)
    return pl.pallas_call(
        outputs_kernel,
        out_shape=[wide, wide, jax.ShapeDtypeStruct((8, 128), F32)],
        in_specs=[smem_spec(), vmem_spec()] + [hbm_spec()] * 7,
        out_specs=[hbm_spec()] * 2 + [vmem_spec()],
        scratch_shapes=[
            pltpu.VMEM((ROWS, 1024), BF),
            pltpu.VMEM((ROWS, 1024), BF),
            pltpu.VMEM((ROWS, 1024), BF),
            pltpu.VMEM((2, ROWS + 16, 1024), BF),
            pltpu.VMEM((1024, 2048), BF),
            pltpu.VMEM((1024, 1024), BF),
            pltpu.SemaphoreType.DMA((6,)),
            pltpu.SemaphoreType.DMA((2,)),
        ],
        name="outputs",
    )(info, gain, x, g, act, both, w, pw, after_this)


def local(features, cotangent, lengths, norm_gain, lift_weight, conv_kernel, proj_weight):
    x, g = features[0], cotangent[0]
    frames, width = x.shape
    edge = jnp.stack([x[-EDGE:], g[-EDGE:]])
    start = jnp.stack([x[:EDGE], g[:EDGE]])
    before = lax.ppermute(edge, ("yh", "x"), [(i, i + 1) for i in range(7)])
    after = lax.ppermute(start, ("yh", "x"), [(i + 1, i) for i in range(7)])
    gain = norm_gain[None]
    normed, gb_keep, gb_give = early(lengths, gain, x, g)
    normed_other = pair_swap(normed)
    gb_other = pair_swap(gb_give)
    activated, both, keep, give = forward_backward(
        lengths, gain, conv_kernel, normed, gb_keep, gb_give, before, after, lift_weight, proj_weight
    )
    keep_other = pair_swap(give)
    act_other = pair_swap(activated)
    chunk = (2 * width * width + width * width + 10 * width) // 256
    operands = (normed, normed_other, keep, keep_other, activated, act_other, gb_keep, gb_other, lift_weight)
    blocks = weight_blocks(gain, operands)
    output, grad_features, mark = outputs(lengths, gain, x, g, activated, both, lift_weight, proj_weight, blocks[0])
    grads = own_chunk(reduce_terms(blocks, mark), chunk, float(frames * 256) ** (-0.5))
    return output[None], grad_features[None], grads


def solution(mesh):
    fine = Mesh(mesh.devices.reshape(2, 4, 8, 2, 2), ALL)
    act = P(("z", "yl", "c"), ("yh", "x"), None)

    return jax.shard_map(
        local,
        mesh=fine,
        in_specs=(act, act, P(("z", "yl", "c")), P(), P(), P(), P()),
        out_specs=(act, act, P(ALL)),
        check_vma=False,
    )
```

profile of v0, /device:TPU:11, one launch (start us, length us, event | category | flops | bytes accessed | tf_op | source)
XLA Modules:
  0.0 123.3 jit_solution(1317610440033387058)
XLA Ops:
  0.6 0.8 fusion
  1.5 3.1 %collective-permute-start = (bf16[2,16,1024]{2,1,0:T(8,128)(2,1)S(1)}, bf16[2,16,1024]{2,1,0:T(8,128)(2,1)S(1)}, u32[]{:S(2)}, u32[]{:S(2)}) collective-permute-start(bf16[2,16,1024]{2,1,0:T(8,128)(2,1)S(1)} %pad_maximum_fusion), channel_id=1, source_target_pairs={{0,32},{32,64},{64,96},{96,128},{128,160},{160,192},{192,224},{1,3... | collective-permute-start | bytes 196616 | tf_op jit(solution)/shard_map/ppermute | solution.py:545
  4.6 2.2 %collective-permute-start.1 = (bf16[2,16,1024]{2,1,0:T(8,128)(2,1)S(1)}, bf16[2,16,1024]{2,1,0:T(8,128)(2,1)S(1)}, u32[]{:S(2)}, u32[]{:S(2)}) collective-permute-start(bf16[2,16,1024]{2,1,0:T(8,128)(2,1)S(1)} %pad_maximum_fusion.1), channel_id=1, source_target_pairs={{32,0},{64,32},{96,64},{128,96},{160,128},{192,160},{224,192},{33,... | collective-permute-start | bytes 196616 | tf_op jit(solution)/shard_map/ppermute | solution.py:546
  7.4 5.6 %early.1 = (bf16[384,1024]{1,0:T(8,128)(2,1)}, bf16[384,512]{1,0:T(8,128)(2,1)}, bf16[384,512]{1,0:T(8,128)(2,1)}) custom-call(s32[1]{0:T(128)S(6)} %copy.10.length_ref.info_ref, f32[1,1024]{1,0:T(1,128)} %bitcast.11, bf16[384,1024]{1,0:T(8,128)(2,1)} %bitcast.7, bf16[384,1024]{1,0:T(8,128)(2,1)} %bitcast.9), custom_call_target="tpu_custom_call" | custom-call | tf_op jit(solution)/shard_map/early/pallas_call | solution.py:336
  13.1 0.6 copy-done.9
  13.7 13.5 %forward_backward.1 = (bf16[384,1024]{1,0:T(8,128)(2,1)}, bf16[2,400,1024]{2,1,0:T(8,128)(2,1)}, bf16[400,1024]{1,0:T(8,128)(2,1)}, bf16[400,1024]{1,0:T(8,128)(2,1)}) custom-call(s32[1]{0:T(128)S(6)} %copy.10.length_ref.info_ref, f32[1,1024]{1,0:T(1,128)} %bitcast.12, f32[9,1024]{1,0:T(8,128)} %taps_ref.1, bf16[384,1024]{1,0:T(8,128)(2,1)} %get-tuple-element.31.nh.n0h, ...), custom_call_target="tpu_custom_call" | custom-call | tf_op jit(solution)/shard_map/forward_backward/pallas_call | solution.py:457
  27.2 1.3 %collective-permute-start.3 = (bf16[400,1024]{1,0:T(8,128)(2,1)}, bf16[400,1024]{1,0:T(8,128)(2,1)S(1)}, u32[]{:S(2)}, u32[]{:S(2)}) collective-permute-start(bf16[400,1024]{1,0:T(8,128)(2,1)} %get-tuple-element.37), channel_id=1, source_target_pairs={{0,1},{1,0},{2,3},{3,2},{4,5},{5,4},{6,7},{7,6},{8,9},{9,8},{10,11... | collective-permute-start | bytes 2457608 | tf_op jit(solution)/shard_map/ppermute | solution.py:284
  29.2 4.4 %collective-permute-done.5.g1h = bf16[384,512]{1,0:T(8,128)(2,1)S(1)} collective-permute-done((bf16[384,512]{1,0:T(8,128)(2,1)S(1)}, bf16[384,512]{1,0:T(8,128)(2,1)S(1)}, u32[]{:S(2)}, u32[]{:S(2)}) %collective-permute-start.5) | collective-permute-done | bytes 393248 | tf_op jit(solution)/shard_map/ppermute | solution.py:284
  33.6 0.7 copy-done.7
  35.1 8.8 %weight_grads.1 = (bf16[33,48,128]{2,1,0:T(8,128)(2,1)}, bf16[33,48,128]{2,1,0:T(8,128)(2,1)}, bf16[33,48,128]{2,1,0:T(8,128)(2,1)}, bf16[33,48,128]{2,1,0:T(8,1...) custom-call(f32[1,1024]{1,0:T(1,128)} %bitcast.13, ...), custom_call_target="tpu_custom_call" | custom-call | tf_op jit(solution)/shard_map/weight_grads/pallas_call | solution.py:114
  43.8 2.1 %collective-permute-start.12 = (bf16[32,48,128]{2,1,0:T(8,128)(2,1)}, bf16[32,48,128]{2,1,0:T(8,128)(2,1)S(1)}, u32[]{:S(2)}, u32[]{:S(2)}) collective-permute-start(bf16[32,48,128]{2,1,0:T(8,128)(2,1)} %get-tuple-element.50), channel_id=1, source_target_pairs={{0,128},{2,130},{128,0},{130,2},{1,129},{3,131},{129,1},{131,3},{4... | collective-permute-start | bytes 1179656 | tf_op jit(solution)/shard_map/ppermute | solution.py:169
  45.9 1.5 %collective-permute-start.14 = (bf16[32,48,128]{2,1,0:T(8,128)(2,1)}, bf16[32,48,128]{2,1,0:T(8,128)(2,1)S(1)}, u32[]{:S(2)}, u32[]{:S(2)}) collective-permute-start(bf16[32,48,128]{2,1,0:T(8,128)(2,1)} %get-tuple-element.52), channel_id=1, source_target_pairs={{0,130},{2,0},{128,2},{130,128},{1,131},{3,1},{129,3},{131,129},{4... | collective-permute-start | bytes 1179656 | tf_op jit(solution)/shard_map/ppermute | solution.py:169
  47.4 2.3 %collective-permute-start.6 = (bf16[33,48,128]{2,1,0:T(8,128)(2,1)}, bf16[33,48,128]{2,1,0:T(8,128)(2,1)S(1)}, u32[]{:S(2)}, u32[]{:S(2)}) collective-permute-start(bf16[33,48,128]{2,1,0:T(8,128)(2,1)} %get-tuple-element.41), channel_id=1, source_target_pairs={{0,64},{32,96},{64,0},{96,32},{1,65},{33,97},{65,1},{97,33},{2,66}... | collective-permute-start | bytes 1216520 | tf_op jit(solution)/shard_map/ppermute | solution.py:169
  49.8 2.7 %collective-permute-start.7 = (bf16[33,48,128]{2,1,0:T(8,128)(2,1)}, bf16[33,48,128]{2,1,0:T(8,128)(2,1)S(1)}, u32[]{:S(2)}, u32[]{:S(2)}) collective-permute-start(bf16[33,48,128]{2,1,0:T(8,128)(2,1)} %get-tuple-element.42), channel_id=1, source_target_pairs={{0,32},{32,64},{64,96},{96,0},{1,33},{33,65},{65,97},{97,1},{2,34}... | collective-permute-start | bytes 1216520 | tf_op jit(solution)/shard_map/ppermute | solution.py:169
  52.5 3.5 %collective-permute-done.12.i1 = bf16[32,48,128]{2,1,0:T(8,128)(2,1)S(1)} collective-permute-done((bf16[32,48,128]{2,1,0:T(8,128)(2,1)}, bf16[32,48,128]{2,1,0:T(8,128)(2,1)S(1)}, u32[]{:S(2)}, u32[]{:S(2)}) %collective-permute-start.12) | collective-permute-done | bytes 393248 | tf_op jit(solution)/shard_map/ppermute | solution.py:169
  56.0 3.2 %collective-permute-start.8 = (bf16[33,48,128]{2,1,0:T(8,128)(2,1)}, bf16[33,48,128]{2,1,0:T(8,128)(2,1)S(1)}, u32[]{:S(2)}, u32[]{:S(2)}) collective-permute-start(bf16[33,48,128]{2,1,0:T(8,128)(2,1)} %get-tuple-element.43), channel_id=1, source_target_pairs={{0,96},{32,0},{64,32},{96,64},{1,97},{33,1},{65,33},{97,65},{2,98}... | collective-permute-start | bytes 1216520 | tf_op jit(solution)/shard_map/ppermute | solution.py:169
  59.2 5.3 %collective-permute-done.13.i2 = bf16[32,48,128]{2,1,0:T(8,128)(2,1)S(1)} collective-permute-done((bf16[32,48,128]{2,1,0:T(8,128)(2,1)}, bf16[32,48,128]{2,1,0:T(8,128)(2,1)S(1)}, u32[]{:S(2)}, u32[]{:S(2)}) %collective-permute-start.13) | collective-permute-done | bytes 393248 | tf_op jit(solution)/shard_map/ppermute | solution.py:169
  65.1 1.0 copy-done.1
  66.3 3.9 %collective-permute-start.15 = (bf16[8,48,128]{2,1,0:T(8,128)(2,1)S(1)}, bf16[8,48,128]{2,1,0:T(8,128)(2,1)S(1)}, u32[]{:S(2)}, u32[]{:S(2)}) collective-permute-start(bf16[8,48,128]{2,1,0:T(8,128)(2,1)S(1)} %get-tuple-element.54), channel_id=1, source_target_pairs={{0,64},{32,96},{64,0},{96,32},{1,65},{33,97},{65,1},{97,33},{2,66}... | collective-permute-start | bytes 294920 | tf_op jit(solution)/shard_map/ppermute | solution.py:169
  70.2 10.8 %outputs.1 = (bf16[384,1024]{1,0:T(8,128)(2,1)}, bf16[384,1024]{1,0:T(8,128)(2,1)}, f32[8,128]{1,0:T(8,128)}) custom-call(s32[1]{0:T(128)S(6)} %copy.10.length_ref.info_ref, f32[1,1024]{1,0:T(1,128)} %bitcast.14, bf16[384,1024]{1,0:T(8,128)(2,1)} %bitcast.8, bf16[384,1024]{1,0:T(8,128)(2,1)} %bitcast.10, bf16[384,1024]{1,0:T(8,128)(2,1)} %get-tuple-element.34.a0h.acth, ...), custom_call_target="tpu_custom_call" | custom-call | tf_op jit(solution)/shard_map/outputs/pallas_call | solution.py:521
  81.0 0.7 copy-done.2
  82.3 1.9 %collective-permute-start.10 = (bf16[9,48,128]{2,1,0:T(8,128)(2,1)S(1)}, bf16[9,48,128]{2,1,0:T(8,128)(2,1)S(1)}, u32[]{:S(2)}, u32[]{:S(2)}) collective-permute-start(bf16[9,48,128]{2,1,0:T(8,128)(2,1)S(1)} %get-tuple-element.47), channel_id=1, source_target_pairs={{0,2},{2,128},{128,130},{130,0},{1,3},{3,129},{129,131},{131,1},{4... | collective-permute-start | bytes 331784 | tf_op jit(solution)/shard_map/ppermute | solution.py:169
  84.2 2.7 %collective-permute-start.16 = (bf16[8,48,128]{2,1,0:T(8,128)(2,1)S(1)}, bf16[8,48,128]{2,1,0:T(8,128)(2,1)S(1)}, u32[]{:S(2)}, u32[]{:S(2)}) collective-permute-start(bf16[8,48,128]{2,1,0:T(8,128)(2,1)S(1)} %get-tuple-element.55), channel_id=1, source_target_pairs={{0,32},{32,64},{64,96},{96,0},{1,33},{33,65},{65,97},{97,1},{2,34}... | collective-permute-start | bytes 294920 | tf_op jit(solution)/shard_map/ppermute | solution.py:169
  87.0 1.6 %collective-permute-done.16.b2 = bf16[8,48,128]{2,1,0:T(8,128)(2,1)S(1)} collective-permute-done((bf16[8,48,128]{2,1,0:T(8,128)(2,1)S(1)}, bf16[8,48,128]{2,1,0:T(8,128)(2,1)S(1)}, u32[]{:S(2)}, u32[]{:S(2)}) %collective-permute-start.16) | collective-permute-done | bytes 98336 | tf_op jit(solution)/shard_map/ppermute | solution.py:169
  88.6 2.1 %collective-permute-done.17.b3 = bf16[8,48,128]{2,1,0:T(8,128)(2,1)S(1)} collective-permute-done((bf16[8,48,128]{2,1,0:T(8,128)(2,1)S(1)}, bf16[8,48,128]{2,1,0:T(8,128)(2,1)S(1)}, u32[]{:S(2)}, u32[]{:S(2)}) %collective-permute-start.17) | collective-permute-done | bytes 98336 | tf_op jit(solution)/shard_map/ppermute | solution.py:169
  90.9 17.7 %all_to_all.5.parts = bf16[8,144,128]{2,1,0:T(8,128)(2,1)S(1)} all-to-all(bf16[8,144,128]{2,1,0:T(8,128)(2,1)S(1)} %sum_before_z.1), channel_id=1, replica_groups=mesh['yh'=2,'x'=4,'z'=8,'yl'=2,'c'=2] {'z'}, dimensions={0} | all-to-all | bytes 589824 | tf_op jit(solution)/shard_map/all_to_all | solution.py:204
  108.6 4.3 %collective-permute-start.18 = (f32[144,128]{1,0:T(8,128)S(1)}, f32[144,128]{1,0:T(8,128)S(1)}, u32[]{:S(2)}, u32[]{:S(2)}) collective-permute-start(f32[144,128]{1,0:T(8,128)S(1)} %get-tuple-element.57.own), channel_id=1, source_target_pairs={{0,1},{1,0},{2,3},{3,2},{4,5},{5,4},{6,7},{7,6},{8,9},{9,8},{10,11... | collective-permute-start | bytes 221192 | tf_op jit(solution)/shard_map/ppermute | solution.py:270
  112.8 3.4 %collective-permute-start.20 = (f32[48,128]{1,0:T(8,128)S(1)}, f32[48,128]{1,0:T(8,128)S(1)}, u32[]{:S(2)}, u32[]{:S(2)}) collective-permute-start(f32[48,128]{1,0:T(8,128)S(1)} %get-tuple-element.58), channel_id=1, source_target_pairs={{3,1},{5,3},{7,5},{9,7},{11,9},{13,11},{15,13},{17,15},{19,17},{21... | collective-permute-start | bytes 73736 | tf_op jit(solution)/shard_map/ppermute | solution.py:269
  116.2 1.3 %collective-permute-start.19 = (f32[48,128]{1,0:T(8,128)S(1)}, f32[48,128]{1,0:T(8,128)S(1)}, u32[]{:S(2)}, u32[]{:S(2)}) collective-permute-start(f32[48,128]{1,0:T(8,128)S(1)} %get-tuple-element.58), channel_id=1, source_target_pairs={{2,1},{4,3},{6,5},{8,7},{10,9},{12,11},{14,13},{16,15},{18,17},{20... | collective-permute-start | bytes 73736 | tf_op jit(solution)/shard_map/ppermute | solution.py:268
  117.5 0.8 collective-permute-done.20.next1
  118.3 4.0 %collective-permute-done.19.next0 = f32[48,128]{1,0:T(8,128)S(1)} collective-permute-done((f32[48,128]{1,0:T(8,128)S(1)}, f32[48,128]{1,0:T(8,128)S(1)}, u32[]{:S(2)}, u32[]{:S(2)}) %collective-permute-start.19) | collective-permute-done | bytes 24608 | tf_op jit(solution)/shard_map/ppermute | solution.py:268
  122.3 1.0 own_chunk.1
  (45 shorter events, 3.1 us)
Async XLA Ops:
  1.5 11.6 %collective-permute-start = (bf16[2,16,1024]{2,1,0:T(8,128)(2,1)S(1)}, bf16[2,16,1024]{2,1,0:T(8,128)(2,1)S(1)}, u32[]{:S(2)}, u32[]{:S(2)}) collective-permute-start(bf16[2,16,1024]{2,1,0:T(8,128)(2,1)S(1)} %pad_maximum_fusion), channel_id=1, source_target_pairs={{0,32},{32,64},{64,96},{96,128},{128,160},{160,192},{192,224},{1,3... | collective-permute-start | bytes 196616 | tf_op jit(solution)/shard_map/ppermute | solution.py:545
  4.6 8.5 %collective-permute-start.1 = (bf16[2,16,1024]{2,1,0:T(8,128)(2,1)S(1)}, bf16[2,16,1024]{2,1,0:T(8,128)(2,1)S(1)}, u32[]{:S(2)}, u32[]{:S(2)}) collective-permute-start(bf16[2,16,1024]{2,1,0:T(8,128)(2,1)S(1)} %pad_maximum_fusion.1), channel_id=1, source_target_pairs={{32,0},{64,32},{96,64},{128,96},{160,128},{192,160},{224,192},{33,... | collective-permute-start | bytes 196616 | tf_op jit(solution)/shard_map/ppermute | solution.py:546
  13.1 0.6 copy-start.9
  13.1 0.6 copy-start.10
  13.7 14.8 %copy-start.3 = (bf16[384,1024]{1,0:T(8,128)(2,1)S(1)}, bf16[384,1024]{1,0:T(8,128)(2,1)}, u32[]{:S(2)}) copy-start(bf16[384,1024]{1,0:T(8,128)(2,1)} %get-tuple-element.31.nh.n0h) | copy-start | bytes 2359300
  13.7 15.3 %copy-start.8 = (bf16[384,512]{1,0:T(8,128)(2,1)S(1)}, bf16[384,512]{1,0:T(8,128)(2,1)}, u32[]{:S(2)}) copy-start(bf16[384,512]{1,0:T(8,128)(2,1)} %get-tuple-element.33.ggh) | copy-start | bytes 1179652
  27.2 6.3 %collective-permute-start.3 = (bf16[400,1024]{1,0:T(8,128)(2,1)}, bf16[400,1024]{1,0:T(8,128)(2,1)S(1)}, u32[]{:S(2)}, u32[]{:S(2)}) collective-permute-start(bf16[400,1024]{1,0:T(8,128)(2,1)} %get-tuple-element.37), channel_id=1, source_target_pairs={{0,1},{1,0},{2,3},{3,2},{4,5},{5,4},{6,7},{7,6},{8,9},{9,8},{10,11... | collective-permute-start | bytes 2457608 | tf_op jit(solution)/shard_map/ppermute | solution.py:284
  28.6 5.0 %collective-permute-start.2 = (bf16[384,1024]{1,0:T(8,128)(2,1)S(1)}, bf16[384,1024]{1,0:T(8,128)(2,1)S(1)}, u32[]{:S(2)}, u32[]{:S(2)}) collective-permute-start(bf16[384,1024]{1,0:T(8,128)(2,1)S(1)} %copy-done.3), channel_id=1, source_target_pairs={{0,1},{1,0},{2,3},{3,2},{4,5},{5,4},{6,7},{7,6},{8,9},{9,8},{10,11... | collective-permute-start | bytes 2359304 | tf_op jit(solution)/shard_map/ppermute | solution.py:284
  28.7 4.9 %collective-permute-start.4 = (bf16[384,1024]{1,0:T(8,128)(2,1)}, bf16[384,1024]{1,0:T(8,128)(2,1)S(1)}, u32[]{:S(2)}, u32[]{:S(2)}) collective-permute-start(bf16[384,1024]{1,0:T(8,128)(2,1)} %get-tuple-element.34.a0h.acth), channel_id=1, source_target_pairs={{0,1},{1,0},{2,3},{3,2},{4,5},{5,4},{6,7},{7,6},{8,9},{9,8},{10,11... | collective-permute-start | bytes 2359304 | tf_op jit(solution)/shard_map/ppermute | solution.py:284
  29.1 4.5 %collective-permute-start.5 = (bf16[384,512]{1,0:T(8,128)(2,1)S(1)}, bf16[384,512]{1,0:T(8,128)(2,1)S(1)}, u32[]{:S(2)}, u32[]{:S(2)}) collective-permute-start(bf16[384,512]{1,0:T(8,128)(2,1)S(1)} %copy-done.8), channel_id=1, source_target_pairs={{0,1},{1,0},{2,3},{3,2},{4,5},{5,4},{6,7},{7,6},{8,9},{9,8},{10,11... | collective-permute-start | bytes 1179656 | tf_op jit(solution)/shard_map/ppermute | solution.py:284
  33.5 0.7 copy-start.7
  33.5 1.0 copy-start.5
  33.5 1.3 %copy-start.6 = (bf16[384,1024]{1,0:T(8,128)(2,1)}, bf16[384,1024]{1,0:T(8,128)(2,1)S(1)}, u32[]{:S(2)}) copy-start(bf16[384,1024]{1,0:T(8,128)(2,1)S(1)} %collective-permute-done.4.a1h) | copy-start | bytes 2359300
  33.6 1.5 %copy-start.4 = (bf16[400,1024]{1,0:T(8,128)(2,1)}, bf16[400,1024]{1,0:T(8,128)(2,1)S(1)}, u32[]{:S(2)}) copy-start(bf16[400,1024]{1,0:T(8,128)(2,1)S(1)} %collective-permute-done.3.k1h) | copy-start | bytes 2457604
  43.8 12.1 %collective-permute-start.12 = (bf16[32,48,128]{2,1,0:T(8,128)(2,1)}, bf16[32,48,128]{2,1,0:T(8,128)(2,1)S(1)}, u32[]{:S(2)}, u32[]{:S(2)}) collective-permute-start(bf16[32,48,128]{2,1,0:T(8,128)(2,1)} %get-tuple-element.50), channel_id=1, source_target_pairs={{0,128},{2,130},{128,0},{130,2},{1,129},{3,131},{129,1},{131,3},{4... | collective-permute-start | bytes 1179656 | tf_op jit(solution)/shard_map/ppermute | solution.py:169
  45.9 18.6 %collective-permute-start.13 = (bf16[32,48,128]{2,1,0:T(8,128)(2,1)}, bf16[32,48,128]{2,1,0:T(8,128)(2,1)S(1)}, u32[]{:S(2)}, u32[]{:S(2)}) collective-permute-start(bf16[32,48,128]{2,1,0:T(8,128)(2,1)} %get-tuple-element.51), channel_id=1, source_target_pairs={{0,2},{2,128},{128,130},{130,0},{1,3},{3,129},{129,131},{131,1},{4... | collective-permute-start | bytes 1179656 | tf_op jit(solution)/shard_map/ppermute | solution.py:169
  45.9 19.2 %collective-permute-start.14 = (bf16[32,48,128]{2,1,0:T(8,128)(2,1)}, bf16[32,48,128]{2,1,0:T(8,128)(2,1)S(1)}, u32[]{:S(2)}, u32[]{:S(2)}) collective-permute-start(bf16[32,48,128]{2,1,0:T(8,128)(2,1)} %get-tuple-element.52), channel_id=1, source_target_pairs={{0,130},{2,0},{128,2},{130,128},{1,131},{3,1},{129,3},{131,129},{4... | collective-permute-start | bytes 1179656 | tf_op jit(solution)/shard_map/ppermute | solution.py:169
  47.4 33.5 %collective-permute-start.6 = (bf16[33,48,128]{2,1,0:T(8,128)(2,1)}, bf16[33,48,128]{2,1,0:T(8,128)(2,1)S(1)}, u32[]{:S(2)}, u32[]{:S(2)}) collective-permute-start(bf16[33,48,128]{2,1,0:T(8,128)(2,1)} %get-tuple-element.41), channel_id=1, source_target_pairs={{0,64},{32,96},{64,0},{96,32},{1,65},{33,97},{65,1},{97,33},{2,66}... | collective-permute-start | bytes 1216520 | tf_op jit(solution)/shard_map/ppermute | solution.py:169
  49.8 31.2 %collective-permute-start.7 = (bf16[33,48,128]{2,1,0:T(8,128)(2,1)}, bf16[33,48,128]{2,1,0:T(8,128)(2,1)S(1)}, u32[]{:S(2)}, u32[]{:S(2)}) collective-permute-start(bf16[33,48,128]{2,1,0:T(8,128)(2,1)} %get-tuple-element.42), channel_id=1, source_target_pairs={{0,32},{32,64},{64,96},{96,0},{1,33},{33,65},{65,97},{97,1},{2,34}... | collective-permute-start | bytes 1216520 | tf_op jit(solution)/shard_map/ppermute | solution.py:169
  56.0 25.0 %collective-permute-start.8 = (bf16[33,48,128]{2,1,0:T(8,128)(2,1)}, bf16[33,48,128]{2,1,0:T(8,128)(2,1)S(1)}, u32[]{:S(2)}, u32[]{:S(2)}) collective-permute-start(bf16[33,48,128]{2,1,0:T(8,128)(2,1)} %get-tuple-element.43), channel_id=1, source_target_pairs={{0,96},{32,0},{64,32},{96,64},{1,97},{33,1},{65,33},{97,65},{2,98}... | collective-permute-start | bytes 1216520 | tf_op jit(solution)/shard_map/ppermute | solution.py:169
  65.1 1.0 copy-start.1
  66.3 20.7 %collective-permute-start.15 = (bf16[8,48,128]{2,1,0:T(8,128)(2,1)S(1)}, bf16[8,48,128]{2,1,0:T(8,128)(2,1)S(1)}, u32[]{:S(2)}, u32[]{:S(2)}) collective-permute-start(bf16[8,48,128]{2,1,0:T(8,128)(2,1)S(1)} %get-tuple-element.54), channel_id=1, source_target_pairs={{0,64},{32,96},{64,0},{96,32},{1,65},{33,97},{65,1},{97,33},{2,66}... | collective-permute-start | bytes 294920 | tf_op jit(solution)/shard_map/ppermute | solution.py:169
  70.2 10.8 %copy-start = (bf16[33,48,128]{2,1,0:T(8,128)(2,1)S(1)}, bf16[33,48,128]{2,1,0:T(8,128)(2,1)}, u32[]{:S(2)}) copy-start(bf16[33,48,128]{2,1,0:T(8,128)(2,1)} %get-tuple-element.38.after_this.i0) | copy-start | bytes 1216516
  81.0 0.7 copy-start.2
  81.9 8.8 %collective-permute-start.9 = (bf16[9,48,128]{2,1,0:T(8,128)(2,1)S(1)}, bf16[9,48,128]{2,1,0:T(8,128)(2,1)S(1)}, u32[]{:S(2)}, u32[]{:S(2)}) collective-permute-start(bf16[9,48,128]{2,1,0:T(8,128)(2,1)S(1)} %get-tuple-element.46), channel_id=1, source_target_pairs={{0,128},{2,130},{128,0},{130,2},{1,129},{3,131},{129,1},{131,3},{4... | collective-permute-start | bytes 331784 | tf_op jit(solution)/shard_map/ppermute | solution.py:169
  82.3 8.5 %collective-permute-start.10 = (bf16[9,48,128]{2,1,0:T(8,128)(2,1)S(1)}, bf16[9,48,128]{2,1,0:T(8,128)(2,1)S(1)}, u32[]{:S(2)}, u32[]{:S(2)}) collective-permute-start(bf16[9,48,128]{2,1,0:T(8,128)(2,1)S(1)} %get-tuple-element.47), channel_id=1, source_target_pairs={{0,2},{2,128},{128,130},{130,0},{1,3},{3,129},{129,131},{131,1},{4... | collective-permute-start | bytes 331784 | tf_op jit(solution)/shard_map/ppermute | solution.py:169
  84.2 6.5 %collective-permute-start.11 = (bf16[9,48,128]{2,1,0:T(8,128)(2,1)S(1)}, bf16[9,48,128]{2,1,0:T(8,128)(2,1)S(1)}, u32[]{:S(2)}, u32[]{:S(2)}) collective-permute-start(bf16[9,48,128]{2,1,0:T(8,128)(2,1)S(1)} %get-tuple-element.48), channel_id=1, source_target_pairs={{0,130},{2,0},{128,2},{130,128},{1,131},{3,1},{129,3},{131,129},{4... | collective-permute-start | bytes 331784 | tf_op jit(solution)/shard_map/ppermute | solution.py:169
  84.2 4.4 %collective-permute-start.16 = (bf16[8,48,128]{2,1,0:T(8,128)(2,1)S(1)}, bf16[8,48,128]{2,1,0:T(8,128)(2,1)S(1)}, u32[]{:S(2)}, u32[]{:S(2)}) collective-permute-start(bf16[8,48,128]{2,1,0:T(8,128)(2,1)S(1)} %get-tuple-element.55), channel_id=1, source_target_pairs={{0,32},{32,64},{64,96},{96,0},{1,33},{33,65},{65,97},{97,1},{2,34}... | collective-permute-start | bytes 294920 | tf_op jit(solution)/shard_map/ppermute | solution.py:169
  87.0 3.8 %collective-permute-start.17 = (bf16[8,48,128]{2,1,0:T(8,128)(2,1)S(1)}, bf16[8,48,128]{2,1,0:T(8,128)(2,1)S(1)}, u32[]{:S(2)}, u32[]{:S(2)}) collective-permute-start(bf16[8,48,128]{2,1,0:T(8,128)(2,1)S(1)} %get-tuple-element.56), channel_id=1, source_target_pairs={{0,96},{32,0},{64,32},{96,64},{1,97},{33,1},{65,33},{97,65},{2,98}... | collective-permute-start | bytes 294920 | tf_op jit(solution)/shard_map/ppermute | solution.py:169
  108.6 13.7 %collective-permute-start.18 = (f32[144,128]{1,0:T(8,128)S(1)}, f32[144,128]{1,0:T(8,128)S(1)}, u32[]{:S(2)}, u32[]{:S(2)}) collective-permute-start(f32[144,128]{1,0:T(8,128)S(1)} %get-tuple-element.57.own), channel_id=1, source_target_pairs={{0,1},{1,0},{2,3},{3,2},{4,5},{5,4},{6,7},{7,6},{8,9},{9,8},{10,11... | collective-permute-start | bytes 221192 | tf_op jit(solution)/shard_map/ppermute | solution.py:270
  112.8 5.5 %collective-permute-start.20 = (f32[48,128]{1,0:T(8,128)S(1)}, f32[48,128]{1,0:T(8,128)S(1)}, u32[]{:S(2)}, u32[]{:S(2)}) collective-permute-start(f32[48,128]{1,0:T(8,128)S(1)} %get-tuple-element.58), channel_id=1, source_target_pairs={{3,1},{5,3},{7,5},{9,7},{11,9},{13,11},{15,13},{17,15},{19,17},{21... | collective-permute-start | bytes 73736 | tf_op jit(solution)/shard_map/ppermute | solution.py:269
  116.2 6.0 %collective-permute-start.19 = (f32[48,128]{1,0:T(8,128)S(1)}, f32[48,128]{1,0:T(8,128)S(1)}, u32[]{:S(2)}, u32[]{:S(2)}) collective-permute-start(f32[48,128]{1,0:T(8,128)S(1)} %get-tuple-element.58), channel_id=1, source_target_pairs={{2,1},{4,3},{6,5},{8,7},{10,9},{12,11},{14,13},{16,15},{18,17},{20... | collective-permute-start | bytes 73736 | tf_op jit(solution)/shard_map/ppermute | solution.py:268
where the time goes:
time: 124 us; the launch traced here: 123 us
  Pallas kernels  40.2 us (32%)
  starting transfers between devices  36.9 us (30%)
  waiting for transfers between devices  22.3 us (18%)
  blocking collectives  17.7 us (14%)
  local copies, waits for them, and re-layouts  4.63 us (4%)
  between operations  1.49 us (1%)
    ppermute x12, starting transfers between devices, send(): lax.ppermute(blocks[step], axes, [(i, (i + step) % n) for i in range(n)])  20.8 us
    all_to_all x1, blocking collectives, reduce_terms(): return lax.all_to_all(ready, 'z', split_axis=0, concat_axis=0, tiled=True)  17.7 us
    pallas_call x1, Pallas kernels, forward_backward(): pl.pallas_call(main_kernel, out_shape=[wide, jax.ShapeDtypeStruct((2, ROW...  13.5 us
    ppermute x12, waiting for transfers between devices, send(): lax.ppermute(blocks[step], axes, [(i, (i + step) % n) for i in range(n)])  13.2 us
    pallas_call x1, Pallas kernels, outputs(): pl.pallas_call(outputs_kernel, out_shape=[wide, wide, jax.ShapeDtypeStruc...  10.8 us
    pallas_call x1, Pallas kernels, weight_blocks(): pl.pallas_call(weight_kernel, out_shape=blocks, in_specs=[vmem_spec()] +...  8.76 us
    pallas_call x1, Pallas kernels, early(): pl.pallas_call(early_kernel, out_shape=[wide, half, half], in_specs=[smem...  5.61 us
    ppermute x4, waiting for transfers between devices, pair_swap(): return lax.ppermute(array, 'c', [(0, 1), (1, 0)])  4.36 us
  transfers between devices with their start and end apart: 21, of which 8 were waited for; matrix products, arithmetic and copies ran while one was open for 0% of the time, Pallas kernels for 14%

commit v1 on v0

--- a/solution.py
+++ b/solution.py
@@ -178,7 +178,7 @@
     after_x = pl.pallas_call(
         first_x_kernel,
         out_shape=[block9] * 4,
-        in_specs=[vmem_spec()] * 5,
+        in_specs=[vmem_spec()] * 4 + [any_spec()],
         out_specs=[vmem_spec()] * 4,
         compiler_params=pltpu.CompilerParams(vmem_limit_bytes=8 << 20),
         name="sum_after_x",
@@ -301,31 +301,32 @@
     return (center * scale * gain).astype(BF)
 
 
+PART = 96
+
+
 def early_kernel(length_ref, gain_ref, xh, gh, normed_o, keep_o, give_o, x, g, sem, sem_out):
     core = lax.axis_index("c")
-    loads = [pltpu.make_async_copy(xh, x, sem.at[0]), pltpu.make_async_copy(gh, g, sem.at[1])]
+    parts = [pl.ds(PART * i, PART) for i in range(ROWS // PART)]
+    loads = [pltpu.make_async_copy(xh.at[p], x.at[p], sem.at[0, i]) for i, p in enumerate(parts)]
+    loads += [pltpu.make_async_copy(gh.at[p], g.at[p], sem.at[1, i]) for i, p in enumerate(parts)]
     for load in loads:
         load.start()
-    for load in loads:
-        load.wait()
     gain = gain_ref[...]
-
-    def step(i, _):
-        for j in range(2):
-            r = pl.multiple_of(i * 64 + 32 * j, 32)
-            rows = pl.ds(r, 32)
+    sends = []
+    for i, p in enumerate(parts):
+        loads[i].wait()
+        for j in range(0, PART, 16):
+            rows = pl.ds(PART * i + j, 16)
             x[rows, :] = normed_rows(x[rows, :], gain)
-            g[rows, :] = jnp.where(inside(length_ref, r, (32, 1024)), g[rows, :].astype(F32), 0.0).astype(BF)
-        return 0
-
-    lax.fori_loop(0, ROWS // 64, step, 0)
-    sends = [
-        pltpu.make_async_copy(x, normed_o, sem_out.at[0]),
-        pltpu.make_async_copy(g.at[:, pl.ds(core * 512, 512)], keep_o, sem_out.at[1]),
-        pltpu.make_async_copy(g.at[:, pl.ds(512 - core * 512, 512)], give_o, sem_out.at[2]),
-    ]
-    for copy in sends:
-        copy.start()
+        sends.append(pltpu.make_async_copy(x.at[p], normed_o.at[p], sem_out.at[0, i]))
+        sends[-1].start()
+    for i, p in enumerate(parts):
+        loads[len(parts) + i].wait()
+        valid = inside(length_ref, PART * i, (PART, 1024))
+        g[p, :] = jnp.where(valid, g[p, :].astype(F32), 0.0).astype(BF)
+        for k, (out, at) in enumerate(((keep_o, core * 512), (give_o, 512 - core * 512))):
+            sends.append(pltpu.make_async_copy(g.at[p, pl.ds(at, 512)], out.at[p], sem_out.at[1 + k, i]))
+            sends[-1].start()
     for copy in sends:
         copy.wait()
 
@@ -341,8 +342,8 @@
         scratch_shapes=[
             pltpu.VMEM((ROWS, 1024), BF),
             pltpu.VMEM((ROWS, 1024), BF),
-            pltpu.SemaphoreType.DMA((2,)),
-            pltpu.SemaphoreType.DMA((3,)),
+            pltpu.SemaphoreType.DMA((2, ROWS // PART)),
+            pltpu.SemaphoreType.DMA((3, ROWS // PART)),
         ],
         name="early",
     )(lengths, gain, x, g)
@@ -406,8 +407,9 @@
             for k in range(1, 9):
                 conv = conv + taps[k] * gat[h, pl.ds(r + k - 4, 56), :]
             s = jax.nn.sigmoid(conv)
-            acf[h, rows, :] = conv * s
-            grad = lifts[4 + h, rows, :] * s * (1.0 + conv * (1.0 - s))
+            active = conv * s
+            acf[h, rows, :] = active
+            grad = lifts[4 + h, rows, :] * (s + active * (1.0 - s))
             gcon[h, rows, :] = grad.astype(BF).astype(F32)
         sums = [jnp.zeros((8, 128), F32) for _ in range(9)]
         for i in range(8):

time: 124 us -> 123 us (level)
  the two profiles are of different devices: /device:TPU:11 before, /device:TPU:9 now
where the time goes in v1:
time: 123 us
  Pallas kernels  38.2 us (31%)
  starting transfers between devices  37.3 us (30%)
  waiting for transfers between devices  23.4 us (19%)
  blocking collectives  17.7 us (14%)
  local copies, waits for them, and re-layouts  4.64 us (4%)
  between operations  1.52 us (1%)
    ppermute x12, starting transfers between devices, send(): lax.ppermute(blocks[step], axes, [(i, (i + step) % n) for i in range(n)])  20.1 us
    all_to_all x1, blocking collectives, reduce_terms(): return lax.all_to_all(ready, 'z', split_axis=0, concat_axis=0, tiled=True)  17.7 us
    ppermute x12, waiting for transfers between devices, send(): lax.ppermute(blocks[step], axes, [(i, (i + step) % n) for i in range(n)])  14.3 us
    pallas_call x1, Pallas kernels, forward_backward(): pl.pallas_call(main_kernel, out_shape=[wide, jax.ShapeDtypeStruct((2, ROW...  13.5 us
    pallas_call x1, Pallas kernels, outputs(): pl.pallas_call(outputs_kernel, out_shape=[wide, wide, jax.ShapeDtypeStruc...  10.8 us
    pallas_call x1, Pallas kernels, weight_blocks(): pl.pallas_call(weight_kernel, out_shape=blocks, in_specs=[vmem_spec()] +...  8.76 us
    ppermute x1, waiting for transfers between devices, own_chunk(): next0 = lax.ppermute(head, ALL, [(2 * j, 2 * j - 1) for j in range(1, 128)])  4.73 us
    ppermute x1, starting transfers between devices, own_chunk(): lax.ppermute(head, ALL, [(2 * j + 1, 2 * j - 1) for j in range(1, 128)])  4.71 us
  transfers between devices with their start and end apart: 21, of which 6 were waited for; matrix products, arithmetic and copies ran while one was open for 0% of the time, Pallas kernels for 12%

profile of v1, /device:TPU:9, one launch (start us, length us, event | category | flops | bytes accessed | tf_op | source)
XLA Modules:
  0.0 122.8 jit_solution(16342557333447504469)
XLA Ops:
  0.6 0.8 fusion
  1.5 3.1 %collective-permute-start = (bf16[2,16,1024]{2,1,0:T(8,128)(2,1)S(1)}, bf16[2,16,1024]{2,1,0:T(8,128)(2,1)S(1)}, u32[]{:S(2)}, u32[]{:S(2)}) collective-permute-start(bf16[2,16,1024]{2,1,0:T(8,128)(2,1)S(1)} %pad_maximum_fusion), channel_id=1, source_target_pairs={{0,32},{32,64},{64,96},{96,128},{128,160},{160,192},{192,224},{1,3... | collective-permute-start | bytes 196616 | tf_op jit(solution)/shard_map/ppermute | solution.py:547
  4.6 1.3 %collective-permute-start.1 = (bf16[2,16,1024]{2,1,0:T(8,128)(2,1)S(1)}, bf16[2,16,1024]{2,1,0:T(8,128)(2,1)S(1)}, u32[]{:S(2)}, u32[]{:S(2)}) collective-permute-start(bf16[2,16,1024]{2,1,0:T(8,128)(2,1)S(1)} %pad_maximum_fusion.1), channel_id=1, source_target_pairs={{32,0},{64,32},{96,64},{128,96},{160,128},{192,160},{224,192},{33,... | collective-permute-start | bytes 196616 | tf_op jit(solution)/shard_map/ppermute | solution.py:548
  6.6 3.6 %early.1 = (bf16[384,1024]{1,0:T(8,128)(2,1)}, bf16[384,512]{1,0:T(8,128)(2,1)}, bf16[384,512]{1,0:T(8,128)(2,1)}) custom-call(s32[1]{0:T(128)S(6)} %copy.10.length_ref.info_ref, f32[1,1024]{1,0:T(1,128)} %bitcast.11, bf16[384,1024]{1,0:T(8,128)(2,1)} %bitcast.7, bf16[384,1024]{1,0:T(8,128)(2,1)} %bitcast.9), custom_call_target="tpu_custom_call" | custom-call | tf_op jit(solution)/shard_map/early/pallas_call | solution.py:337
  10.2 0.6 copy-done.9
  10.9 13.5 %forward_backward.1 = (bf16[384,1024]{1,0:T(8,128)(2,1)}, bf16[2,400,1024]{2,1,0:T(8,128)(2,1)}, bf16[400,1024]{1,0:T(8,128)(2,1)}, bf16[400,1024]{1,0:T(8,128)(2,1)}) custom-call(s32[1]{0:T(128)S(6)} %copy.10.length_ref.info_ref, f32[1,1024]{1,0:T(1,128)} %bitcast.12, f32[9,1024]{1,0:T(8,128)} %taps_ref.1, bf16[384,1024]{1,0:T(8,128)(2,1)} %get-tuple-element.31.nh.n0h, ...), custom_call_target="tpu_custom_call" | custom-call | tf_op jit(solution)/shard_map/forward_backward/pallas_call | solution.py:459
  24.3 1.6 %collective-permute-start.3 = (bf16[400,1024]{1,0:T(8,128)(2,1)}, bf16[400,1024]{1,0:T(8,128)(2,1)S(1)}, u32[]{:S(2)}, u32[]{:S(2)}) collective-permute-start(bf16[400,1024]{1,0:T(8,128)(2,1)} %get-tuple-element.37), channel_id=1, source_target_pairs={{0,1},{1,0},{2,3},{3,2},{4,5},{5,4},{6,7},{7,6},{8,9},{9,8},{10,11... | collective-permute-start | bytes 2457608 | tf_op jit(solution)/shard_map/ppermute | solution.py:284
  26.0 0.4 collective-permute-start.4
  26.5 4.4 %collective-permute-done.5.g1h = bf16[384,512]{1,0:T(8,128)(2,1)S(1)} collective-permute-done((bf16[384,512]{1,0:T(8,128)(2,1)S(1)}, bf16[384,512]{1,0:T(8,128)(2,1)S(1)}, u32[]{:S(2)}, u32[]{:S(2)}) %collective-permute-start.5) | collective-permute-done | bytes 393248 | tf_op jit(solution)/shard_map/ppermute | solution.py:284
  30.9 0.7 copy-done.7
  32.4 8.8 %weight_grads.1 = (bf16[33,48,128]{2,1,0:T(8,128)(2,1)}, bf16[33,48,128]{2,1,0:T(8,128)(2,1)}, bf16[33,48,128]{2,1,0:T(8,128)(2,1)}, bf16[33,48,128]{2,1,0:T(8,1...) custom-call(f32[1,1024]{1,0:T(1,128)} %bitcast.13, ...), custom_call_target="tpu_custom_call" | custom-call | tf_op jit(solution)/shard_map/weight_grads/pallas_call | solution.py:114
  41.2 6.3 %collective-permute-start.12 = (bf16[32,48,128]{2,1,0:T(8,128)(2,1)}, bf16[32,48,128]{2,1,0:T(8,128)(2,1)S(1)}, u32[]{:S(2)}, u32[]{:S(2)}) collective-permute-start(bf16[32,48,128]{2,1,0:T(8,128)(2,1)} %get-tuple-element.50), channel_id=1, source_target_pairs={{0,128},{2,130},{128,0},{130,2},{1,129},{3,131},{129,1},{131,3},{4... | collective-permute-start | bytes 1179656 | tf_op jit(solution)/shard_map/ppermute | solution.py:169
  47.5 1.5 %collective-permute-start.14 = (bf16[32,48,128]{2,1,0:T(8,128)(2,1)}, bf16[32,48,128]{2,1,0:T(8,128)(2,1)S(1)}, u32[]{:S(2)}, u32[]{:S(2)}) collective-permute-start(bf16[32,48,128]{2,1,0:T(8,128)(2,1)} %get-tuple-element.52), channel_id=1, source_target_pairs={{0,130},{2,0},{128,2},{130,128},{1,131},{3,1},{129,3},{131,129},{4... | collective-permute-start | bytes 1179656 | tf_op jit(solution)/shard_map/ppermute | solution.py:169
  49.0 1.9 %collective-permute-start.7 = (bf16[33,48,128]{2,1,0:T(8,128)(2,1)}, bf16[33,48,128]{2,1,0:T(8,128)(2,1)S(1)}, u32[]{:S(2)}, u32[]{:S(2)}) collective-permute-start(bf16[33,48,128]{2,1,0:T(8,128)(2,1)} %get-tuple-element.42), channel_id=1, source_target_pairs={{0,32},{32,64},{64,96},{96,0},{1,33},{33,65},{65,97},{97,1},{2,34}... | collective-permute-start | bytes 1216520 | tf_op jit(solution)/shard_map/ppermute | solution.py:169
  50.9 6.0 %collective-permute-done.12.i1 = bf16[32,48,128]{2,1,0:T(8,128)(2,1)S(1)} collective-permute-done((bf16[32,48,128]{2,1,0:T(8,128)(2,1)}, bf16[32,48,128]{2,1,0:T(8,128)(2,1)S(1)}, u32[]{:S(2)}, u32[]{:S(2)}) %collective-permute-start.12) | collective-permute-done | bytes 393248 | tf_op jit(solution)/shard_map/ppermute | solution.py:169
  56.9 3.2 %collective-permute-start.8 = (bf16[33,48,128]{2,1,0:T(8,128)(2,1)}, bf16[33,48,128]{2,1,0:T(8,128)(2,1)S(1)}, u32[]{:S(2)}, u32[]{:S(2)}) collective-permute-start(bf16[33,48,128]{2,1,0:T(8,128)(2,1)} %get-tuple-element.43), channel_id=1, source_target_pairs={{0,96},{32,0},{64,32},{96,64},{1,97},{33,1},{65,33},{97,65},{2,98}... | collective-permute-start | bytes 1216520 | tf_op jit(solution)/shard_map/ppermute | solution.py:169
  60.1 6.0 %collective-permute-done.13.i2 = bf16[32,48,128]{2,1,0:T(8,128)(2,1)S(1)} collective-permute-done((bf16[32,48,128]{2,1,0:T(8,128)(2,1)}, bf16[32,48,128]{2,1,0:T(8,128)(2,1)S(1)}, u32[]{:S(2)}, u32[]{:S(2)}) %collective-permute-start.13) | collective-permute-done | bytes 393248 | tf_op jit(solution)/shard_map/ppermute | solution.py:169
  66.1 1.0 copy-done.1
  67.6 10.8 %outputs.1 = (bf16[384,1024]{1,0:T(8,128)(2,1)}, bf16[384,1024]{1,0:T(8,128)(2,1)}, f32[8,128]{1,0:T(8,128)}) custom-call(s32[1]{0:T(128)S(6)} %copy.10.length_ref.info_ref, f32[1,1024]{1,0:T(1,128)} %bitcast.14, bf16[384,1024]{1,0:T(8,128)(2,1)} %bitcast.8, bf16[384,1024]{1,0:T(8,128)(2,1)} %bitcast.10, bf16[384,1024]{1,0:T(8,128)(2,1)} %get-tuple-element.34.a0h.acth, ...), custom_call_target="tpu_custom_call" | custom-call | tf_op jit(solution)/shard_map/outputs/pallas_call | solution.py:523
  78.5 0.7 copy-done.2
  79.4 2.7 %collective-permute-start.9 = (bf16[9,48,128]{2,1,0:T(8,128)(2,1)S(1)}, bf16[9,48,128]{2,1,0:T(8,128)(2,1)S(1)}, u32[]{:S(2)}, u32[]{:S(2)}) collective-permute-start(bf16[9,48,128]{2,1,0:T(8,128)(2,1)S(1)} %get-tuple-element.46), channel_id=1, source_target_pairs={{0,128},{2,130},{128,0},{130,2},{1,129},{3,131},{129,1},{131,3},{4... | collective-permute-start | bytes 331784 | tf_op jit(solution)/shard_map/ppermute | solution.py:169
  82.1 1.5 %collective-permute-start.11 = (bf16[9,48,128]{2,1,0:T(8,128)(2,1)S(1)}, bf16[9,48,128]{2,1,0:T(8,128)(2,1)S(1)}, u32[]{:S(2)}, u32[]{:S(2)}) collective-permute-start(bf16[9,48,128]{2,1,0:T(8,128)(2,1)S(1)} %get-tuple-element.48), channel_id=1, source_target_pairs={{0,130},{2,0},{128,2},{130,128},{1,131},{3,1},{129,3},{131,129},{4... | collective-permute-start | bytes 331784 | tf_op jit(solution)/shard_map/ppermute | solution.py:169
  83.5 1.5 %collective-permute-start.16 = (bf16[8,48,128]{2,1,0:T(8,128)(2,1)S(1)}, bf16[8,48,128]{2,1,0:T(8,128)(2,1)S(1)}, u32[]{:S(2)}, u32[]{:S(2)}) collective-permute-start(bf16[8,48,128]{2,1,0:T(8,128)(2,1)S(1)} %get-tuple-element.55), channel_id=1, source_target_pairs={{0,32},{32,64},{64,96},{96,0},{1,33},{33,65},{65,97},{97,1},{2,34}... | collective-permute-start | bytes 294920 | tf_op jit(solution)/shard_map/ppermute | solution.py:169
  85.1 1.1 collective-permute-start.17
  86.2 2.0 %collective-permute-done.16.b2 = bf16[8,48,128]{2,1,0:T(8,128)(2,1)S(1)} collective-permute-done((bf16[8,48,128]{2,1,0:T(8,128)(2,1)S(1)}, bf16[8,48,128]{2,1,0:T(8,128)(2,1)S(1)}, u32[]{:S(2)}, u32[]{:S(2)}) %collective-permute-start.16) | collective-permute-done | bytes 98336 | tf_op jit(solution)/shard_map/ppermute | solution.py:169
  88.2 0.3 collective-permute-done.17.b3
  88.7 17.7 %all_to_all.5.parts = bf16[8,144,128]{2,1,0:T(8,128)(2,1)S(1)} all-to-all(bf16[8,144,128]{2,1,0:T(8,128)(2,1)S(1)} %sum_before_z.1), channel_id=1, replica_groups=mesh['yh'=2,'x'=4,'z'=8,'yl'=2,'c'=2] {'z'}, dimensions={0} | all-to-all | bytes 589824 | tf_op jit(solution)/shard_map/all_to_all | solution.py:204
  106.4 4.6 %collective-permute-start.18 = (f32[144,128]{1,0:T(8,128)S(1)}, f32[144,128]{1,0:T(8,128)S(1)}, u32[]{:S(2)}, u32[]{:S(2)}) collective-permute-start(f32[144,128]{1,0:T(8,128)S(1)} %get-tuple-element.57.own), channel_id=1, source_target_pairs={{0,1},{1,0},{2,3},{3,2},{4,5},{5,4},{6,7},{7,6},{8,9},{9,8},{10,11... | collective-permute-start | bytes 221192 | tf_op jit(solution)/shard_map/ppermute | solution.py:270
  111.0 4.7 %collective-permute-start.20 = (f32[48,128]{1,0:T(8,128)S(1)}, f32[48,128]{1,0:T(8,128)S(1)}, u32[]{:S(2)}, u32[]{:S(2)}) collective-permute-start(f32[48,128]{1,0:T(8,128)S(1)} %get-tuple-element.58), channel_id=1, source_target_pairs={{3,1},{5,3},{7,5},{9,7},{11,9},{13,11},{15,13},{17,15},{19,17},{21... | collective-permute-start | bytes 73736 | tf_op jit(solution)/shard_map/ppermute | solution.py:269
  115.7 1.3 %collective-permute-start.19 = (f32[48,128]{1,0:T(8,128)S(1)}, f32[48,128]{1,0:T(8,128)S(1)}, u32[]{:S(2)}, u32[]{:S(2)}) collective-permute-start(f32[48,128]{1,0:T(8,128)S(1)} %get-tuple-element.58), channel_id=1, source_target_pairs={{2,1},{4,3},{6,5},{8,7},{10,9},{12,11},{14,13},{16,15},{18,17},{20... | collective-permute-start | bytes 73736 | tf_op jit(solution)/shard_map/ppermute | solution.py:268
  117.1 4.7 %collective-permute-done.19.next0 = f32[48,128]{1,0:T(8,128)S(1)} collective-permute-done((f32[48,128]{1,0:T(8,128)S(1)}, f32[48,128]{1,0:T(8,128)S(1)}, u32[]{:S(2)}, u32[]{:S(2)}) %collective-permute-start.19) | collective-permute-done | bytes 24608 | tf_op jit(solution)/shard_map/ppermute | solution.py:268
  121.8 1.0 own_chunk.1
  (45 shorter events, 2.0 us)
Async XLA Ops:
  1.5 8.7 %collective-permute-start = (bf16[2,16,1024]{2,1,0:T(8,128)(2,1)S(1)}, bf16[2,16,1024]{2,1,0:T(8,128)(2,1)S(1)}, u32[]{:S(2)}, u32[]{:S(2)}) collective-permute-start(bf16[2,16,1024]{2,1,0:T(8,128)(2,1)S(1)} %pad_maximum_fusion), channel_id=1, source_target_pairs={{0,32},{32,64},{64,96},{96,128},{128,160},{160,192},{192,224},{1,3... | collective-permute-start | bytes 196616 | tf_op jit(solution)/shard_map/ppermute | solution.py:547
  4.6 5.6 %collective-permute-start.1 = (bf16[2,16,1024]{2,1,0:T(8,128)(2,1)S(1)}, bf16[2,16,1024]{2,1,0:T(8,128)(2,1)S(1)}, u32[]{:S(2)}, u32[]{:S(2)}) collective-permute-start(bf16[2,16,1024]{2,1,0:T(8,128)(2,1)S(1)} %pad_maximum_fusion.1), channel_id=1, source_target_pairs={{32,0},{64,32},{96,64},{128,96},{160,128},{192,160},{224,192},{33,... | collective-permute-start | bytes 196616 | tf_op jit(solution)/shard_map/ppermute | solution.py:548
  10.2 0.6 copy-start.9
  10.2 0.6 copy-start.10
  10.9 15.0 %copy-start.3 = (bf16[384,1024]{1,0:T(8,128)(2,1)S(1)}, bf16[384,1024]{1,0:T(8,128)(2,1)}, u32[]{:S(2)}) copy-start(bf16[384,1024]{1,0:T(8,128)(2,1)} %get-tuple-element.31.nh.n0h) | copy-start | bytes 2359300
  10.9 15.5 %copy-start.8 = (bf16[384,512]{1,0:T(8,128)(2,1)S(1)}, bf16[384,512]{1,0:T(8,128)(2,1)}, u32[]{:S(2)}) copy-start(bf16[384,512]{1,0:T(8,128)(2,1)} %get-tuple-element.33.ggh) | copy-start | bytes 1179652
  24.3 6.6 %collective-permute-start.3 = (bf16[400,1024]{1,0:T(8,128)(2,1)}, bf16[400,1024]{1,0:T(8,128)(2,1)S(1)}, u32[]{:S(2)}, u32[]{:S(2)}) collective-permute-start(bf16[400,1024]{1,0:T(8,128)(2,1)} %get-tuple-element.37), channel_id=1, source_target_pairs={{0,1},{1,0},{2,3},{3,2},{4,5},{5,4},{6,7},{7,6},{8,9},{9,8},{10,11... | collective-permute-start | bytes 2457608 | tf_op jit(solution)/shard_map/ppermute | solution.py:284
  25.9 5.0 %collective-permute-start.2 = (bf16[384,1024]{1,0:T(8,128)(2,1)S(1)}, bf16[384,1024]{1,0:T(8,128)(2,1)S(1)}, u32[]{:S(2)}, u32[]{:S(2)}) collective-permute-start(bf16[384,1024]{1,0:T(8,128)(2,1)S(1)} %copy-done.3), channel_id=1, source_target_pairs={{0,1},{1,0},{2,3},{3,2},{4,5},{5,4},{6,7},{7,6},{8,9},{9,8},{10,11... | collective-permute-start | bytes 2359304 | tf_op jit(solution)/shard_map/ppermute | solution.py:284
  26.0 4.9 %collective-permute-start.4 = (bf16[384,1024]{1,0:T(8,128)(2,1)}, bf16[384,1024]{1,0:T(8,128)(2,1)S(1)}, u32[]{:S(2)}, u32[]{:S(2)}) collective-permute-start(bf16[384,1024]{1,0:T(8,128)(2,1)} %get-tuple-element.34.a0h.acth), channel_id=1, source_target_pairs={{0,1},{1,0},{2,3},{3,2},{4,5},{5,4},{6,7},{7,6},{8,9},{9,8},{10,11... | collective-permute-start | bytes 2359304 | tf_op jit(solution)/shard_map/ppermute | solution.py:284
  26.4 4.5 %collective-permute-start.5 = (bf16[384,512]{1,0:T(8,128)(2,1)S(1)}, bf16[384,512]{1,0:T(8,128)(2,1)S(1)}, u32[]{:S(2)}, u32[]{:S(2)}) collective-permute-start(bf16[384,512]{1,0:T(8,128)(2,1)S(1)} %copy-done.8), channel_id=1, source_target_pairs={{0,1},{1,0},{2,3},{3,2},{4,5},{5,4},{6,7},{7,6},{8,9},{9,8},{10,11... | collective-permute-start | bytes 1179656 | tf_op jit(solution)/shard_map/ppermute | solution.py:284
  30.9 0.7 copy-start.7
  30.9 1.0 copy-start.5
  30.9 1.3 %copy-start.6 = (bf16[384,1024]{1,0:T(8,128)(2,1)}, bf16[384,1024]{1,0:T(8,128)(2,1)S(1)}, u32[]{:S(2)}) copy-start(bf16[384,1024]{1,0:T(8,128)(2,1)S(1)} %collective-permute-done.4.a1h) | copy-start | bytes 2359300
  30.9 1.5 %copy-start.4 = (bf16[400,1024]{1,0:T(8,128)(2,1)}, bf16[400,1024]{1,0:T(8,128)(2,1)S(1)}, u32[]{:S(2)}) copy-start(bf16[400,1024]{1,0:T(8,128)(2,1)S(1)} %collective-permute-done.3.k1h) | copy-start | bytes 2457604
  41.2 15.7 %collective-permute-start.12 = (bf16[32,48,128]{2,1,0:T(8,128)(2,1)}, bf16[32,48,128]{2,1,0:T(8,128)(2,1)S(1)}, u32[]{:S(2)}, u32[]{:S(2)}) collective-permute-start(bf16[32,48,128]{2,1,0:T(8,128)(2,1)} %get-tuple-element.50), channel_id=1, source_target_pairs={{0,128},{2,130},{128,0},{130,2},{1,129},{3,131},{129,1},{131,3},{4... | collective-permute-start | bytes 1179656 | tf_op jit(solution)/shard_map/ppermute | solution.py:169
  47.5 18.6 %collective-permute-start.13 = (bf16[32,48,128]{2,1,0:T(8,128)(2,1)}, bf16[32,48,128]{2,1,0:T(8,128)(2,1)S(1)}, u32[]{:S(2)}, u32[]{:S(2)}) collective-permute-start(bf16[32,48,128]{2,1,0:T(8,128)(2,1)} %get-tuple-element.51), channel_id=1, source_target_pairs={{0,2},{2,128},{128,130},{130,0},{1,3},{3,129},{129,131},{131,1},{4... | collective-permute-start | bytes 1179656 | tf_op jit(solution)/shard_map/ppermute | solution.py:169
  47.5 18.6 %collective-permute-start.14 = (bf16[32,48,128]{2,1,0:T(8,128)(2,1)}, bf16[32,48,128]{2,1,0:T(8,128)(2,1)S(1)}, u32[]{:S(2)}, u32[]{:S(2)}) collective-permute-start(bf16[32,48,128]{2,1,0:T(8,128)(2,1)} %get-tuple-element.52), channel_id=1, source_target_pairs={{0,130},{2,0},{128,2},{130,128},{1,131},{3,1},{129,3},{131,129},{4... | collective-permute-start | bytes 1179656 | tf_op jit(solution)/shard_map/ppermute | solution.py:169
  49.0 29.4 %collective-permute-start.6 = (bf16[33,48,128]{2,1,0:T(8,128)(2,1)}, bf16[33,48,128]{2,1,0:T(8,128)(2,1)S(1)}, u32[]{:S(2)}, u32[]{:S(2)}) collective-permute-start(bf16[33,48,128]{2,1,0:T(8,128)(2,1)} %get-tuple-element.41), channel_id=1, source_target_pairs={{0,64},{32,96},{64,0},{96,32},{1,65},{33,97},{65,1},{97,33},{2,66}... | collective-permute-start | bytes 1216520 | tf_op jit(solution)/shard_map/ppermute | solution.py:169
  49.0 29.4 %collective-permute-start.7 = (bf16[33,48,128]{2,1,0:T(8,128)(2,1)}, bf16[33,48,128]{2,1,0:T(8,128)(2,1)S(1)}, u32[]{:S(2)}, u32[]{:S(2)}) collective-permute-start(bf16[33,48,128]{2,1,0:T(8,128)(2,1)} %get-tuple-element.42), channel_id=1, source_target_pairs={{0,32},{32,64},{64,96},{96,0},{1,33},{33,65},{65,97},{97,1},{2,34}... | collective-permute-start | bytes 1216520 | tf_op jit(solution)/shard_map/ppermute | solution.py:169
  56.9 21.5 %collective-permute-start.8 = (bf16[33,48,128]{2,1,0:T(8,128)(2,1)}, bf16[33,48,128]{2,1,0:T(8,128)(2,1)S(1)}, u32[]{:S(2)}, u32[]{:S(2)}) collective-permute-start(bf16[33,48,128]{2,1,0:T(8,128)(2,1)} %get-tuple-element.43), channel_id=1, source_target_pairs={{0,96},{32,0},{64,32},{96,64},{1,97},{33,1},{65,33},{97,65},{2,98}... | collective-permute-start | bytes 1216520 | tf_op jit(solution)/shard_map/ppermute | solution.py:169
  66.1 1.0 copy-start.1
  67.3 17.8 %collective-permute-start.15 = (bf16[8,48,128]{2,1,0:T(8,128)(2,1)S(1)}, bf16[8,48,128]{2,1,0:T(8,128)(2,1)S(1)}, u32[]{:S(2)}, u32[]{:S(2)}) collective-permute-start(bf16[8,48,128]{2,1,0:T(8,128)(2,1)S(1)} %get-tuple-element.54), channel_id=1, source_target_pairs={{0,64},{32,96},{64,0},{96,32},{1,65},{33,97},{65,1},{97,33},{2,66}... | collective-permute-start | bytes 294920 | tf_op jit(solution)/shard_map/ppermute | solution.py:169
  67.6 10.8 %copy-start = (bf16[33,48,128]{2,1,0:T(8,128)(2,1)S(1)}, bf16[33,48,128]{2,1,0:T(8,128)(2,1)}, u32[]{:S(2)}) copy-start(bf16[33,48,128]{2,1,0:T(8,128)(2,1)} %get-tuple-element.38.after_this.i0) | copy-start | bytes 1216516
  78.5 0.7 copy-start.2
  79.4 9.2 %collective-permute-start.9 = (bf16[9,48,128]{2,1,0:T(8,128)(2,1)S(1)}, bf16[9,48,128]{2,1,0:T(8,128)(2,1)S(1)}, u32[]{:S(2)}, u32[]{:S(2)}) collective-permute-start(bf16[9,48,128]{2,1,0:T(8,128)(2,1)S(1)} %get-tuple-element.46), channel_id=1, source_target_pairs={{0,128},{2,130},{128,0},{130,2},{1,129},{3,131},{129,1},{131,3},{4... | collective-permute-start | bytes 331784 | tf_op jit(solution)/shard_map/ppermute | solution.py:169
  82.1 6.5 %collective-permute-start.10 = (bf16[9,48,128]{2,1,0:T(8,128)(2,1)S(1)}, bf16[9,48,128]{2,1,0:T(8,128)(2,1)S(1)}, u32[]{:S(2)}, u32[]{:S(2)}) collective-permute-start(bf16[9,48,128]{2,1,0:T(8,128)(2,1)S(1)} %get-tuple-element.47), channel_id=1, source_target_pairs={{0,2},{2,128},{128,130},{130,0},{1,3},{3,129},{129,131},{131,1},{4... | collective-permute-start | bytes 331784 | tf_op jit(solution)/shard_map/ppermute | solution.py:169
  82.1 6.5 %collective-permute-start.11 = (bf16[9,48,128]{2,1,0:T(8,128)(2,1)S(1)}, bf16[9,48,128]{2,1,0:T(8,128)(2,1)S(1)}, u32[]{:S(2)}, u32[]{:S(2)}) collective-permute-start(bf16[9,48,128]{2,1,0:T(8,128)(2,1)S(1)} %get-tuple-element.48), channel_id=1, source_target_pairs={{0,130},{2,0},{128,2},{130,128},{1,131},{3,1},{129,3},{131,129},{4... | collective-permute-start | bytes 331784 | tf_op jit(solution)/shard_map/ppermute | solution.py:169
  83.5 4.7 %collective-permute-start.16 = (bf16[8,48,128]{2,1,0:T(8,128)(2,1)S(1)}, bf16[8,48,128]{2,1,0:T(8,128)(2,1)S(1)}, u32[]{:S(2)}, u32[]{:S(2)}) collective-permute-start(bf16[8,48,128]{2,1,0:T(8,128)(2,1)S(1)} %get-tuple-element.55), channel_id=1, source_target_pairs={{0,32},{32,64},{64,96},{96,0},{1,33},{33,65},{65,97},{97,1},{2,34}... | collective-permute-start | bytes 294920 | tf_op jit(solution)/shard_map/ppermute | solution.py:169
  85.1 3.5 %collective-permute-start.17 = (bf16[8,48,128]{2,1,0:T(8,128)(2,1)S(1)}, bf16[8,48,128]{2,1,0:T(8,128)(2,1)S(1)}, u32[]{:S(2)}, u32[]{:S(2)}) collective-permute-start(bf16[8,48,128]{2,1,0:T(8,128)(2,1)S(1)} %get-tuple-element.56), channel_id=1, source_target_pairs={{0,96},{32,0},{64,32},{96,64},{1,97},{33,1},{65,33},{97,65},{2,98}... | collective-permute-start | bytes 294920 | tf_op jit(solution)/shard_map/ppermute | solution.py:169
  106.4 15.4 %collective-permute-start.18 = (f32[144,128]{1,0:T(8,128)S(1)}, f32[144,128]{1,0:T(8,128)S(1)}, u32[]{:S(2)}, u32[]{:S(2)}) collective-permute-start(f32[144,128]{1,0:T(8,128)S(1)} %get-tuple-element.57.own), channel_id=1, source_target_pairs={{0,1},{1,0},{2,3},{3,2},{4,5},{5,4},{6,7},{7,6},{8,9},{9,8},{10,11... | collective-permute-start | bytes 221192 | tf_op jit(solution)/shard_map/ppermute | solution.py:270
  111.0 6.0 %collective-permute-start.20 = (f32[48,128]{1,0:T(8,128)S(1)}, f32[48,128]{1,0:T(8,128)S(1)}, u32[]{:S(2)}, u32[]{:S(2)}) collective-permute-start(f32[48,128]{1,0:T(8,128)S(1)} %get-tuple-element.58), channel_id=1, source_target_pairs={{3,1},{5,3},{7,5},{9,7},{11,9},{13,11},{15,13},{17,15},{19,17},{21... | collective-permute-start | bytes 73736 | tf_op jit(solution)/shard_map/ppermute | solution.py:269
  115.7 6.0 %collective-permute-start.19 = (f32[48,128]{1,0:T(8,128)S(1)}, f32[48,128]{1,0:T(8,128)S(1)}, u32[]{:S(2)}, u32[]{:S(2)}) collective-permute-start(f32[48,128]{1,0:T(8,128)S(1)} %get-tuple-element.58), channel_id=1, source_target_pairs={{2,1},{4,3},{6,5},{8,7},{10,9},{12,11},{14,13},{16,15},{18,17},{20... | collective-permute-start | bytes 73736 | tf_op jit(solution)/shard_map/ppermute | solution.py:268

commit v2 on v1

--- a/solution.py
+++ b/solution.py
@@ -58,11 +58,13 @@
             )
         )
     ]
-    for load in loads:
+    for load in loads[:4]:
         load.start()
     contract = (((0,), (0,)), ((), ()))
     for load in loads[:4]:
         load.wait()
+    for load in loads[4:]:
+        load.start()
     for m in range(4):
         cols = slice(256 * m, 256 * m + 256)
         done = lax.dot_general(a0[:, cols], g0[...], contract, preferred_element_type=F32)
@@ -207,15 +209,14 @@
 ALL = ("yh", "x", "z", "yl", "c")
 
 
-def total_kernel(parts, total, head):
+def total_kernel(parts, total):
     done = parts[0].astype(F32)
     for z in range(1, 8):
         done = done + parts[z].astype(F32)
     total[...] = done
-    head[...] = done[0:48, :]
-
-
-def chunk_kernel(own, other, next0, next1, out, half0, half1, flat, *, chunk, scale):
+
+
+def chunk_kernel(own, other, follow, out, half0, half1, flat, *, chunk, scale):
     core = lax.axis_index("c")
     chip = lax.axis_index(("yh", "x", "z", "yl"))
     first = core == 0
@@ -226,8 +227,8 @@
     small1 = jnp.where(first, others[96:144], mine[96:144])
     both = small0[40:48] + small1[40:48]
     last = chip == 127
-    half0[96:144, :] = jnp.where(last, small0, next0[...])
-    half1[96:144, :] = jnp.where(last, small1, next1[...])
+    half0[96:144, :] = jnp.where(last, small0, follow[0:48])
+    half1[96:144, :] = jnp.where(last, small1, follow[48:96])
 
     @pl.when(last)
     def _():
@@ -257,26 +258,26 @@
 
 
 def own_chunk(swapped, chunk, grad_scale):
-    total, head = pl.pallas_call(
+    total = pl.pallas_call(
         total_kernel,
-        out_shape=[jax.ShapeDtypeStruct((144, 128), F32), jax.ShapeDtypeStruct((48, 128), F32)],
+        out_shape=jax.ShapeDtypeStruct((144, 128), F32),
         in_specs=[vmem_spec()],
-        out_specs=[vmem_spec()] * 2,
+        out_specs=vmem_spec(),
         compiler_params=pltpu.CompilerParams(vmem_limit_bytes=4 << 20),
         name="sum_after_z",
     )(swapped)
-    next0 = lax.ppermute(head, ALL, [(2 * j, 2 * j - 1) for j in range(1, 128)])
-    next1 = lax.ppermute(head, ALL, [(2 * j + 1, 2 * j - 1) for j in range(1, 128)])
     other = lax.ppermute(total, "c", [(0, 1), (1, 0)])
+    heads = jnp.concatenate([other[:48], total[:48]])
+    follow = lax.ppermute(heads, ALL, [(2 * j + 1, 2 * j - 1) for j in range(1, 128)])
     out = pl.pallas_call(
         functools.partial(chunk_kernel, chunk=chunk, scale=grad_scale),
         out_shape=jax.ShapeDtypeStruct((104, 128), F32),
-        in_specs=[vmem_spec()] * 4,
+        in_specs=[vmem_spec()] * 3,
         out_specs=vmem_spec(),
         scratch_shapes=[pltpu.VMEM((144, 128), F32), pltpu.VMEM((144, 128), F32), pltpu.VMEM((312, 128), F32)],
         compiler_params=pltpu.CompilerParams(vmem_limit_bytes=4 << 20),
         name="own_chunk",
-    )(total, other, next0, next1)
+    )(total, other, follow)
     return out.reshape(-1)[:chunk]
 
 
@@ -367,7 +368,7 @@
         pairs.append((wh.at[:, pl.ds(1024 + 256 * n, 256)], w.at[:, pl.ds(1024 + 256 * n, 256)]))
         pairs.append((pwh.at[pl.ds(256 * n, 256)], pw.at[pl.ds(256 * n, 256)]))
     loads = [pltpu.make_async_copy(src, dst, sem.at[i]) for i, (src, dst) in enumerate(pairs)]
-    for load in loads:
+    for load in loads[:10]:
         load.start()
     mask[...] = inside(info_ref, -EDGE, (LONG, 128)).astype(F32)
     krows[...] = jnp.zeros((2, 16, 1024), F32)
@@ -379,6 +380,8 @@
         gs[rows, :] = jnp.where(inside(info_ref, first - EDGE, (EDGE, 1024)), gs[rows, :].astype(F32), 0.0).astype(BF)
     for load in loads[4:7]:
         load.wait()
+    for load in loads[10:]:
+        load.start()
 
     def multiply(n, lifts):
         for load in loads[7 + 3 * n : 10 + 3 * n]:

time: 123 us -> 123 us (level)
  the two profiles are of different devices: /device:TPU:9 before, /device:TPU:1 now
where the time goes in v2:
time: 123 us; the launch traced here: 122 us
  Pallas kernels  39.3 us (32%)
  starting transfers between devices  35.6 us (29%)
  waiting for transfers between devices  23.6 us (19%)
  blocking collectives  17.7 us (14%)
  local copies, waits for them, and re-layouts  4.66 us (4%)
  between operations  1.5 us (1%)
    ppermute x12, starting transfers between devices, send(): lax.ppermute(blocks[step], axes, [(i, (i + step) % n) for i in range(n)])  21.9 us
    all_to_all x1, blocking collectives, reduce_terms(): return lax.all_to_all(ready, 'z', split_axis=0, concat_axis=0, tiled=True)  17.7 us
    ppermute x12, waiting for transfers between devices, send(): lax.ppermute(blocks[step], axes, [(i, (i + step) % n) for i in range(n)])  14.8 us
    pallas_call x1, Pallas kernels, forward_backward(): pl.pallas_call(main_kernel, out_shape=[wide, jax.ShapeDtypeStruct((2, ROW...  13.7 us
    pallas_call x1, Pallas kernels, outputs(): pl.pallas_call(outputs_kernel, out_shape=[wide, wide, jax.ShapeDtypeStruc...  10.8 us
    pallas_call x1, Pallas kernels, weight_blocks(): pl.pallas_call(weight_kernel, out_shape=blocks, in_specs=[vmem_spec()] +...  9.64 us
    ppermute x1, starting transfers between devices, own_chunk(): other = lax.ppermute(total, 'c', [(0, 1), (1, 0)])  5 us
    ppermute x4, waiting for transfers between devices, pair_swap(): return lax.ppermute(array, 'c', [(0, 1), (1, 0)])  4.36 us
  transfers between devices with their start and end apart: 20, of which 7 were waited for; matrix products, arithmetic and copies ran while one was open for 0% of the time, Pallas kernels for 12%

profile of v2, /device:TPU:1, one launch (start us, length us, event | category | flops | bytes accessed | tf_op | source)
XLA Modules:
  0.0 122.4 jit_solution(10349180388124431146)
XLA Ops:
  0.6 0.8 fusion
  1.5 3.9 %collective-permute-start = (bf16[2,16,1024]{2,1,0:T(8,128)(2,1)S(1)}, bf16[2,16,1024]{2,1,0:T(8,128)(2,1)S(1)}, u32[]{:S(2)}, u32[]{:S(2)}) collective-permute-start(bf16[2,16,1024]{2,1,0:T(8,128)(2,1)S(1)} %pad_maximum_fusion), channel_id=1, source_target_pairs={{0,32},{32,64},{64,96},{96,128},{128,160},{160,192},{192,224},{1,3... | collective-permute-start | bytes 196616 | tf_op jit(solution)/shard_map/ppermute | solution.py:550
  5.4 1.3 %collective-permute-start.1 = (bf16[2,16,1024]{2,1,0:T(8,128)(2,1)S(1)}, bf16[2,16,1024]{2,1,0:T(8,128)(2,1)S(1)}, u32[]{:S(2)}, u32[]{:S(2)}) collective-permute-start(bf16[2,16,1024]{2,1,0:T(8,128)(2,1)S(1)} %pad_maximum_fusion.1), channel_id=1, source_target_pairs={{32,0},{64,32},{96,64},{128,96},{160,128},{192,160},{224,192},{33,... | collective-permute-start | bytes 196616 | tf_op jit(solution)/shard_map/ppermute | solution.py:551
  7.4 3.6 %early.1 = (bf16[384,1024]{1,0:T(8,128)(2,1)}, bf16[384,512]{1,0:T(8,128)(2,1)}, bf16[384,512]{1,0:T(8,128)(2,1)}) custom-call(s32[1]{0:T(128)S(6)} %copy.10.length_ref.info_ref, f32[1,1024]{1,0:T(1,128)} %bitcast.11, bf16[384,1024]{1,0:T(8,128)(2,1)} %bitcast.7, bf16[384,1024]{1,0:T(8,128)(2,1)} %bitcast.9), custom_call_target="tpu_custom_call" | custom-call | tf_op jit(solution)/shard_map/early/pallas_call | solution.py:338
  11.1 0.6 copy-done.9
  11.7 13.7 %forward_backward.1 = (bf16[384,1024]{1,0:T(8,128)(2,1)}, bf16[2,400,1024]{2,1,0:T(8,128)(2,1)}, bf16[400,1024]{1,0:T(8,128)(2,1)}, bf16[400,1024]{1,0:T(8,128)(2,1)}) custom-call(s32[1]{0:T(128)S(6)} %copy.10.length_ref.info_ref, f32[1,1024]{1,0:T(1,128)} %bitcast.12, f32[9,1024]{1,0:T(8,128)} %taps_ref.1, bf16[384,1024]{1,0:T(8,128)(2,1)} %get-tuple-element.29.nh.n0h, ...), custom_call_target="tpu_custom_call" | custom-call | tf_op jit(solution)/shard_map/forward_backward/pallas_call | solution.py:462
  25.4 1.6 %collective-permute-start.3 = (bf16[400,1024]{1,0:T(8,128)(2,1)}, bf16[400,1024]{1,0:T(8,128)(2,1)S(1)}, u32[]{:S(2)}, u32[]{:S(2)}) collective-permute-start(bf16[400,1024]{1,0:T(8,128)(2,1)} %get-tuple-element.35), channel_id=1, source_target_pairs={{0,1},{1,0},{2,3},{3,2},{4,5},{5,4},{6,7},{7,6},{8,9},{9,8},{10,11... | collective-permute-start | bytes 2457608 | tf_op jit(solution)/shard_map/ppermute | solution.py:285
  27.1 0.4 collective-permute-start.4
  27.6 4.4 %collective-permute-done.5.g1h = bf16[384,512]{1,0:T(8,128)(2,1)S(1)} collective-permute-done((bf16[384,512]{1,0:T(8,128)(2,1)S(1)}, bf16[384,512]{1,0:T(8,128)(2,1)S(1)}, u32[]{:S(2)}, u32[]{:S(2)}) %collective-permute-start.5) | collective-permute-done | bytes 393248 | tf_op jit(solution)/shard_map/ppermute | solution.py:285
  32.0 0.7 copy-done.7
  33.5 9.6 %weight_grads.1 = (bf16[33,48,128]{2,1,0:T(8,128)(2,1)}, bf16[33,48,128]{2,1,0:T(8,128)(2,1)}, bf16[33,48,128]{2,1,0:T(8,128)(2,1)}, bf16[33,48,128]{2,1,0:T(8,1...) custom-call(f32[1,1024]{1,0:T(1,128)} %bitcast.13, ...), custom_call_target="tpu_custom_call" | custom-call | tf_op jit(solution)/shard_map/weight_grads/pallas_call | solution.py:116
  43.2 7.2 %collective-permute-start.12 = (bf16[32,48,128]{2,1,0:T(8,128)(2,1)}, bf16[32,48,128]{2,1,0:T(8,128)(2,1)S(1)}, u32[]{:S(2)}, u32[]{:S(2)}) collective-permute-start(bf16[32,48,128]{2,1,0:T(8,128)(2,1)} %get-tuple-element.48), channel_id=1, source_target_pairs={{0,128},{2,130},{128,0},{130,2},{1,129},{3,131},{129,1},{131,3},{4... | collective-permute-start | bytes 1179656 | tf_op jit(solution)/shard_map/ppermute | solution.py:171
  50.8 2.3 %collective-permute-start.14 = (bf16[32,48,128]{2,1,0:T(8,128)(2,1)}, bf16[32,48,128]{2,1,0:T(8,128)(2,1)S(1)}, u32[]{:S(2)}, u32[]{:S(2)}) collective-permute-start(bf16[32,48,128]{2,1,0:T(8,128)(2,1)} %get-tuple-element.50), channel_id=1, source_target_pairs={{0,130},{2,0},{128,2},{130,128},{1,131},{3,1},{129,3},{131,129},{4... | collective-permute-start | bytes 1179656 | tf_op jit(solution)/shard_map/ppermute | solution.py:171
  53.1 1.2 %collective-permute-start.7 = (bf16[33,48,128]{2,1,0:T(8,128)(2,1)}, bf16[33,48,128]{2,1,0:T(8,128)(2,1)S(1)}, u32[]{:S(2)}, u32[]{:S(2)}) collective-permute-start(bf16[33,48,128]{2,1,0:T(8,128)(2,1)} %get-tuple-element.40), channel_id=1, source_target_pairs={{0,32},{32,64},{64,96},{96,0},{1,33},{33,65},{65,97},{97,1},{2,34}... | collective-permute-start | bytes 1216520 | tf_op jit(solution)/shard_map/ppermute | solution.py:171
  54.3 5.4 %collective-permute-done.12.i1 = bf16[32,48,128]{2,1,0:T(8,128)(2,1)S(1)} collective-permute-done((bf16[32,48,128]{2,1,0:T(8,128)(2,1)}, bf16[32,48,128]{2,1,0:T(8,128)(2,1)S(1)}, u32[]{:S(2)}, u32[]{:S(2)}) %collective-permute-start.12) | collective-permute-done | bytes 393248 | tf_op jit(solution)/shard_map/ppermute | solution.py:171
  59.8 3.2 %collective-permute-start.8 = (bf16[33,48,128]{2,1,0:T(8,128)(2,1)}, bf16[33,48,128]{2,1,0:T(8,128)(2,1)S(1)}, u32[]{:S(2)}, u32[]{:S(2)}) collective-permute-start(bf16[33,48,128]{2,1,0:T(8,128)(2,1)} %get-tuple-element.41), channel_id=1, source_target_pairs={{0,96},{32,0},{64,32},{96,64},{1,97},{33,1},{65,33},{97,65},{2,98}... | collective-permute-start | bytes 1216520 | tf_op jit(solution)/shard_map/ppermute | solution.py:171
  63.0 5.6 %collective-permute-done.13.i2 = bf16[32,48,128]{2,1,0:T(8,128)(2,1)S(1)} collective-permute-done((bf16[32,48,128]{2,1,0:T(8,128)(2,1)}, bf16[32,48,128]{2,1,0:T(8,128)(2,1)S(1)}, u32[]{:S(2)}, u32[]{:S(2)}) %collective-permute-start.13) | collective-permute-done | bytes 393248 | tf_op jit(solution)/shard_map/ppermute | solution.py:171
  68.6 1.0 copy-done.1
  70.1 10.8 %outputs.1 = (bf16[384,1024]{1,0:T(8,128)(2,1)}, bf16[384,1024]{1,0:T(8,128)(2,1)}, f32[8,128]{1,0:T(8,128)}) custom-call(s32[1]{0:T(128)S(6)} %copy.10.length_ref.info_ref, f32[1,1024]{1,0:T(1,128)} %bitcast.14, bf16[384,1024]{1,0:T(8,128)(2,1)} %bitcast.8, bf16[384,1024]{1,0:T(8,128)(2,1)} %bitcast.10, bf16[384,1024]{1,0:T(8,128)(2,1)} %get-tuple-element.32.a0h.acth, ...), custom_call_target="tpu_custom_call" | custom-call | tf_op jit(solution)/shard_map/outputs/pallas_call | solution.py:526
  81.0 0.7 copy-done.2
  81.9 1.5 %collective-permute-start.9 = (bf16[9,48,128]{2,1,0:T(8,128)(2,1)S(1)}, bf16[9,48,128]{2,1,0:T(8,128)(2,1)S(1)}, u32[]{:S(2)}, u32[]{:S(2)}) collective-permute-start(bf16[9,48,128]{2,1,0:T(8,128)(2,1)S(1)} %get-tuple-element.44), channel_id=1, source_target_pairs={{0,128},{2,130},{128,0},{130,2},{1,129},{3,131},{129,1},{131,3},{4... | collective-permute-start | bytes 331784 | tf_op jit(solution)/shard_map/ppermute | solution.py:171
  83.4 1.9 %collective-permute-start.10 = (bf16[9,48,128]{2,1,0:T(8,128)(2,1)S(1)}, bf16[9,48,128]{2,1,0:T(8,128)(2,1)S(1)}, u32[]{:S(2)}, u32[]{:S(2)}) collective-permute-start(bf16[9,48,128]{2,1,0:T(8,128)(2,1)S(1)} %get-tuple-element.45), channel_id=1, source_target_pairs={{0,2},{2,128},{128,130},{130,0},{1,3},{3,129},{129,131},{131,1},{4... | collective-permute-start | bytes 331784 | tf_op jit(solution)/shard_map/ppermute | solution.py:171
  85.3 0.8 collective-permute-start.11
  86.1 2.9 %collective-permute-start.16 = (bf16[8,48,128]{2,1,0:T(8,128)(2,1)S(1)}, bf16[8,48,128]{2,1,0:T(8,128)(2,1)S(1)}, u32[]{:S(2)}, u32[]{:S(2)}) collective-permute-start(bf16[8,48,128]{2,1,0:T(8,128)(2,1)S(1)} %get-tuple-element.53), channel_id=1, source_target_pairs={{0,32},{32,64},{64,96},{96,0},{1,33},{33,65},{65,97},{97,1},{2,34}... | collective-permute-start | bytes 294920 | tf_op jit(solution)/shard_map/ppermute | solution.py:171
  89.0 1.9 %collective-permute-done.16.b2 = bf16[8,48,128]{2,1,0:T(8,128)(2,1)S(1)} collective-permute-done((bf16[8,48,128]{2,1,0:T(8,128)(2,1)S(1)}, bf16[8,48,128]{2,1,0:T(8,128)(2,1)S(1)}, u32[]{:S(2)}, u32[]{:S(2)}) %collective-permute-start.16) | collective-permute-done | bytes 98336 | tf_op jit(solution)/shard_map/ppermute | solution.py:171
  90.9 1.9 %collective-permute-done.17.b3 = bf16[8,48,128]{2,1,0:T(8,128)(2,1)S(1)} collective-permute-done((bf16[8,48,128]{2,1,0:T(8,128)(2,1)S(1)}, bf16[8,48,128]{2,1,0:T(8,128)(2,1)S(1)}, u32[]{:S(2)}, u32[]{:S(2)}) %collective-permute-start.17) | collective-permute-done | bytes 98336 | tf_op jit(solution)/shard_map/ppermute | solution.py:171
  92.9 17.7 %all_to_all.5.parts = bf16[8,144,128]{2,1,0:T(8,128)(2,1)S(1)} all-to-all(bf16[8,144,128]{2,1,0:T(8,128)(2,1)S(1)} %sum_before_z.1), channel_id=1, replica_groups=mesh['yh'=2,'x'=4,'z'=8,'yl'=2,'c'=2] {'z'}, dimensions={0} | all-to-all | bytes 589824 | tf_op jit(solution)/shard_map/all_to_all | solution.py:206
  110.6 5.0 %collective-permute-start.18 = (f32[144,128]{1,0:T(8,128)S(1)}, f32[144,128]{1,0:T(8,128)S(1)}, u32[]{:S(2)}, u32[]{:S(2)}) collective-permute-start(f32[144,128]{1,0:T(8,128)S(1)} %sum_after_z.1.own), channel_id=1, source_target_pairs={{0,1},{1,0},{2,3},{3,2},{4,5},{5,4},{6,7},{7,6},{8,9},{9,8},{10,11... | collective-permute-start | bytes 221192 | tf_op jit(solution)/shard_map/ppermute | solution.py:269
  115.7 0.9 collective-permute-done.18.other
  116.6 1.3 %collective-permute-start.19 = (f32[96,128]{1,0:T(8,128)S(1)}, f32[96,128]{1,0:T(8,128)S(1)}, u32[]{:S(2)}, u32[]{:S(2)}) collective-permute-start(f32[96,128]{1,0:T(8,128)S(1)} %pad_maximum_fusion.2), channel_id=1, source_target_pairs={{3,1},{5,3},{7,5},{9,7},{11,9},{13,11},{15,13},{17,15},{19,17},{21... | collective-permute-start | bytes 147464 | tf_op jit(solution)/shard_map/ppermute | solution.py:271
  117.9 3.5 %collective-permute-done.19.follow = f32[96,128]{1,0:T(8,128)S(1)} collective-permute-done((f32[96,128]{1,0:T(8,128)S(1)}, f32[96,128]{1,0:T(8,128)S(1)}, u32[]{:S(2)}, u32[]{:S(2)}) %collective-permute-start.19) | collective-permute-done | bytes 49184 | tf_op jit(solution)/shard_map/ppermute | solution.py:271
  121.4 1.0 own_chunk.1
  (46 shorter events, 2.5 us)
Async XLA Ops:
  1.5 9.6 %collective-permute-start = (bf16[2,16,1024]{2,1,0:T(8,128)(2,1)S(1)}, bf16[2,16,1024]{2,1,0:T(8,128)(2,1)S(1)}, u32[]{:S(2)}, u32[]{:S(2)}) collective-permute-start(bf16[2,16,1024]{2,1,0:T(8,128)(2,1)S(1)} %pad_maximum_fusion), channel_id=1, source_target_pairs={{0,32},{32,64},{64,96},{96,128},{128,160},{160,192},{192,224},{1,3... | collective-permute-start | bytes 196616 | tf_op jit(solution)/shard_map/ppermute | solution.py:550
  5.4 5.6 %collective-permute-start.1 = (bf16[2,16,1024]{2,1,0:T(8,128)(2,1)S(1)}, bf16[2,16,1024]{2,1,0:T(8,128)(2,1)S(1)}, u32[]{:S(2)}, u32[]{:S(2)}) collective-permute-start(bf16[2,16,1024]{2,1,0:T(8,128)(2,1)S(1)} %pad_maximum_fusion.1), channel_id=1, source_target_pairs={{32,0},{64,32},{96,64},{128,96},{160,128},{192,160},{224,192},{33,... | collective-permute-start | bytes 196616 | tf_op jit(solution)/shard_map/ppermute | solution.py:551
  11.0 0.6 copy-start.9
  11.1 0.6 copy-start.10
  11.7 15.3 %copy-start.3 = (bf16[384,1024]{1,0:T(8,128)(2,1)S(1)}, bf16[384,1024]{1,0:T(8,128)(2,1)}, u32[]{:S(2)}) copy-start(bf16[384,1024]{1,0:T(8,128)(2,1)} %get-tuple-element.29.nh.n0h) | copy-start | bytes 2359300
  11.7 15.8 %copy-start.8 = (bf16[384,512]{1,0:T(8,128)(2,1)S(1)}, bf16[384,512]{1,0:T(8,128)(2,1)}, u32[]{:S(2)}) copy-start(bf16[384,512]{1,0:T(8,128)(2,1)} %get-tuple-element.31.ggh) | copy-start | bytes 1179652
  25.4 6.6 %collective-permute-start.3 = (bf16[400,1024]{1,0:T(8,128)(2,1)}, bf16[400,1024]{1,0:T(8,128)(2,1)S(1)}, u32[]{:S(2)}, u32[]{:S(2)}) collective-permute-start(bf16[400,1024]{1,0:T(8,128)(2,1)} %get-tuple-element.35), channel_id=1, source_target_pairs={{0,1},{1,0},{2,3},{3,2},{4,5},{5,4},{6,7},{7,6},{8,9},{9,8},{10,11... | collective-permute-start | bytes 2457608 | tf_op jit(solution)/shard_map/ppermute | solution.py:285
  27.0 5.0 %collective-permute-start.2 = (bf16[384,1024]{1,0:T(8,128)(2,1)S(1)}, bf16[384,1024]{1,0:T(8,128)(2,1)S(1)}, u32[]{:S(2)}, u32[]{:S(2)}) collective-permute-start(bf16[384,1024]{1,0:T(8,128)(2,1)S(1)} %copy-done.3), channel_id=1, source_target_pairs={{0,1},{1,0},{2,3},{3,2},{4,5},{5,4},{6,7},{7,6},{8,9},{9,8},{10,11... | collective-permute-start | bytes 2359304 | tf_op jit(solution)/shard_map/ppermute | solution.py:285
  27.1 4.9 %collective-permute-start.4 = (bf16[384,1024]{1,0:T(8,128)(2,1)}, bf16[384,1024]{1,0:T(8,128)(2,1)S(1)}, u32[]{:S(2)}, u32[]{:S(2)}) collective-permute-start(bf16[384,1024]{1,0:T(8,128)(2,1)} %get-tuple-element.32.a0h.acth), channel_id=1, source_target_pairs={{0,1},{1,0},{2,3},{3,2},{4,5},{5,4},{6,7},{7,6},{8,9},{9,8},{10,11... | collective-permute-start | bytes 2359304 | tf_op jit(solution)/shard_map/ppermute | solution.py:285
  27.5 4.5 %collective-permute-start.5 = (bf16[384,512]{1,0:T(8,128)(2,1)S(1)}, bf16[384,512]{1,0:T(8,128)(2,1)S(1)}, u32[]{:S(2)}, u32[]{:S(2)}) collective-permute-start(bf16[384,512]{1,0:T(8,128)(2,1)S(1)} %copy-done.8), channel_id=1, source_target_pairs={{0,1},{1,0},{2,3},{3,2},{4,5},{5,4},{6,7},{7,6},{8,9},{9,8},{10,11... | collective-permute-start | bytes 1179656 | tf_op jit(solution)/shard_map/ppermute | solution.py:285
  32.0 0.7 copy-start.7
  32.0 1.0 copy-start.5
  32.0 1.3 %copy-start.6 = (bf16[384,1024]{1,0:T(8,128)(2,1)}, bf16[384,1024]{1,0:T(8,128)(2,1)S(1)}, u32[]{:S(2)}) copy-start(bf16[384,1024]{1,0:T(8,128)(2,1)S(1)} %collective-permute-done.4.a1h) | copy-start | bytes 2359300
  32.0 1.5 %copy-start.4 = (bf16[400,1024]{1,0:T(8,128)(2,1)}, bf16[400,1024]{1,0:T(8,128)(2,1)S(1)}, u32[]{:S(2)}) copy-start(bf16[400,1024]{1,0:T(8,128)(2,1)S(1)} %collective-permute-done.3.k1h) | copy-start | bytes 2457604
  43.2 16.6 %collective-permute-start.12 = (bf16[32,48,128]{2,1,0:T(8,128)(2,1)}, bf16[32,48,128]{2,1,0:T(8,128)(2,1)S(1)}, u32[]{:S(2)}, u32[]{:S(2)}) collective-permute-start(bf16[32,48,128]{2,1,0:T(8,128)(2,1)} %get-tuple-element.48), channel_id=1, source_target_pairs={{0,128},{2,130},{128,0},{130,2},{1,129},{3,131},{129,1},{131,3},{4... | collective-permute-start | bytes 1179656 | tf_op jit(solution)/shard_map/ppermute | solution.py:171
  50.4 18.2 %collective-permute-start.13 = (bf16[32,48,128]{2,1,0:T(8,128)(2,1)}, bf16[32,48,128]{2,1,0:T(8,128)(2,1)S(1)}, u32[]{:S(2)}, u32[]{:S(2)}) collective-permute-start(bf16[32,48,128]{2,1,0:T(8,128)(2,1)} %get-tuple-element.49), channel_id=1, source_target_pairs={{0,2},{2,128},{128,130},{130,0},{1,3},{3,129},{129,131},{131,1},{4... | collective-permute-start | bytes 1179656 | tf_op jit(solution)/shard_map/ppermute | solution.py:171
  50.8 17.8 %collective-permute-start.14 = (bf16[32,48,128]{2,1,0:T(8,128)(2,1)}, bf16[32,48,128]{2,1,0:T(8,128)(2,1)S(1)}, u32[]{:S(2)}, u32[]{:S(2)}) collective-permute-start(bf16[32,48,128]{2,1,0:T(8,128)(2,1)} %get-tuple-element.50), channel_id=1, source_target_pairs={{0,130},{2,0},{128,2},{130,128},{1,131},{3,1},{129,3},{131,129},{4... | collective-permute-start | bytes 1179656 | tf_op jit(solution)/shard_map/ppermute | solution.py:171
  53.1 27.8 %collective-permute-start.6 = (bf16[33,48,128]{2,1,0:T(8,128)(2,1)}, bf16[33,48,128]{2,1,0:T(8,128)(2,1)S(1)}, u32[]{:S(2)}, u32[]{:S(2)}) collective-permute-start(bf16[33,48,128]{2,1,0:T(8,128)(2,1)} %get-tuple-element.39), channel_id=1, source_target_pairs={{0,64},{32,96},{64,0},{96,32},{1,65},{33,97},{65,1},{97,33},{2,66}... | collective-permute-start | bytes 1216520 | tf_op jit(solution)/shard_map/ppermute | solution.py:171
  53.1 27.8 %collective-permute-start.7 = (bf16[33,48,128]{2,1,0:T(8,128)(2,1)}, bf16[33,48,128]{2,1,0:T(8,128)(2,1)S(1)}, u32[]{:S(2)}, u32[]{:S(2)}) collective-permute-start(bf16[33,48,128]{2,1,0:T(8,128)(2,1)} %get-tuple-element.40), channel_id=1, source_target_pairs={{0,32},{32,64},{64,96},{96,0},{1,33},{33,65},{65,97},{97,1},{2,34}... | collective-permute-start | bytes 1216520 | tf_op jit(solution)/shard_map/ppermute | solution.py:171
  59.8 21.2 %collective-permute-start.8 = (bf16[33,48,128]{2,1,0:T(8,128)(2,1)}, bf16[33,48,128]{2,1,0:T(8,128)(2,1)S(1)}, u32[]{:S(2)}, u32[]{:S(2)}) collective-permute-start(bf16[33,48,128]{2,1,0:T(8,128)(2,1)} %get-tuple-element.41), channel_id=1, source_target_pairs={{0,96},{32,0},{64,32},{96,64},{1,97},{33,1},{65,33},{97,65},{2,98}... | collective-permute-start | bytes 1216520 | tf_op jit(solution)/shard_map/ppermute | solution.py:171
  68.6 1.0 copy-start.1
  69.8 19.2 %collective-permute-start.15 = (bf16[8,48,128]{2,1,0:T(8,128)(2,1)S(1)}, bf16[8,48,128]{2,1,0:T(8,128)(2,1)S(1)}, u32[]{:S(2)}, u32[]{:S(2)}) collective-permute-start(bf16[8,48,128]{2,1,0:T(8,128)(2,1)S(1)} %get-tuple-element.52), channel_id=1, source_target_pairs={{0,64},{32,96},{64,0},{96,32},{1,65},{33,97},{65,1},{97,33},{2,66}... | collective-permute-start | bytes 294920 | tf_op jit(solution)/shard_map/ppermute | solution.py:171
  70.1 10.8 %copy-start = (bf16[33,48,128]{2,1,0:T(8,128)(2,1)S(1)}, bf16[33,48,128]{2,1,0:T(8,128)(2,1)}, u32[]{:S(2)}) copy-start(bf16[33,48,128]{2,1,0:T(8,128)(2,1)} %get-tuple-element.36.after_this.i0) | copy-start | bytes 1216516
  81.0 0.7 copy-start.2
  81.9 10.9 %collective-permute-start.9 = (bf16[9,48,128]{2,1,0:T(8,128)(2,1)S(1)}, bf16[9,48,128]{2,1,0:T(8,128)(2,1)S(1)}, u32[]{:S(2)}, u32[]{:S(2)}) collective-permute-start(bf16[9,48,128]{2,1,0:T(8,128)(2,1)S(1)} %get-tuple-element.44), channel_id=1, source_target_pairs={{0,128},{2,130},{128,0},{130,2},{1,129},{3,131},{129,1},{131,3},{4... | collective-permute-start | bytes 331784 | tf_op jit(solution)/shard_map/ppermute | solution.py:171
  83.4 9.4 %collective-permute-start.10 = (bf16[9,48,128]{2,1,0:T(8,128)(2,1)S(1)}, bf16[9,48,128]{2,1,0:T(8,128)(2,1)S(1)}, u32[]{:S(2)}, u32[]{:S(2)}) collective-permute-start(bf16[9,48,128]{2,1,0:T(8,128)(2,1)S(1)} %get-tuple-element.45), channel_id=1, source_target_pairs={{0,2},{2,128},{128,130},{130,0},{1,3},{3,129},{129,131},{131,1},{4... | collective-permute-start | bytes 331784 | tf_op jit(solution)/shard_map/ppermute | solution.py:171
  85.3 7.5 %collective-permute-start.11 = (bf16[9,48,128]{2,1,0:T(8,128)(2,1)S(1)}, bf16[9,48,128]{2,1,0:T(8,128)(2,1)S(1)}, u32[]{:S(2)}, u32[]{:S(2)}) collective-permute-start(bf16[9,48,128]{2,1,0:T(8,128)(2,1)S(1)} %get-tuple-element.46), channel_id=1, source_target_pairs={{0,130},{2,0},{128,2},{130,128},{1,131},{3,1},{129,3},{131,129},{4... | collective-permute-start | bytes 331784 | tf_op jit(solution)/shard_map/ppermute | solution.py:171
  86.1 4.8 %collective-permute-start.16 = (bf16[8,48,128]{2,1,0:T(8,128)(2,1)S(1)}, bf16[8,48,128]{2,1,0:T(8,128)(2,1)S(1)}, u32[]{:S(2)}, u32[]{:S(2)}) collective-permute-start(bf16[8,48,128]{2,1,0:T(8,128)(2,1)S(1)} %get-tuple-element.53), channel_id=1, source_target_pairs={{0,32},{32,64},{64,96},{96,0},{1,33},{33,65},{65,97},{97,1},{2,34}... | collective-permute-start | bytes 294920 | tf_op jit(solution)/shard_map/ppermute | solution.py:171
  89.0 3.8 %collective-permute-start.17 = (bf16[8,48,128]{2,1,0:T(8,128)(2,1)S(1)}, bf16[8,48,128]{2,1,0:T(8,128)(2,1)S(1)}, u32[]{:S(2)}, u32[]{:S(2)}) collective-permute-start(bf16[8,48,128]{2,1,0:T(8,128)(2,1)S(1)} %get-tuple-element.54), channel_id=1, source_target_pairs={{0,96},{32,0},{64,32},{96,64},{1,97},{33,1},{65,33},{97,65},{2,98}... | collective-permute-start | bytes 294920 | tf_op jit(solution)/shard_map/ppermute | solution.py:171
  110.6 5.9 %collective-permute-start.18 = (f32[144,128]{1,0:T(8,128)S(1)}, f32[144,128]{1,0:T(8,128)S(1)}, u32[]{:S(2)}, u32[]{:S(2)}) collective-permute-start(f32[144,128]{1,0:T(8,128)S(1)} %sum_after_z.1.own), channel_id=1, source_target_pairs={{0,1},{1,0},{2,3},{3,2},{4,5},{5,4},{6,7},{7,6},{8,9},{9,8},{10,11... | collective-permute-start | bytes 221192 | tf_op jit(solution)/shard_map/ppermute | solution.py:269
  116.6 4.8 %collective-permute-start.19 = (f32[96,128]{1,0:T(8,128)S(1)}, f32[96,128]{1,0:T(8,128)S(1)}, u32[]{:S(2)}, u32[]{:S(2)}) collective-permute-start(f32[96,128]{1,0:T(8,128)S(1)} %pad_maximum_fusion.2), channel_id=1, source_target_pairs={{3,1},{5,3},{7,5},{9,7},{11,9},{13,11},{15,13},{17,15},{19,17},{21... | collective-permute-start | bytes 147464 | tf_op jit(solution)/shard_map/ppermute | solution.py:271

commit v3 on v2

--- a/solution.py
+++ b/solution.py
@@ -58,13 +58,11 @@
             )
         )
     ]
-    for load in loads[:4]:
+    for load in loads:
         load.start()
     contract = (((0,), (0,)), ((), ()))
     for load in loads[:4]:
         load.wait()
-    for load in loads[4:]:
-        load.start()
     for m in range(4):
         cols = slice(256 * m, 256 * m + 256)
         done = lax.dot_general(a0[:, cols], g0[...], contract, preferred_element_type=F32)
@@ -368,7 +366,7 @@
         pairs.append((wh.at[:, pl.ds(1024 + 256 * n, 256)], w.at[:, pl.ds(1024 + 256 * n, 256)]))
         pairs.append((pwh.at[pl.ds(256 * n, 256)], pw.at[pl.ds(256 * n, 256)]))
     loads = [pltpu.make_async_copy(src, dst, sem.at[i]) for i, (src, dst) in enumerate(pairs)]
-    for load in loads[:10]:
+    for load in loads:
         load.start()
     mask[...] = inside(info_ref, -EDGE, (LONG, 128)).astype(F32)
     krows[...] = jnp.zeros((2, 16, 1024), F32)
@@ -380,8 +378,6 @@
         gs[rows, :] = jnp.where(inside(info_ref, first - EDGE, (EDGE, 1024)), gs[rows, :].astype(F32), 0.0).astype(BF)
     for load in loads[4:7]:
         load.wait()
-    for load in loads[10:]:
-        load.start()
 
     def multiply(n, lifts):
         for load in loads[7 + 3 * n : 10 + 3 * n]:
@@ -435,23 +431,30 @@
             krows[k % 2, k // 2 : k // 2 + 1, at : at + 128] = jnp.sum(sums[k], axis=0, keepdims=True)
 
     lifts = (lifts0, lifts1)
+    sends = []
     multiply(0, lifts0)
     for n in range(4):
         if n < 3:
             multiply(n + 1, lifts[(n + 1) % 2])
         for h in range(2):
             channels(n, h, lifts[n % 2])
+        own, lanes = pl.ds(0, ROWS), pl.ds(256 * n, 256)
+        for i, (src, dst) in enumerate(
+            (
+                (both.at[1 - core, own, lanes], give_o.at[own, lanes]),
+                (act.at[:, lanes], act_o.at[:, lanes]),
+                (both.at[core, own, lanes], keep_o.at[own, lanes]),
+                (both.at[:, own, lanes], both_o.at[:, :, lanes]),
+            )
+        ):
+            sends.append(pltpu.make_async_copy(src, dst, sem_out.at[n, i]))
+            sends[-1].start()
+    tail = pl.ds(ROWS, 16)
     for c in range(2):
         both[c, ROWS:, :] = krows[c].astype(BF)
-    sends = [
-        (both.at[1 - core], give_o),
-        (act, act_o),
-        (both.at[core], keep_o),
-        (both, both_o),
-    ]
-    sends = [pltpu.make_async_copy(src, dst, sem_out.at[i]) for i, (src, dst) in enumerate(sends)]
-    for copy in sends:
-        copy.start()
+    for i, (c, dst) in enumerate(((1 - core, give_o), (core, keep_o))):
+        sends.append(pltpu.make_async_copy(both.at[c, tail], dst.at[tail], sem_out.at[4, i]))
+        sends[-1].start()
     for copy in sends:
         copy.wait()
 
@@ -461,7 +464,7 @@
     tall = jax.ShapeDtypeStruct((ROWS + 16, 1024), BF)
     return pl.pallas_call(
         main_kernel,
-        out_shape=[wide, jax.ShapeDtypeStruct((2, ROWS + 16, 1024), BF), tall, tall],
+        out_shape=[wide, jax.ShapeDtypeStruct((2, ROWS, 1024), BF), tall, tall],
         in_specs=[smem_spec(), vmem_spec(), vmem_spec()] + [hbm_spec()] * 7,
         out_specs=[hbm_spec()] * 4,
         scratch_shapes=[
@@ -479,7 +482,7 @@
             pltpu.VMEM((LONG, 128), F32),
             pltpu.VMEM((2, 16, 1024), F32),
             pltpu.SemaphoreType.DMA((19,)),
-            pltpu.SemaphoreType.DMA((4,)),
+            pltpu.SemaphoreType.DMA((5, 4)),
         ],
         name="forward_backward",
     )(lengths, gain, taps, normed, gb_keep, gb_give, before, after, w, pw)
@@ -532,7 +535,7 @@
             pltpu.VMEM((ROWS, 1024), BF),
             pltpu.VMEM((ROWS, 1024), BF),
             pltpu.VMEM((ROWS, 1024), BF),
-            pltpu.VMEM((2, ROWS + 16, 1024), BF),
+            pltpu.VMEM((2, ROWS, 1024), BF),
             pltpu.VMEM((1024, 2048), BF),
             pltpu.VMEM((1024, 1024), BF),
             pltpu.SemaphoreType.DMA((6,)),

time: 123 us -> 121 us (0.984)
  Pallas kernels: 39.3 us -> 37 us
    pallas_call x1, Pallas kernels: 13.7 us -> 12.4 us  [forward_backward(): pl.pallas_call(main_kernel, out_shape=[wide, jax.ShapeDtypeStruct((2, ROW...]
where the time goes in v3:
time: 121 us; the launch traced here: 120 us
  Pallas kernels  37 us (31%)
  starting transfers between devices  35.6 us (29%)
  waiting for transfers between devices  23.6 us (20%)
  blocking collectives  17.7 us (15%)
  local copies, waits for them, and re-layouts  4.66 us (4%)
  between operations  1.5 us (1%)
    ppermute x12, starting transfers between devices, send(): lax.ppermute(blocks[step], axes, [(i, (i + step) % n) for i in range(n)])  21.9 us
    all_to_all x1, blocking collectives, reduce_terms(): return lax.all_to_all(ready, 'z', split_axis=0, concat_axis=0, tiled=True)  17.7 us
    ppermute x12, waiting for transfers between devices, send(): lax.ppermute(blocks[step], axes, [(i, (i + step) % n) for i in range(n)])  14.8 us
    pallas_call x1, Pallas kernels, forward_backward(): pl.pallas_call(main_kernel, out_shape=[wide, jax.ShapeDtypeStruct((2, ROW...  12.4 us
    pallas_call x1, Pallas kernels, outputs(): pl.pallas_call(outputs_kernel, out_shape=[wide, wide, jax.ShapeDtypeStruc...  10.7 us
    pallas_call x1, Pallas kernels, weight_blocks(): pl.pallas_call(weight_kernel, out_shape=blocks, in_specs=[vmem_spec()] +...  8.74 us
    ppermute x1, starting transfers between devices, own_chunk(): other = lax.ppermute(total, 'c', [(0, 1), (1, 0)])  5 us
    ppermute x4, waiting for transfers between devices, pair_swap(): return lax.ppermute(array, 'c', [(0, 1), (1, 0)])  4.36 us
  transfers between devices with their start and end apart: 20, of which 7 were waited for; matrix products, arithmetic and copies ran while one was open for 0% of the time, Pallas kernels for 12%

profile of v3, /device:TPU:1, one launch (start us, length us, event | category | flops | bytes accessed | tf_op | source)
XLA Modules:
  0.0 120.1 jit_solution(18072910384905838781)
XLA Ops:
  0.6 0.8 fusion
  1.5 3.9 %collective-permute-start = (bf16[2,16,1024]{2,1,0:T(8,128)(2,1)S(1)}, bf16[2,16,1024]{2,1,0:T(8,128)(2,1)S(1)}, u32[]{:S(2)}, u32[]{:S(2)}) collective-permute-start(bf16[2,16,1024]{2,1,0:T(8,128)(2,1)S(1)} %pad_maximum_fusion), channel_id=1, source_target_pairs={{0,32},{32,64},{64,96},{96,128},{128,160},{160,192},{192,224},{1,3... | collective-permute-start | bytes 196616 | tf_op jit(solution)/shard_map/ppermute | solution.py:553
  5.4 1.3 %collective-permute-start.1 = (bf16[2,16,1024]{2,1,0:T(8,128)(2,1)S(1)}, bf16[2,16,1024]{2,1,0:T(8,128)(2,1)S(1)}, u32[]{:S(2)}, u32[]{:S(2)}) collective-permute-start(bf16[2,16,1024]{2,1,0:T(8,128)(2,1)S(1)} %pad_maximum_fusion.1), channel_id=1, source_target_pairs={{32,0},{64,32},{96,64},{128,96},{160,128},{192,160},{224,192},{33,... | collective-permute-start | bytes 196616 | tf_op jit(solution)/shard_map/ppermute | solution.py:554
  7.4 3.6 %early.1 = (bf16[384,1024]{1,0:T(8,128)(2,1)}, bf16[384,512]{1,0:T(8,128)(2,1)}, bf16[384,512]{1,0:T(8,128)(2,1)}) custom-call(s32[1]{0:T(128)S(6)} %copy.10.length_ref.info_ref, f32[1,1024]{1,0:T(1,128)} %bitcast.11, bf16[384,1024]{1,0:T(8,128)(2,1)} %bitcast.7, bf16[384,1024]{1,0:T(8,128)(2,1)} %bitcast.9), custom_call_target="tpu_custom_call" | custom-call | tf_op jit(solution)/shard_map/early/pallas_call | solution.py:336
  11.1 0.6 copy-done.9
  11.7 12.4 %forward_backward.1 = (bf16[384,1024]{1,0:T(8,128)(2,1)}, bf16[2,384,1024]{2,1,0:T(8,128)(2,1)}, bf16[400,1024]{1,0:T(8,128)(2,1)}, bf16[400,1024]{1,0:T(8,128)(2,1)}) custom-call(s32[1]{0:T(128)S(6)} %copy.10.length_ref.info_ref, f32[1,1024]{1,0:T(1,128)} %bitcast.12, f32[9,1024]{1,0:T(8,128)} %taps_ref.1, bf16[384,1024]{1,0:T(8,128)(2,1)} %get-tuple-element.29.nh.n0h, ...), custom_call_target="tpu_custom_call" | custom-call | tf_op jit(solution)/shard_map/forward_backward/pallas_call | solution.py:465
  24.1 1.6 %collective-permute-start.3 = (bf16[400,1024]{1,0:T(8,128)(2,1)}, bf16[400,1024]{1,0:T(8,128)(2,1)S(1)}, u32[]{:S(2)}, u32[]{:S(2)}) collective-permute-start(bf16[400,1024]{1,0:T(8,128)(2,1)} %get-tuple-element.35), channel_id=1, source_target_pairs={{0,1},{1,0},{2,3},{3,2},{4,5},{5,4},{6,7},{7,6},{8,9},{9,8},{10,11... | collective-permute-start | bytes 2457608 | tf_op jit(solution)/shard_map/ppermute | solution.py:283
  25.7 0.4 collective-permute-start.4
  26.3 4.4 %collective-permute-done.5.g1h = bf16[384,512]{1,0:T(8,128)(2,1)S(1)} collective-permute-done((bf16[384,512]{1,0:T(8,128)(2,1)S(1)}, bf16[384,512]{1,0:T(8,128)(2,1)S(1)}, u32[]{:S(2)}, u32[]{:S(2)}) %collective-permute-start.5) | collective-permute-done | bytes 393248 | tf_op jit(solution)/shard_map/ppermute | solution.py:283
  30.7 0.7 copy-done.7
  32.2 8.7 %weight_grads.1 = (bf16[33,48,128]{2,1,0:T(8,128)(2,1)}, bf16[33,48,128]{2,1,0:T(8,128)(2,1)}, bf16[33,48,128]{2,1,0:T(8,128)(2,1)}, bf16[33,48,128]{2,1,0:T(8,1...) custom-call(f32[1,1024]{1,0:T(1,128)} %bitcast.13, ...), custom_call_target="tpu_custom_call" | custom-call | tf_op jit(solution)/shard_map/weight_grads/pallas_call | solution.py:114
  40.9 7.2 %collective-permute-start.12 = (bf16[32,48,128]{2,1,0:T(8,128)(2,1)}, bf16[32,48,128]{2,1,0:T(8,128)(2,1)S(1)}, u32[]{:S(2)}, u32[]{:S(2)}) collective-permute-start(bf16[32,48,128]{2,1,0:T(8,128)(2,1)} %get-tuple-element.48), channel_id=1, source_target_pairs={{0,128},{2,130},{128,0},{130,2},{1,129},{3,131},{129,1},{131,3},{4... | collective-permute-start | bytes 1179656 | tf_op jit(solution)/shard_map/ppermute | solution.py:169
  48.6 2.3 %collective-permute-start.14 = (bf16[32,48,128]{2,1,0:T(8,128)(2,1)}, bf16[32,48,128]{2,1,0:T(8,128)(2,1)S(1)}, u32[]{:S(2)}, u32[]{:S(2)}) collective-permute-start(bf16[32,48,128]{2,1,0:T(8,128)(2,1)} %get-tuple-element.50), channel_id=1, source_target_pairs={{0,130},{2,0},{128,2},{130,128},{1,131},{3,1},{129,3},{131,129},{4... | collective-permute-start | bytes 1179656 | tf_op jit(solution)/shard_map/ppermute | solution.py:169
  50.8 1.3 %collective-permute-start.7 = (bf16[33,48,128]{2,1,0:T(8,128)(2,1)}, bf16[33,48,128]{2,1,0:T(8,128)(2,1)S(1)}, u32[]{:S(2)}, u32[]{:S(2)}) collective-permute-start(bf16[33,48,128]{2,1,0:T(8,128)(2,1)} %get-tuple-element.40), channel_id=1, source_target_pairs={{0,32},{32,64},{64,96},{96,0},{1,33},{33,65},{65,97},{97,1},{2,34}... | collective-permute-start | bytes 1216520 | tf_op jit(solution)/shard_map/ppermute | solution.py:169
  52.1 5.4 %collective-permute-done.12.i1 = bf16[32,48,128]{2,1,0:T(8,128)(2,1)S(1)} collective-permute-done((bf16[32,48,128]{2,1,0:T(8,128)(2,1)}, bf16[32,48,128]{2,1,0:T(8,128)(2,1)S(1)}, u32[]{:S(2)}, u32[]{:S(2)}) %collective-permute-start.12) | collective-permute-done | bytes 393248 | tf_op jit(solution)/shard_map/ppermute | solution.py:169
  57.5 3.2 %collective-permute-start.8 = (bf16[33,48,128]{2,1,0:T(8,128)(2,1)}, bf16[33,48,128]{2,1,0:T(8,128)(2,1)S(1)}, u32[]{:S(2)}, u32[]{:S(2)}) collective-permute-start(bf16[33,48,128]{2,1,0:T(8,128)(2,1)} %get-tuple-element.41), channel_id=1, source_target_pairs={{0,96},{32,0},{64,32},{96,64},{1,97},{33,1},{65,33},{97,65},{2,98}... | collective-permute-start | bytes 1216520 | tf_op jit(solution)/shard_map/ppermute | solution.py:169
  60.8 5.6 %collective-permute-done.13.i2 = bf16[32,48,128]{2,1,0:T(8,128)(2,1)S(1)} collective-permute-done((bf16[32,48,128]{2,1,0:T(8,128)(2,1)}, bf16[32,48,128]{2,1,0:T(8,128)(2,1)S(1)}, u32[]{:S(2)}, u32[]{:S(2)}) %collective-permute-start.13) | collective-permute-done | bytes 393248 | tf_op jit(solution)/shard_map/ppermute | solution.py:169
  66.4 1.0 copy-done.1
  67.9 10.7 %outputs.1 = (bf16[384,1024]{1,0:T(8,128)(2,1)}, bf16[384,1024]{1,0:T(8,128)(2,1)}, f32[8,128]{1,0:T(8,128)}) custom-call(s32[1]{0:T(128)S(6)} %copy.10.length_ref.info_ref, f32[1,1024]{1,0:T(1,128)} %bitcast.14, bf16[384,1024]{1,0:T(8,128)(2,1)} %bitcast.8, bf16[384,1024]{1,0:T(8,128)(2,1)} %bitcast.10, bf16[384,1024]{1,0:T(8,128)(2,1)} %get-tuple-element.32.a0h.acth, ...), custom_call_target="tpu_custom_call" | custom-call | tf_op jit(solution)/shard_map/outputs/pallas_call | solution.py:529
  78.7 0.7 copy-done.2
  79.6 1.5 %collective-permute-start.9 = (bf16[9,48,128]{2,1,0:T(8,128)(2,1)S(1)}, bf16[9,48,128]{2,1,0:T(8,128)(2,1)S(1)}, u32[]{:S(2)}, u32[]{:S(2)}) collective-permute-start(bf16[9,48,128]{2,1,0:T(8,128)(2,1)S(1)} %get-tuple-element.44), channel_id=1, source_target_pairs={{0,128},{2,130},{128,0},{130,2},{1,129},{3,131},{129,1},{131,3},{4... | collective-permute-start | bytes 331784 | tf_op jit(solution)/shard_map/ppermute | solution.py:169
  81.2 1.9 %collective-permute-start.10 = (bf16[9,48,128]{2,1,0:T(8,128)(2,1)S(1)}, bf16[9,48,128]{2,1,0:T(8,128)(2,1)S(1)}, u32[]{:S(2)}, u32[]{:S(2)}) collective-permute-start(bf16[9,48,128]{2,1,0:T(8,128)(2,1)S(1)} %get-tuple-element.45), channel_id=1, source_target_pairs={{0,2},{2,128},{128,130},{130,0},{1,3},{3,129},{129,131},{131,1},{4... | collective-permute-start | bytes 331784 | tf_op jit(solution)/shard_map/ppermute | solution.py:169
  83.1 0.8 collective-permute-start.11
  83.9 2.9 %collective-permute-start.16 = (bf16[8,48,128]{2,1,0:T(8,128)(2,1)S(1)}, bf16[8,48,128]{2,1,0:T(8,128)(2,1)S(1)}, u32[]{:S(2)}, u32[]{:S(2)}) collective-permute-start(bf16[8,48,128]{2,1,0:T(8,128)(2,1)S(1)} %get-tuple-element.53), channel_id=1, source_target_pairs={{0,32},{32,64},{64,96},{96,0},{1,33},{33,65},{65,97},{97,1},{2,34}... | collective-permute-start | bytes 294920 | tf_op jit(solution)/shard_map/ppermute | solution.py:169
  86.8 1.9 %collective-permute-done.16.b2 = bf16[8,48,128]{2,1,0:T(8,128)(2,1)S(1)} collective-permute-done((bf16[8,48,128]{2,1,0:T(8,128)(2,1)S(1)}, bf16[8,48,128]{2,1,0:T(8,128)(2,1)S(1)}, u32[]{:S(2)}, u32[]{:S(2)}) %collective-permute-start.16) | collective-permute-done | bytes 98336 | tf_op jit(solution)/shard_map/ppermute | solution.py:169
  88.7 1.9 %collective-permute-done.17.b3 = bf16[8,48,128]{2,1,0:T(8,128)(2,1)S(1)} collective-permute-done((bf16[8,48,128]{2,1,0:T(8,128)(2,1)S(1)}, bf16[8,48,128]{2,1,0:T(8,128)(2,1)S(1)}, u32[]{:S(2)}, u32[]{:S(2)}) %collective-permute-start.17) | collective-permute-done | bytes 98336 | tf_op jit(solution)/shard_map/ppermute | solution.py:169
  90.7 17.7 %all_to_all.5.parts = bf16[8,144,128]{2,1,0:T(8,128)(2,1)S(1)} all-to-all(bf16[8,144,128]{2,1,0:T(8,128)(2,1)S(1)} %sum_before_z.1), channel_id=1, replica_groups=mesh['yh'=2,'x'=4,'z'=8,'yl'=2,'c'=2] {'z'}, dimensions={0} | all-to-all | bytes 589824 | tf_op jit(solution)/shard_map/all_to_all | solution.py:204
  108.4 5.0 %collective-permute-start.18 = (f32[144,128]{1,0:T(8,128)S(1)}, f32[144,128]{1,0:T(8,128)S(1)}, u32[]{:S(2)}, u32[]{:S(2)}) collective-permute-start(f32[144,128]{1,0:T(8,128)S(1)} %sum_after_z.1.own), channel_id=1, source_target_pairs={{0,1},{1,0},{2,3},{3,2},{4,5},{5,4},{6,7},{7,6},{8,9},{9,8},{10,11... | collective-permute-start | bytes 221192 | tf_op jit(solution)/shard_map/ppermute | solution.py:267
  113.4 0.9 collective-permute-done.18.other
  114.3 1.3 %collective-permute-start.19 = (f32[96,128]{1,0:T(8,128)S(1)}, f32[96,128]{1,0:T(8,128)S(1)}, u32[]{:S(2)}, u32[]{:S(2)}) collective-permute-start(f32[96,128]{1,0:T(8,128)S(1)} %pad_maximum_fusion.2), channel_id=1, source_target_pairs={{3,1},{5,3},{7,5},{9,7},{11,9},{13,11},{15,13},{17,15},{19,17},{21... | collective-permute-start | bytes 147464 | tf_op jit(solution)/shard_map/ppermute | solution.py:269
  115.6 3.5 %collective-permute-done.19.follow = f32[96,128]{1,0:T(8,128)S(1)} collective-permute-done((f32[96,128]{1,0:T(8,128)S(1)}, f32[96,128]{1,0:T(8,128)S(1)}, u32[]{:S(2)}, u32[]{:S(2)}) %collective-permute-start.19) | collective-permute-done | bytes 49184 | tf_op jit(solution)/shard_map/ppermute | solution.py:269
  119.1 1.0 own_chunk.1
  (46 shorter events, 2.5 us)
Async XLA Ops:
  1.5 9.6 %collective-permute-start = (bf16[2,16,1024]{2,1,0:T(8,128)(2,1)S(1)}, bf16[2,16,1024]{2,1,0:T(8,128)(2,1)S(1)}, u32[]{:S(2)}, u32[]{:S(2)}) collective-permute-start(bf16[2,16,1024]{2,1,0:T(8,128)(2,1)S(1)} %pad_maximum_fusion), channel_id=1, source_target_pairs={{0,32},{32,64},{64,96},{96,128},{128,160},{160,192},{192,224},{1,3... | collective-permute-start | bytes 196616 | tf_op jit(solution)/shard_map/ppermute | solution.py:553
  5.4 5.6 %collective-permute-start.1 = (bf16[2,16,1024]{2,1,0:T(8,128)(2,1)S(1)}, bf16[2,16,1024]{2,1,0:T(8,128)(2,1)S(1)}, u32[]{:S(2)}, u32[]{:S(2)}) collective-permute-start(bf16[2,16,1024]{2,1,0:T(8,128)(2,1)S(1)} %pad_maximum_fusion.1), channel_id=1, source_target_pairs={{32,0},{64,32},{96,64},{128,96},{160,128},{192,160},{224,192},{33,... | collective-permute-start | bytes 196616 | tf_op jit(solution)/shard_map/ppermute | solution.py:554
  11.0 0.6 copy-start.9
  11.1 0.6 copy-start.10
  11.7 14.0 %copy-start.3 = (bf16[384,1024]{1,0:T(8,128)(2,1)S(1)}, bf16[384,1024]{1,0:T(8,128)(2,1)}, u32[]{:S(2)}) copy-start(bf16[384,1024]{1,0:T(8,128)(2,1)} %get-tuple-element.29.nh.n0h) | copy-start | bytes 2359300
  11.7 14.5 %copy-start.8 = (bf16[384,512]{1,0:T(8,128)(2,1)S(1)}, bf16[384,512]{1,0:T(8,128)(2,1)}, u32[]{:S(2)}) copy-start(bf16[384,512]{1,0:T(8,128)(2,1)} %get-tuple-element.31.ggh) | copy-start | bytes 1179652
  24.1 6.6 %collective-permute-start.3 = (bf16[400,1024]{1,0:T(8,128)(2,1)}, bf16[400,1024]{1,0:T(8,128)(2,1)S(1)}, u32[]{:S(2)}, u32[]{:S(2)}) collective-permute-start(bf16[400,1024]{1,0:T(8,128)(2,1)} %get-tuple-element.35), channel_id=1, source_target_pairs={{0,1},{1,0},{2,3},{3,2},{4,5},{5,4},{6,7},{7,6},{8,9},{9,8},{10,11... | collective-permute-start | bytes 2457608 | tf_op jit(solution)/shard_map/ppermute | solution.py:283
  25.6 5.0 %collective-permute-start.2 = (bf16[384,1024]{1,0:T(8,128)(2,1)S(1)}, bf16[384,1024]{1,0:T(8,128)(2,1)S(1)}, u32[]{:S(2)}, u32[]{:S(2)}) collective-permute-start(bf16[384,1024]{1,0:T(8,128)(2,1)S(1)} %copy-done.3), channel_id=1, source_target_pairs={{0,1},{1,0},{2,3},{3,2},{4,5},{5,4},{6,7},{7,6},{8,9},{9,8},{10,11... | collective-permute-start | bytes 2359304 | tf_op jit(solution)/shard_map/ppermute | solution.py:283
  25.7 4.9 %collective-permute-start.4 = (bf16[384,1024]{1,0:T(8,128)(2,1)}, bf16[384,1024]{1,0:T(8,128)(2,1)S(1)}, u32[]{:S(2)}, u32[]{:S(2)}) collective-permute-start(bf16[384,1024]{1,0:T(8,128)(2,1)} %get-tuple-element.32.a0h.acth), channel_id=1, source_target_pairs={{0,1},{1,0},{2,3},{3,2},{4,5},{5,4},{6,7},{7,6},{8,9},{9,8},{10,11... | collective-permute-start | bytes 2359304 | tf_op jit(solution)/shard_map/ppermute | solution.py:283
  26.2 4.5 %collective-permute-start.5 = (bf16[384,512]{1,0:T(8,128)(2,1)S(1)}, bf16[384,512]{1,0:T(8,128)(2,1)S(1)}, u32[]{:S(2)}, u32[]{:S(2)}) collective-permute-start(bf16[384,512]{1,0:T(8,128)(2,1)S(1)} %copy-done.8), channel_id=1, source_target_pairs={{0,1},{1,0},{2,3},{3,2},{4,5},{5,4},{6,7},{7,6},{8,9},{9,8},{10,11... | collective-permute-start | bytes 1179656 | tf_op jit(solution)/shard_map/ppermute | solution.py:283
  30.6 0.7 copy-start.7
  30.6 1.0 copy-start.5
  30.6 1.3 %copy-start.6 = (bf16[384,1024]{1,0:T(8,128)(2,1)}, bf16[384,1024]{1,0:T(8,128)(2,1)S(1)}, u32[]{:S(2)}) copy-start(bf16[384,1024]{1,0:T(8,128)(2,1)S(1)} %collective-permute-done.4.a1h) | copy-start | bytes 2359300
  30.7 1.5 %copy-start.4 = (bf16[400,1024]{1,0:T(8,128)(2,1)}, bf16[400,1024]{1,0:T(8,128)(2,1)S(1)}, u32[]{:S(2)}) copy-start(bf16[400,1024]{1,0:T(8,128)(2,1)S(1)} %collective-permute-done.3.k1h) | copy-start | bytes 2457604
  40.9 16.6 %collective-permute-start.12 = (bf16[32,48,128]{2,1,0:T(8,128)(2,1)}, bf16[32,48,128]{2,1,0:T(8,128)(2,1)S(1)}, u32[]{:S(2)}, u32[]{:S(2)}) collective-permute-start(bf16[32,48,128]{2,1,0:T(8,128)(2,1)} %get-tuple-element.48), channel_id=1, source_target_pairs={{0,128},{2,130},{128,0},{130,2},{1,129},{3,131},{129,1},{131,3},{4... | collective-permute-start | bytes 1179656 | tf_op jit(solution)/shard_map/ppermute | solution.py:169
  48.2 18.2 %collective-permute-start.13 = (bf16[32,48,128]{2,1,0:T(8,128)(2,1)}, bf16[32,48,128]{2,1,0:T(8,128)(2,1)S(1)}, u32[]{:S(2)}, u32[]{:S(2)}) collective-permute-start(bf16[32,48,128]{2,1,0:T(8,128)(2,1)} %get-tuple-element.49), channel_id=1, source_target_pairs={{0,2},{2,128},{128,130},{130,0},{1,3},{3,129},{129,131},{131,1},{4... | collective-permute-start | bytes 1179656 | tf_op jit(solution)/shard_map/ppermute | solution.py:169
  48.6 17.8 %collective-permute-start.14 = (bf16[32,48,128]{2,1,0:T(8,128)(2,1)}, bf16[32,48,128]{2,1,0:T(8,128)(2,1)S(1)}, u32[]{:S(2)}, u32[]{:S(2)}) collective-permute-start(bf16[32,48,128]{2,1,0:T(8,128)(2,1)} %get-tuple-element.50), channel_id=1, source_target_pairs={{0,130},{2,0},{128,2},{130,128},{1,131},{3,1},{129,3},{131,129},{4... | collective-permute-start | bytes 1179656 | tf_op jit(solution)/shard_map/ppermute | solution.py:169
  50.8 27.8 %collective-permute-start.6 = (bf16[33,48,128]{2,1,0:T(8,128)(2,1)}, bf16[33,48,128]{2,1,0:T(8,128)(2,1)S(1)}, u32[]{:S(2)}, u32[]{:S(2)}) collective-permute-start(bf16[33,48,128]{2,1,0:T(8,128)(2,1)} %get-tuple-element.39), channel_id=1, source_target_pairs={{0,64},{32,96},{64,0},{96,32},{1,65},{33,97},{65,1},{97,33},{2,66}... | collective-permute-start | bytes 1216520 | tf_op jit(solution)/shard_map/ppermute | solution.py:169
  50.8 27.8 %collective-permute-start.7 = (bf16[33,48,128]{2,1,0:T(8,128)(2,1)}, bf16[33,48,128]{2,1,0:T(8,128)(2,1)S(1)}, u32[]{:S(2)}, u32[]{:S(2)}) collective-permute-start(bf16[33,48,128]{2,1,0:T(8,128)(2,1)} %get-tuple-element.40), channel_id=1, source_target_pairs={{0,32},{32,64},{64,96},{96,0},{1,33},{33,65},{65,97},{97,1},{2,34}... | collective-permute-start | bytes 1216520 | tf_op jit(solution)/shard_map/ppermute | solution.py:169
  57.5 21.1 %collective-permute-start.8 = (bf16[33,48,128]{2,1,0:T(8,128)(2,1)}, bf16[33,48,128]{2,1,0:T(8,128)(2,1)S(1)}, u32[]{:S(2)}, u32[]{:S(2)}) collective-permute-start(bf16[33,48,128]{2,1,0:T(8,128)(2,1)} %get-tuple-element.41), channel_id=1, source_target_pairs={{0,96},{32,0},{64,32},{96,64},{1,97},{33,1},{65,33},{97,65},{2,98}... | collective-permute-start | bytes 1216520 | tf_op jit(solution)/shard_map/ppermute | solution.py:169
  66.4 1.0 copy-start.1
  67.6 19.2 %collective-permute-start.15 = (bf16[8,48,128]{2,1,0:T(8,128)(2,1)S(1)}, bf16[8,48,128]{2,1,0:T(8,128)(2,1)S(1)}, u32[]{:S(2)}, u32[]{:S(2)}) collective-permute-start(bf16[8,48,128]{2,1,0:T(8,128)(2,1)S(1)} %get-tuple-element.52), channel_id=1, source_target_pairs={{0,64},{32,96},{64,0},{96,32},{1,65},{33,97},{65,1},{97,33},{2,66}... | collective-permute-start | bytes 294920 | tf_op jit(solution)/shard_map/ppermute | solution.py:169
  67.9 10.8 %copy-start = (bf16[33,48,128]{2,1,0:T(8,128)(2,1)S(1)}, bf16[33,48,128]{2,1,0:T(8,128)(2,1)}, u32[]{:S(2)}) copy-start(bf16[33,48,128]{2,1,0:T(8,128)(2,1)} %get-tuple-element.36.after_this.i0) | copy-start | bytes 1216516
  78.7 0.7 copy-start.2
  79.6 10.9 %collective-permute-start.9 = (bf16[9,48,128]{2,1,0:T(8,128)(2,1)S(1)}, bf16[9,48,128]{2,1,0:T(8,128)(2,1)S(1)}, u32[]{:S(2)}, u32[]{:S(2)}) collective-permute-start(bf16[9,48,128]{2,1,0:T(8,128)(2,1)S(1)} %get-tuple-element.44), channel_id=1, source_target_pairs={{0,128},{2,130},{128,0},{130,2},{1,129},{3,131},{129,1},{131,3},{4... | collective-permute-start | bytes 331784 | tf_op jit(solution)/shard_map/ppermute | solution.py:169
  81.2 9.4 %collective-permute-start.10 = (bf16[9,48,128]{2,1,0:T(8,128)(2,1)S(1)}, bf16[9,48,128]{2,1,0:T(8,128)(2,1)S(1)}, u32[]{:S(2)}, u32[]{:S(2)}) collective-permute-start(bf16[9,48,128]{2,1,0:T(8,128)(2,1)S(1)} %get-tuple-element.45), channel_id=1, source_target_pairs={{0,2},{2,128},{128,130},{130,0},{1,3},{3,129},{129,131},{131,1},{4... | collective-permute-start | bytes 331784 | tf_op jit(solution)/shard_map/ppermute | solution.py:169
  83.1 7.5 %collective-permute-start.11 = (bf16[9,48,128]{2,1,0:T(8,128)(2,1)S(1)}, bf16[9,48,128]{2,1,0:T(8,128)(2,1)S(1)}, u32[]{:S(2)}, u32[]{:S(2)}) collective-permute-start(bf16[9,48,128]{2,1,0:T(8,128)(2,1)S(1)} %get-tuple-element.46), channel_id=1, source_target_pairs={{0,130},{2,0},{128,2},{130,128},{1,131},{3,1},{129,3},{131,129},{4... | collective-permute-start | bytes 331784 | tf_op jit(solution)/shard_map/ppermute | solution.py:169
  83.9 4.8 %collective-permute-start.16 = (bf16[8,48,128]{2,1,0:T(8,128)(2,1)S(1)}, bf16[8,48,128]{2,1,0:T(8,128)(2,1)S(1)}, u32[]{:S(2)}, u32[]{:S(2)}) collective-permute-start(bf16[8,48,128]{2,1,0:T(8,128)(2,1)S(1)} %get-tuple-element.53), channel_id=1, source_target_pairs={{0,32},{32,64},{64,96},{96,0},{1,33},{33,65},{65,97},{97,1},{2,34}... | collective-permute-start | bytes 294920 | tf_op jit(solution)/shard_map/ppermute | solution.py:169
  86.8 3.8 %collective-permute-start.17 = (bf16[8,48,128]{2,1,0:T(8,128)(2,1)S(1)}, bf16[8,48,128]{2,1,0:T(8,128)(2,1)S(1)}, u32[]{:S(2)}, u32[]{:S(2)}) collective-permute-start(bf16[8,48,128]{2,1,0:T(8,128)(2,1)S(1)} %get-tuple-element.54), channel_id=1, source_target_pairs={{0,96},{32,0},{64,32},{96,64},{1,97},{33,1},{65,33},{97,65},{2,98}... | collective-permute-start | bytes 294920 | tf_op jit(solution)/shard_map/ppermute | solution.py:169
  108.4 5.9 %collective-permute-start.18 = (f32[144,128]{1,0:T(8,128)S(1)}, f32[144,128]{1,0:T(8,128)S(1)}, u32[]{:S(2)}, u32[]{:S(2)}) collective-permute-start(f32[144,128]{1,0:T(8,128)S(1)} %sum_after_z.1.own), channel_id=1, source_target_pairs={{0,1},{1,0},{2,3},{3,2},{4,5},{5,4},{6,7},{7,6},{8,9},{9,8},{10,11... | collective-permute-start | bytes 221192 | tf_op jit(solution)/shard_map/ppermute | solution.py:267
  114.3 4.8 %collective-permute-start.19 = (f32[96,128]{1,0:T(8,128)S(1)}, f32[96,128]{1,0:T(8,128)S(1)}, u32[]{:S(2)}, u32[]{:S(2)}) collective-permute-start(f32[96,128]{1,0:T(8,128)S(1)} %pad_maximum_fusion.2), channel_id=1, source_target_pairs={{3,1},{5,3},{7,5},{9,7},{11,9},{13,11},{15,13},{17,15},{19,17},{21... | collective-permute-start | bytes 147464 | tf_op jit(solution)/shard_map/ppermute | solution.py:269

commit v4 on v3

--- a/solution.py
+++ b/solution.py
@@ -61,6 +61,24 @@
     for load in loads:
         load.start()
     contract = (((0,), (0,)), ((), ()))
+    copies = []
+
+    def ship(yh, x):
+        moves = [(part_a.at[yh, pl.ds(16 * x, 16)], outs[:4], pl.ds(16 * yh, 16), (x - lax.axis_index("x") + 4) % 4)]
+        for yl in range(2):
+            y = 2 * yh + yl
+            slot = (y - lax.axis_index(("yh", "yl")) + 4) % 4
+            moves.append((part_b.at[y, pl.ds(8 * x, 8)], outs[4:], pl.ds(8 * x, 8), slot))
+        for i, (src, blocks, rows, slot) in enumerate(moves):
+            at = sem.at[3 * (4 * yh + x) + i]
+            for s in range(4):
+
+                @pl.when(slot == s)
+                def _(s=s, src=src, blocks=blocks, rows=rows, at=at):
+                    pltpu.make_async_copy(src, blocks[s].at[rows], at).start()
+
+            copies.append(pltpu.make_async_copy(src, blocks[0].at[rows], at))
+
     for load in loads[:4]:
         load.wait()
     for m in range(4):
@@ -70,6 +88,8 @@
         for v in range(4):
             wide[pl.ds(v, 256, stride=4), :] = done[:, 128 * v : 128 * v + 128]
         place(part_a, part_b, wide, 8192 + 1024 * m, 1024)
+    ship(1, 2)
+    ship(1, 3)
     for load in loads[4:]:
         load.wait()
     gains = []
@@ -84,6 +104,8 @@
             folded = folded + piece * w[cols, 128 * v : 128 * v + 128].astype(F32)
         gains.append(jnp.sum(folded.T, axis=0, keepdims=True))
         place(part_a, part_b, wide, 2048 * m, 2048)
+        for group in ((0,), (1,), (2, 3), (4, 5))[m]:
+            ship(*divmod(group, 4))
     for m in range(4):
         for j in range(2):
             at = 256 * m + 128 * j
@@ -94,17 +116,9 @@
             extra[8 * p + v : 8 * p + v + 1, :] = taps[p : p + 1, 128 * v : 128 * v + 128]
     small = part_b.at[4, 0]
     small[...] = extra[...].astype(BF)
-    copies = []
     for s in range(4):
-        x = (lax.axis_index("x") + s) % 4
-        y = (lax.axis_index(("yh", "yl")) + s) % 4
-        for yh in range(2):
-            copies.append((part_a.at[yh, pl.ds(x * 16, 16)], outs[s].at[pl.ds(yh * 16, 16)]))
-        copies.append((small, outs[s].at[32]))
-        copies.append((part_b.at[y], outs[4 + s]))
-    copies = [pltpu.make_async_copy(src, dst, sem.at[i]) for i, (src, dst) in enumerate(copies)]
-    for copy in copies:
-        copy.start()
+        copies.append(pltpu.make_async_copy(small, outs[s].at[32], sem.at[24 + s]))
+        copies[-1].start()
     for copy in copies:
         copy.wait()
 
@@ -123,7 +137,7 @@
             pltpu.VMEM((5, 32, 48, 128), BF),
             pltpu.VMEM((2048, 128), F32),
             pltpu.VMEM((48, 128), F32),
-            pltpu.SemaphoreType.DMA((16,)),
+            pltpu.SemaphoreType.DMA((28,)),
             pltpu.SemaphoreType.DMA((9,)),
         ],
         compiler_params=pltpu.CompilerParams(vmem_limit_bytes=57 << 20),

time: 121 us -> 120 us (level)
  no operation moved by 1% of the time
where the time goes in v4:
time: 120 us; the launch traced here: 119 us
  Pallas kernels  36.3 us (30%)
  starting transfers between devices  35.6 us (30%)
  waiting for transfers between devices  23.6 us (20%)
  blocking collectives  17.7 us (15%)
  local copies, waits for them, and re-layouts  4.66 us (4%)
  between operations  1.5 us (1%)
    ppermute x12, starting transfers between devices, send(): lax.ppermute(blocks[step], axes, [(i, (i + step) % n) for i in range(n)])  21.9 us
    all_to_all x1, blocking collectives, reduce_terms(): return lax.all_to_all(ready, 'z', split_axis=0, concat_axis=0, tiled=True)  17.7 us
    ppermute x12, waiting for transfers between devices, send(): lax.ppermute(blocks[step], axes, [(i, (i + step) % n) for i in range(n)])  14.8 us
    pallas_call x1, Pallas kernels, forward_backward(): pl.pallas_call(main_kernel, out_shape=[wide, jax.ShapeDtypeStruct((2, ROW...  12.4 us
    pallas_call x1, Pallas kernels, outputs(): pl.pallas_call(outputs_kernel, out_shape=[wide, wide, jax.ShapeDtypeStruc...  10.7 us
    pallas_call x1, Pallas kernels, weight_blocks(): pl.pallas_call(weight_kernel, out_shape=blocks, in_specs=[vmem_spec()] +...  8.04 us
    ppermute x1, starting transfers between devices, own_chunk(): other = lax.ppermute(total, 'c', [(0, 1), (1, 0)])  5 us
    ppermute x4, waiting for transfers between devices, pair_swap(): return lax.ppermute(array, 'c', [(0, 1), (1, 0)])  4.36 us
  transfers between devices with their start and end apart: 20, of which 7 were waited for; matrix products, arithmetic and copies ran while one was open for 0% of the time, Pallas kernels for 12%

profile of v4, /device:TPU:1, one launch (start us, length us, event | category | flops | bytes accessed | tf_op | source)
XLA Modules:
  0.0 119.4 jit_solution(6831793280288585804)
XLA Ops:
  0.6 0.8 fusion
  1.5 3.9 %collective-permute-start = (bf16[2,16,1024]{2,1,0:T(8,128)(2,1)S(1)}, bf16[2,16,1024]{2,1,0:T(8,128)(2,1)S(1)}, u32[]{:S(2)}, u32[]{:S(2)}) collective-permute-start(bf16[2,16,1024]{2,1,0:T(8,128)(2,1)S(1)} %pad_maximum_fusion), channel_id=1, source_target_pairs={{0,32},{32,64},{64,96},{96,128},{128,160},{160,192},{192,224},{1,3... | collective-permute-start | bytes 196616 | tf_op jit(solution)/shard_map/ppermute | solution.py:567
  5.4 1.3 %collective-permute-start.1 = (bf16[2,16,1024]{2,1,0:T(8,128)(2,1)S(1)}, bf16[2,16,1024]{2,1,0:T(8,128)(2,1)S(1)}, u32[]{:S(2)}, u32[]{:S(2)}) collective-permute-start(bf16[2,16,1024]{2,1,0:T(8,128)(2,1)S(1)} %pad_maximum_fusion.1), channel_id=1, source_target_pairs={{32,0},{64,32},{96,64},{128,96},{160,128},{192,160},{224,192},{33,... | collective-permute-start | bytes 196616 | tf_op jit(solution)/shard_map/ppermute | solution.py:568
  7.4 3.6 %early.1 = (bf16[384,1024]{1,0:T(8,128)(2,1)}, bf16[384,512]{1,0:T(8,128)(2,1)}, bf16[384,512]{1,0:T(8,128)(2,1)}) custom-call(s32[1]{0:T(128)S(6)} %copy.10.length_ref.info_ref, f32[1,1024]{1,0:T(1,128)} %bitcast.11, bf16[384,1024]{1,0:T(8,128)(2,1)} %bitcast.7, bf16[384,1024]{1,0:T(8,128)(2,1)} %bitcast.9), custom_call_target="tpu_custom_call" | custom-call | tf_op jit(solution)/shard_map/early/pallas_call | solution.py:350
  11.1 0.6 copy-done.9
  11.7 12.4 %forward_backward.1 = (bf16[384,1024]{1,0:T(8,128)(2,1)}, bf16[2,384,1024]{2,1,0:T(8,128)(2,1)}, bf16[400,1024]{1,0:T(8,128)(2,1)}, bf16[400,1024]{1,0:T(8,128)(2,1)}) custom-call(s32[1]{0:T(128)S(6)} %copy.10.length_ref.info_ref, f32[1,1024]{1,0:T(1,128)} %bitcast.12, f32[9,1024]{1,0:T(8,128)} %taps_ref.1, bf16[384,1024]{1,0:T(8,128)(2,1)} %get-tuple-element.29.nh.n0h, ...), custom_call_target="tpu_custom_call" | custom-call | tf_op jit(solution)/shard_map/forward_backward/pallas_call | solution.py:479
  24.1 1.6 %collective-permute-start.3 = (bf16[400,1024]{1,0:T(8,128)(2,1)}, bf16[400,1024]{1,0:T(8,128)(2,1)S(1)}, u32[]{:S(2)}, u32[]{:S(2)}) collective-permute-start(bf16[400,1024]{1,0:T(8,128)(2,1)} %get-tuple-element.35), channel_id=1, source_target_pairs={{0,1},{1,0},{2,3},{3,2},{4,5},{5,4},{6,7},{7,6},{8,9},{9,8},{10,11... | collective-permute-start | bytes 2457608 | tf_op jit(solution)/shard_map/ppermute | solution.py:297
  25.7 0.4 collective-permute-start.4
  26.3 4.4 %collective-permute-done.5.g1h = bf16[384,512]{1,0:T(8,128)(2,1)S(1)} collective-permute-done((bf16[384,512]{1,0:T(8,128)(2,1)S(1)}, bf16[384,512]{1,0:T(8,128)(2,1)S(1)}, u32[]{:S(2)}, u32[]{:S(2)}) %collective-permute-start.5) | collective-permute-done | bytes 393248 | tf_op jit(solution)/shard_map/ppermute | solution.py:297
  30.7 0.7 copy-done.7
  32.2 8.0 %weight_grads.1 = (bf16[33,48,128]{2,1,0:T(8,128)(2,1)}, bf16[33,48,128]{2,1,0:T(8,128)(2,1)}, bf16[33,48,128]{2,1,0:T(8,128)(2,1)}, bf16[33,48,128]{2,1,0:T(8,1...) custom-call(f32[1,1024]{1,0:T(1,128)} %bitcast.13, ...), custom_call_target="tpu_custom_call" | custom-call | tf_op jit(solution)/shard_map/weight_grads/pallas_call | solution.py:128
  40.2 7.3 %collective-permute-start.12 = (bf16[32,48,128]{2,1,0:T(8,128)(2,1)}, bf16[32,48,128]{2,1,0:T(8,128)(2,1)S(1)}, u32[]{:S(2)}, u32[]{:S(2)}) collective-permute-start(bf16[32,48,128]{2,1,0:T(8,128)(2,1)} %get-tuple-element.48), channel_id=1, source_target_pairs={{0,128},{2,130},{128,0},{130,2},{1,129},{3,131},{129,1},{131,3},{4... | collective-permute-start | bytes 1179656 | tf_op jit(solution)/shard_map/ppermute | solution.py:183
  47.9 2.3 %collective-permute-start.14 = (bf16[32,48,128]{2,1,0:T(8,128)(2,1)}, bf16[32,48,128]{2,1,0:T(8,128)(2,1)S(1)}, u32[]{:S(2)}, u32[]{:S(2)}) collective-permute-start(bf16[32,48,128]{2,1,0:T(8,128)(2,1)} %get-tuple-element.50), channel_id=1, source_target_pairs={{0,130},{2,0},{128,2},{130,128},{1,131},{3,1},{129,3},{131,129},{4... | collective-permute-start | bytes 1179656 | tf_op jit(solution)/shard_map/ppermute | solution.py:183
  50.2 1.3 %collective-permute-start.7 = (bf16[33,48,128]{2,1,0:T(8,128)(2,1)}, bf16[33,48,128]{2,1,0:T(8,128)(2,1)S(1)}, u32[]{:S(2)}, u32[]{:S(2)}) collective-permute-start(bf16[33,48,128]{2,1,0:T(8,128)(2,1)} %get-tuple-element.40), channel_id=1, source_target_pairs={{0,32},{32,64},{64,96},{96,0},{1,33},{33,65},{65,97},{97,1},{2,34}... | collective-permute-start | bytes 1216520 | tf_op jit(solution)/shard_map/ppermute | solution.py:183
  51.4 5.4 %collective-permute-done.12.i1 = bf16[32,48,128]{2,1,0:T(8,128)(2,1)S(1)} collective-permute-done((bf16[32,48,128]{2,1,0:T(8,128)(2,1)}, bf16[32,48,128]{2,1,0:T(8,128)(2,1)S(1)}, u32[]{:S(2)}, u32[]{:S(2)}) %collective-permute-start.12) | collective-permute-done | bytes 393248 | tf_op jit(solution)/shard_map/ppermute | solution.py:183
  56.9 3.2 %collective-permute-start.8 = (bf16[33,48,128]{2,1,0:T(8,128)(2,1)}, bf16[33,48,128]{2,1,0:T(8,128)(2,1)S(1)}, u32[]{:S(2)}, u32[]{:S(2)}) collective-permute-start(bf16[33,48,128]{2,1,0:T(8,128)(2,1)} %get-tuple-element.41), channel_id=1, source_target_pairs={{0,96},{32,0},{64,32},{96,64},{1,97},{33,1},{65,33},{97,65},{2,98}... | collective-permute-start | bytes 1216520 | tf_op jit(solution)/shard_map/ppermute | solution.py:183
  60.1 5.6 %collective-permute-done.13.i2 = bf16[32,48,128]{2,1,0:T(8,128)(2,1)S(1)} collective-permute-done((bf16[32,48,128]{2,1,0:T(8,128)(2,1)}, bf16[32,48,128]{2,1,0:T(8,128)(2,1)S(1)}, u32[]{:S(2)}, u32[]{:S(2)}) %collective-permute-start.13) | collective-permute-done | bytes 393248 | tf_op jit(solution)/shard_map/ppermute | solution.py:183
  65.7 1.0 copy-done.1
  67.2 10.7 %outputs.1 = (bf16[384,1024]{1,0:T(8,128)(2,1)}, bf16[384,1024]{1,0:T(8,128)(2,1)}, f32[8,128]{1,0:T(8,128)}) custom-call(s32[1]{0:T(128)S(6)} %copy.10.length_ref.info_ref, f32[1,1024]{1,0:T(1,128)} %bitcast.14, bf16[384,1024]{1,0:T(8,128)(2,1)} %bitcast.8, bf16[384,1024]{1,0:T(8,128)(2,1)} %bitcast.10, bf16[384,1024]{1,0:T(8,128)(2,1)} %get-tuple-element.32.a0h.acth, ...), custom_call_target="tpu_custom_call" | custom-call | tf_op jit(solution)/shard_map/outputs/pallas_call | solution.py:543
  78.0 0.7 copy-done.2
  79.0 1.5 %collective-permute-start.9 = (bf16[9,48,128]{2,1,0:T(8,128)(2,1)S(1)}, bf16[9,48,128]{2,1,0:T(8,128)(2,1)S(1)}, u32[]{:S(2)}, u32[]{:S(2)}) collective-permute-start(bf16[9,48,128]{2,1,0:T(8,128)(2,1)S(1)} %get-tuple-element.44), channel_id=1, source_target_pairs={{0,128},{2,130},{128,0},{130,2},{1,129},{3,131},{129,1},{131,3},{4... | collective-permute-start | bytes 331784 | tf_op jit(solution)/shard_map/ppermute | solution.py:183
  80.5 1.9 %collective-permute-start.10 = (bf16[9,48,128]{2,1,0:T(8,128)(2,1)S(1)}, bf16[9,48,128]{2,1,0:T(8,128)(2,1)S(1)}, u32[]{:S(2)}, u32[]{:S(2)}) collective-permute-start(bf16[9,48,128]{2,1,0:T(8,128)(2,1)S(1)} %get-tuple-element.45), channel_id=1, source_target_pairs={{0,2},{2,128},{128,130},{130,0},{1,3},{3,129},{129,131},{131,1},{4... | collective-permute-start | bytes 331784 | tf_op jit(solution)/shard_map/ppermute | solution.py:183
  82.4 0.8 collective-permute-start.11
  83.2 3.0 %collective-permute-start.16 = (bf16[8,48,128]{2,1,0:T(8,128)(2,1)S(1)}, bf16[8,48,128]{2,1,0:T(8,128)(2,1)S(1)}, u32[]{:S(2)}, u32[]{:S(2)}) collective-permute-start(bf16[8,48,128]{2,1,0:T(8,128)(2,1)S(1)} %get-tuple-element.53), channel_id=1, source_target_pairs={{0,32},{32,64},{64,96},{96,0},{1,33},{33,65},{65,97},{97,1},{2,34}... | collective-permute-start | bytes 294920 | tf_op jit(solution)/shard_map/ppermute | solution.py:183
  86.1 1.9 %collective-permute-done.16.b2 = bf16[8,48,128]{2,1,0:T(8,128)(2,1)S(1)} collective-permute-done((bf16[8,48,128]{2,1,0:T(8,128)(2,1)S(1)}, bf16[8,48,128]{2,1,0:T(8,128)(2,1)S(1)}, u32[]{:S(2)}, u32[]{:S(2)}) %collective-permute-start.16) | collective-permute-done | bytes 98336 | tf_op jit(solution)/shard_map/ppermute | solution.py:183
  88.0 1.9 %collective-permute-done.17.b3 = bf16[8,48,128]{2,1,0:T(8,128)(2,1)S(1)} collective-permute-done((bf16[8,48,128]{2,1,0:T(8,128)(2,1)S(1)}, bf16[8,48,128]{2,1,0:T(8,128)(2,1)S(1)}, u32[]{:S(2)}, u32[]{:S(2)}) %collective-permute-start.17) | collective-permute-done | bytes 98336 | tf_op jit(solution)/shard_map/ppermute | solution.py:183
  90.0 17.7 %all_to_all.5.parts = bf16[8,144,128]{2,1,0:T(8,128)(2,1)S(1)} all-to-all(bf16[8,144,128]{2,1,0:T(8,128)(2,1)S(1)} %sum_before_z.1), channel_id=1, replica_groups=mesh['yh'=2,'x'=4,'z'=8,'yl'=2,'c'=2] {'z'}, dimensions={0} | all-to-all | bytes 589824 | tf_op jit(solution)/shard_map/all_to_all | solution.py:218
  107.7 5.0 %collective-permute-start.18 = (f32[144,128]{1,0:T(8,128)S(1)}, f32[144,128]{1,0:T(8,128)S(1)}, u32[]{:S(2)}, u32[]{:S(2)}) collective-permute-start(f32[144,128]{1,0:T(8,128)S(1)} %sum_after_z.1.own), channel_id=1, source_target_pairs={{0,1},{1,0},{2,3},{3,2},{4,5},{5,4},{6,7},{7,6},{8,9},{9,8},{10,11... | collective-permute-start | bytes 221192 | tf_op jit(solution)/shard_map/ppermute | solution.py:281
  112.7 0.9 collective-permute-done.18.other
  113.6 1.3 %collective-permute-start.19 = (f32[96,128]{1,0:T(8,128)S(1)}, f32[96,128]{1,0:T(8,128)S(1)}, u32[]{:S(2)}, u32[]{:S(2)}) collective-permute-start(f32[96,128]{1,0:T(8,128)S(1)} %pad_maximum_fusion.2), channel_id=1, source_target_pairs={{3,1},{5,3},{7,5},{9,7},{11,9},{13,11},{15,13},{17,15},{19,17},{21... | collective-permute-start | bytes 147464 | tf_op jit(solution)/shard_map/ppermute | solution.py:283
  114.9 3.5 %collective-permute-done.19.follow = f32[96,128]{1,0:T(8,128)S(1)} collective-permute-done((f32[96,128]{1,0:T(8,128)S(1)}, f32[96,128]{1,0:T(8,128)S(1)}, u32[]{:S(2)}, u32[]{:S(2)}) %collective-permute-start.19) | collective-permute-done | bytes 49184 | tf_op jit(solution)/shard_map/ppermute | solution.py:283
  118.5 1.0 own_chunk.1
  (46 shorter events, 2.4 us)
Async XLA Ops:
  1.5 9.6 %collective-permute-start = (bf16[2,16,1024]{2,1,0:T(8,128)(2,1)S(1)}, bf16[2,16,1024]{2,1,0:T(8,128)(2,1)S(1)}, u32[]{:S(2)}, u32[]{:S(2)}) collective-permute-start(bf16[2,16,1024]{2,1,0:T(8,128)(2,1)S(1)} %pad_maximum_fusion), channel_id=1, source_target_pairs={{0,32},{32,64},{64,96},{96,128},{128,160},{160,192},{192,224},{1,3... | collective-permute-start | bytes 196616 | tf_op jit(solution)/shard_map/ppermute | solution.py:567
  5.4 5.6 %collective-permute-start.1 = (bf16[2,16,1024]{2,1,0:T(8,128)(2,1)S(1)}, bf16[2,16,1024]{2,1,0:T(8,128)(2,1)S(1)}, u32[]{:S(2)}, u32[]{:S(2)}) collective-permute-start(bf16[2,16,1024]{2,1,0:T(8,128)(2,1)S(1)} %pad_maximum_fusion.1), channel_id=1, source_target_pairs={{32,0},{64,32},{96,64},{128,96},{160,128},{192,160},{224,192},{33,... | collective-permute-start | bytes 196616 | tf_op jit(solution)/shard_map/ppermute | solution.py:568
  11.0 0.6 copy-start.9
  11.1 0.6 copy-start.10
  11.7 14.0 %copy-start.3 = (bf16[384,1024]{1,0:T(8,128)(2,1)S(1)}, bf16[384,1024]{1,0:T(8,128)(2,1)}, u32[]{:S(2)}) copy-start(bf16[384,1024]{1,0:T(8,128)(2,1)} %get-tuple-element.29.nh.n0h) | copy-start | bytes 2359300
  11.7 14.5 %copy-start.8 = (bf16[384,512]{1,0:T(8,128)(2,1)S(1)}, bf16[384,512]{1,0:T(8,128)(2,1)}, u32[]{:S(2)}) copy-start(bf16[384,512]{1,0:T(8,128)(2,1)} %get-tuple-element.31.ggh) | copy-start | bytes 1179652
  24.1 6.6 %collective-permute-start.3 = (bf16[400,1024]{1,0:T(8,128)(2,1)}, bf16[400,1024]{1,0:T(8,128)(2,1)S(1)}, u32[]{:S(2)}, u32[]{:S(2)}) collective-permute-start(bf16[400,1024]{1,0:T(8,128)(2,1)} %get-tuple-element.35), channel_id=1, source_target_pairs={{0,1},{1,0},{2,3},{3,2},{4,5},{5,4},{6,7},{7,6},{8,9},{9,8},{10,11... | collective-permute-start | bytes 2457608 | tf_op jit(solution)/shard_map/ppermute | solution.py:297
  25.6 5.0 %collective-permute-start.2 = (bf16[384,1024]{1,0:T(8,128)(2,1)S(1)}, bf16[384,1024]{1,0:T(8,128)(2,1)S(1)}, u32[]{:S(2)}, u32[]{:S(2)}) collective-permute-start(bf16[384,1024]{1,0:T(8,128)(2,1)S(1)} %copy-done.3), channel_id=1, source_target_pairs={{0,1},{1,0},{2,3},{3,2},{4,5},{5,4},{6,7},{7,6},{8,9},{9,8},{10,11... | collective-permute-start | bytes 2359304 | tf_op jit(solution)/shard_map/ppermute | solution.py:297
  25.7 4.9 %collective-permute-start.4 = (bf16[384,1024]{1,0:T(8,128)(2,1)}, bf16[384,1024]{1,0:T(8,128)(2,1)S(1)}, u32[]{:S(2)}, u32[]{:S(2)}) collective-permute-start(bf16[384,1024]{1,0:T(8,128)(2,1)} %get-tuple-element.32.a0h.acth), channel_id=1, source_target_pairs={{0,1},{1,0},{2,3},{3,2},{4,5},{5,4},{6,7},{7,6},{8,9},{9,8},{10,11... | collective-permute-start | bytes 2359304 | tf_op jit(solution)/shard_map/ppermute | solution.py:297
  26.2 4.5 %collective-permute-start.5 = (bf16[384,512]{1,0:T(8,128)(2,1)S(1)}, bf16[384,512]{1,0:T(8,128)(2,1)S(1)}, u32[]{:S(2)}, u32[]{:S(2)}) collective-permute-start(bf16[384,512]{1,0:T(8,128)(2,1)S(1)} %copy-done.8), channel_id=1, source_target_pairs={{0,1},{1,0},{2,3},{3,2},{4,5},{5,4},{6,7},{7,6},{8,9},{9,8},{10,11... | collective-permute-start | bytes 1179656 | tf_op jit(solution)/shard_map/ppermute | solution.py:297
  30.6 0.7 copy-start.7
  30.6 1.0 copy-start.5
  30.6 1.3 %copy-start.6 = (bf16[384,1024]{1,0:T(8,128)(2,1)}, bf16[384,1024]{1,0:T(8,128)(2,1)S(1)}, u32[]{:S(2)}) copy-start(bf16[384,1024]{1,0:T(8,128)(2,1)S(1)} %collective-permute-done.4.a1h) | copy-start | bytes 2359300
  30.7 1.5 %copy-start.4 = (bf16[400,1024]{1,0:T(8,128)(2,1)}, bf16[400,1024]{1,0:T(8,128)(2,1)S(1)}, u32[]{:S(2)}) copy-start(bf16[400,1024]{1,0:T(8,128)(2,1)S(1)} %collective-permute-done.3.k1h) | copy-start | bytes 2457604
  40.2 16.6 %collective-permute-start.12 = (bf16[32,48,128]{2,1,0:T(8,128)(2,1)}, bf16[32,48,128]{2,1,0:T(8,128)(2,1)S(1)}, u32[]{:S(2)}, u32[]{:S(2)}) collective-permute-start(bf16[32,48,128]{2,1,0:T(8,128)(2,1)} %get-tuple-element.48), channel_id=1, source_target_pairs={{0,128},{2,130},{128,0},{130,2},{1,129},{3,131},{129,1},{131,3},{4... | collective-permute-start | bytes 1179656 | tf_op jit(solution)/shard_map/ppermute | solution.py:183
  47.5 18.2 %collective-permute-start.13 = (bf16[32,48,128]{2,1,0:T(8,128)(2,1)}, bf16[32,48,128]{2,1,0:T(8,128)(2,1)S(1)}, u32[]{:S(2)}, u32[]{:S(2)}) collective-permute-start(bf16[32,48,128]{2,1,0:T(8,128)(2,1)} %get-tuple-element.49), channel_id=1, source_target_pairs={{0,2},{2,128},{128,130},{130,0},{1,3},{3,129},{129,131},{131,1},{4... | collective-permute-start | bytes 1179656 | tf_op jit(solution)/shard_map/ppermute | solution.py:183
  47.9 17.9 %collective-permute-start.14 = (bf16[32,48,128]{2,1,0:T(8,128)(2,1)}, bf16[32,48,128]{2,1,0:T(8,128)(2,1)S(1)}, u32[]{:S(2)}, u32[]{:S(2)}) collective-permute-start(bf16[32,48,128]{2,1,0:T(8,128)(2,1)} %get-tuple-element.50), channel_id=1, source_target_pairs={{0,130},{2,0},{128,2},{130,128},{1,131},{3,1},{129,3},{131,129},{4... | collective-permute-start | bytes 1179656 | tf_op jit(solution)/shard_map/ppermute | solution.py:183
  50.2 27.8 %collective-permute-start.6 = (bf16[33,48,128]{2,1,0:T(8,128)(2,1)}, bf16[33,48,128]{2,1,0:T(8,128)(2,1)S(1)}, u32[]{:S(2)}, u32[]{:S(2)}) collective-permute-start(bf16[33,48,128]{2,1,0:T(8,128)(2,1)} %get-tuple-element.39), channel_id=1, source_target_pairs={{0,64},{32,96},{64,0},{96,32},{1,65},{33,97},{65,1},{97,33},{2,66}... | collective-permute-start | bytes 1216520 | tf_op jit(solution)/shard_map/ppermute | solution.py:183
  50.2 27.8 %collective-permute-start.7 = (bf16[33,48,128]{2,1,0:T(8,128)(2,1)}, bf16[33,48,128]{2,1,0:T(8,128)(2,1)S(1)}, u32[]{:S(2)}, u32[]{:S(2)}) collective-permute-start(bf16[33,48,128]{2,1,0:T(8,128)(2,1)} %get-tuple-element.40), channel_id=1, source_target_pairs={{0,32},{32,64},{64,96},{96,0},{1,33},{33,65},{65,97},{97,1},{2,34}... | collective-permute-start | bytes 1216520 | tf_op jit(solution)/shard_map/ppermute | solution.py:183
  56.9 21.1 %collective-permute-start.8 = (bf16[33,48,128]{2,1,0:T(8,128)(2,1)}, bf16[33,48,128]{2,1,0:T(8,128)(2,1)S(1)}, u32[]{:S(2)}, u32[]{:S(2)}) collective-permute-start(bf16[33,48,128]{2,1,0:T(8,128)(2,1)} %get-tuple-element.41), channel_id=1, source_target_pairs={{0,96},{32,0},{64,32},{96,64},{1,97},{33,1},{65,33},{97,65},{2,98}... | collective-permute-start | bytes 1216520 | tf_op jit(solution)/shard_map/ppermute | solution.py:183
  65.7 1.0 copy-start.1
  66.9 19.2 %collective-permute-start.15 = (bf16[8,48,128]{2,1,0:T(8,128)(2,1)S(1)}, bf16[8,48,128]{2,1,0:T(8,128)(2,1)S(1)}, u32[]{:S(2)}, u32[]{:S(2)}) collective-permute-start(bf16[8,48,128]{2,1,0:T(8,128)(2,1)S(1)} %get-tuple-element.52), channel_id=1, source_target_pairs={{0,64},{32,96},{64,0},{96,32},{1,65},{33,97},{65,1},{97,33},{2,66}... | collective-permute-start | bytes 294920 | tf_op jit(solution)/shard_map/ppermute | solution.py:183
  67.2 10.8 %copy-start = (bf16[33,48,128]{2,1,0:T(8,128)(2,1)S(1)}, bf16[33,48,128]{2,1,0:T(8,128)(2,1)}, u32[]{:S(2)}) copy-start(bf16[33,48,128]{2,1,0:T(8,128)(2,1)} %get-tuple-element.36.after_this.i0) | copy-start | bytes 1216516
  78.0 0.7 copy-start.2
  79.0 10.9 %collective-permute-start.9 = (bf16[9,48,128]{2,1,0:T(8,128)(2,1)S(1)}, bf16[9,48,128]{2,1,0:T(8,128)(2,1)S(1)}, u32[]{:S(2)}, u32[]{:S(2)}) collective-permute-start(bf16[9,48,128]{2,1,0:T(8,128)(2,1)S(1)} %get-tuple-element.44), channel_id=1, source_target_pairs={{0,128},{2,130},{128,0},{130,2},{1,129},{3,131},{129,1},{131,3},{4... | collective-permute-start | bytes 331784 | tf_op jit(solution)/shard_map/ppermute | solution.py:183
  80.5 9.4 %collective-permute-start.10 = (bf16[9,48,128]{2,1,0:T(8,128)(2,1)S(1)}, bf16[9,48,128]{2,1,0:T(8,128)(2,1)S(1)}, u32[]{:S(2)}, u32[]{:S(2)}) collective-permute-start(bf16[9,48,128]{2,1,0:T(8,128)(2,1)S(1)} %get-tuple-element.45), channel_id=1, source_target_pairs={{0,2},{2,128},{128,130},{130,0},{1,3},{3,129},{129,131},{131,1},{4... | collective-permute-start | bytes 331784 | tf_op jit(solution)/shard_map/ppermute | solution.py:183
  82.4 7.5 %collective-permute-start.11 = (bf16[9,48,128]{2,1,0:T(8,128)(2,1)S(1)}, bf16[9,48,128]{2,1,0:T(8,128)(2,1)S(1)}, u32[]{:S(2)}, u32[]{:S(2)}) collective-permute-start(bf16[9,48,128]{2,1,0:T(8,128)(2,1)S(1)} %get-tuple-element.46), channel_id=1, source_target_pairs={{0,130},{2,0},{128,2},{130,128},{1,131},{3,1},{129,3},{131,129},{4... | collective-permute-start | bytes 331784 | tf_op jit(solution)/shard_map/ppermute | solution.py:183
  83.2 4.8 %collective-permute-start.16 = (bf16[8,48,128]{2,1,0:T(8,128)(2,1)S(1)}, bf16[8,48,128]{2,1,0:T(8,128)(2,1)S(1)}, u32[]{:S(2)}, u32[]{:S(2)}) collective-permute-start(bf16[8,48,128]{2,1,0:T(8,128)(2,1)S(1)} %get-tuple-element.53), channel_id=1, source_target_pairs={{0,32},{32,64},{64,96},{96,0},{1,33},{33,65},{65,97},{97,1},{2,34}... | collective-permute-start | bytes 294920 | tf_op jit(solution)/shard_map/ppermute | solution.py:183
  86.1 3.8 %collective-permute-start.17 = (bf16[8,48,128]{2,1,0:T(8,128)(2,1)S(1)}, bf16[8,48,128]{2,1,0:T(8,128)(2,1)S(1)}, u32[]{:S(2)}, u32[]{:S(2)}) collective-permute-start(bf16[8,48,128]{2,1,0:T(8,128)(2,1)S(1)} %get-tuple-element.54), channel_id=1, source_target_pairs={{0,96},{32,0},{64,32},{96,64},{1,97},{33,1},{65,33},{97,65},{2,98}... | collective-permute-start | bytes 294920 | tf_op jit(solution)/shard_map/ppermute | solution.py:183
  107.7 5.9 %collective-permute-start.18 = (f32[144,128]{1,0:T(8,128)S(1)}, f32[144,128]{1,0:T(8,128)S(1)}, u32[]{:S(2)}, u32[]{:S(2)}) collective-permute-start(f32[144,128]{1,0:T(8,128)S(1)} %sum_after_z.1.own), channel_id=1, source_target_pairs={{0,1},{1,0},{2,3},{3,2},{4,5},{5,4},{6,7},{7,6},{8,9},{9,8},{10,11... | collective-permute-start | bytes 221192 | tf_op jit(solution)/shard_map/ppermute | solution.py:281
  113.6 4.8 %collective-permute-start.19 = (f32[96,128]{1,0:T(8,128)S(1)}, f32[96,128]{1,0:T(8,128)S(1)}, u32[]{:S(2)}, u32[]{:S(2)}) collective-permute-start(f32[96,128]{1,0:T(8,128)S(1)} %pad_maximum_fusion.2), channel_id=1, source_target_pairs={{3,1},{5,3},{7,5},{9,7},{11,9},{13,11},{15,13},{17,15},{19,17},{21... | collective-permute-start | bytes 147464 | tf_op jit(solution)/shard_map/ppermute | solution.py:283
